TPU v7x, 128 devices: a whole 4x4x4 slice. The times are simulated.
128 devices in a mesh: mem: 16 (over z, y), cell: 8 (over x, core).
Axes of the slice: x: 4, y: 4, z: 4, core: 2. Of those that a mesh axis runs over, the one named last changes fastest.
Arguments:
- turnover_effect: float32 [1024, 65536], P('mem', 'cell'), may hold values from -3 to 3
- base_rate: float32 [65536], P('cell'), may hold values from 0.05 to 0.5
- fast_rate: float32 [65536], P('cell'), may hold values from 0.02 to 0.2
- slow_rate: float32 [65536], P('cell'), may hold values from 0.005 to 0.05
- init_pools: float32 [3, 65536], P(None, 'cell'), may hold values from 1 to 6
- litterfall: float32 [6, 65536], P(None, 'cell'), may hold values from 0.1 to 1
- obs_taps: int32 [16384, 4], P('cell'), may hold values from 0 to 127
- obs_weights: float32 [16384, 4], P('cell'), may hold values from 0.05 to 0.5
- observed: float32 [16384], P('cell'), may hold values from 0.5 to 4
- obs_var: float32 [16384], P('cell'), may hold values from 0.008 to 0.11, as said below
- obs_noise: float32 [1024, 16384], P('mem', 'cell'), may hold values from -6 to 6
Outputs:
- updated_effect: float32 [1024, 65536], P('mem', 'cell')
Inputs may be any that keep to these rules, and one draw needn't show every extreme that they name: `obs_var`: positive variances.
All inputs are finite; a program needn't handle non-finite values.
Results may differ from a plain program's by a relative error of at most 0.00025.
Values sent between devices are 32-bit elements; how exact they have to be, the bound alone decides.
No kernel may reach another device: no remote copies, remote signals or barrier semaphores. Data moves between devices by JAX's collectives and lax.ppermute only.
A program may use at most 192 MiB of HBM per device.

v0:
```python
import math

import jax
import jax.numpy as jnp
from jax import lax
from jax.sharding import PartitionSpec as P

STEPS = 6
BLOCK = 128
TAPS = 4


highest = lax.Precision.HIGHEST


def forward(turnover_effect, base_rate, fast_rate, slow_rate, init_pools, litterfall):
    decayed = 1.0 - jnp.exp(-base_rate[None, :] * jnp.exp(turnover_effect))
    litter = jnp.broadcast_to(init_pools[0][None, :], turnover_effect.shape)
    fast_pool = jnp.broadcast_to(init_pools[1][None, :], turnover_effect.shape)
    slow_pool = jnp.broadcast_to(init_pools[2][None, :], turnover_effect.shape)
    resp_total = jnp.zeros(turnover_effect.shape, jnp.float32)
    for month in range(STEPS):
        litter_out = decayed * litter
        fast_out = fast_rate[None, :] * fast_pool
        slow_out = slow_rate[None, :] * slow_pool
        resp_total = resp_total + 0.6 * litter_out + 0.7 * fast_out + slow_out
        litter = litter - litter_out + litterfall[month][None, :]
        fast_pool = fast_pool + 0.4 * litter_out - fast_out
        slow_pool = slow_pool + 0.3 * fast_out - slow_out
    return resp_total


def observe(resp_total, obs_taps, obs_weights):
    member_count = resp_total.shape[0]
    block_count = resp_total.shape[1] // BLOCK
    positions = jnp.arange(BLOCK, dtype=jnp.int32)
    operator_table = jnp.zeros((obs_taps.shape[0], BLOCK), jnp.float32)
    for tap_index in range(TAPS):
        hits = (obs_taps[:, tap_index][:, None] == positions[None, :]).astype(jnp.float32)
        operator_table = operator_table + obs_weights[:, tap_index][:, None] * hits
    operator_table = operator_table.reshape(block_count, -1, BLOCK)
    blocked = resp_total.reshape(member_count, block_count, BLOCK)
    predicted = jnp.einsum("jbc,boc->jbo", blocked, operator_table, precision=highest)
    return predicted.reshape(member_count, -1)


def spd_solve(matrix, right_side):
    factor = jnp.linalg.cholesky(matrix)
    halfway = lax.linalg.triangular_solve(factor, right_side, left_side=True, lower=True)
    return lax.linalg.triangular_solve(
        factor, halfway, left_side=True, lower=True, transpose_a=True
    )


def contract_last(left, right):
    return lax.dot_general(left, right, (((1,), (1,)), ((), ())), precision=highest)


def body(
    turnover_effect,
    base_rate,
    fast_rate,
    slow_rate,
    init_pools,
    litterfall,
    obs_taps,
    obs_weights,
    observed,
    obs_var,
    obs_noise,
):
    resp_total = forward(turnover_effect, base_rate, fast_rate, slow_rate, init_pools, litterfall)
    predicted = observe(resp_total, obs_taps, obs_weights)
    mem_count = lax.axis_size("mem")
    cell_count = lax.axis_size("cell")
    local_members, local_cells = turnover_effect.shape
    local_obs = predicted.shape[1]
    member_count = local_members * mem_count
    all_obs = local_obs * cell_count
    inv_root = 1.0 / math.sqrt(member_count - 1)
    effect_sum, predicted_sum = lax.psum(
        (jnp.sum(turnover_effect, axis=0), jnp.sum(predicted, axis=0)), "mem"
    )
    anomaly = (turnover_effect - (effect_sum / member_count)[None, :]) * inv_root
    pred_anomaly = (predicted - (predicted_sum / member_count)[None, :]) * inv_root
    residual = observed[None, :] - predicted
    misfit_local = jnp.sum(residual * residual / obs_var[None, :])
    departure = observed[None, :] + jnp.sqrt(obs_var)[None, :] * obs_noise - predicted
    identity_matrix = jnp.eye(member_count, dtype=jnp.float32)
    misfit_sum = lax.psum(misfit_local, ("mem", "cell"))
    stacked = jnp.concatenate(
        [pred_anomaly / obs_var[None, :], departure / obs_var[None, :]], axis=0
    )
    partial_cols = contract_last(lax.all_gather(pred_anomaly, "mem", axis=0, tiled=True), stacked)
    summed = lax.psum(partial_cols, "cell")
    gram = lax.all_gather(summed[:, :local_members], "mem", axis=1, tiled=True)
    step_size = member_count * all_obs / misfit_sum
    local_solve = spd_solve(
        identity_matrix + step_size * gram, step_size * summed[:, local_members:]
    )
    change = jnp.einsum(
        "kj,kc->jc",
        local_solve,
        lax.all_gather(anomaly, "mem", axis=0, tiled=True),
        precision=highest,
    )
    return turnover_effect + change


def solution(mesh):
    in_specs = (
        P("mem", "cell"),
        P("cell"),
        P("cell"),
        P("cell"),
        P(None, "cell"),
        P(None, "cell"),
        P("cell", None),
        P("cell", None),
        P("cell"),
        P("cell"),
        P("mem", "cell"),
    )
    out_specs = P("mem", "cell")
    return jax.shard_map(body, mesh=mesh, in_specs=in_specs, out_specs=out_specs, check_vma=False)
```

profile of v0, /device:TPU:0, one launch (start us, length us, event | category | flops | bytes accessed | tf_op | source)
XLA Modules:
  0.0 691.6 jit_solution(13496281260930924091)
XLA Ops:
  24.5 9.8 %fusion.32 = (f32[]{:T(128)}, f32[64,32]{1,0:T(8,128)S(1)}, f32[64,32,64]{2,1,0:T(8,128)S(1)}) fusion(f32[64,32]{1,0:T(8,128)S(1)} %div.48, f32[64,32]{1,0:T(8,128)S(1)} %sub.84, f32[8,64,8,128]{3,2,1,0:T(8,128)S(1)} %get-tuple-element.42, f32[64,32]{1,0:T(8,128)S(1)} %mul.268, s32[64,32]{1,0:T(8,128)S(1)} %eq.80, f32[64,32]{1,0:T(8,128)S(1)} %mul.265, ...), kind=kOutput, calls=%fused_computation.81 | convolution fusion | flops 204863488 | bytes 2711556 | tf_op jit(solution)/shard_map/jbc,boc->jbo/dot_general | solution.py:43
  34.3 76.0 %all-reduce.1 = (f32[2048]{0:T(1024)S(1)}, f32[8192]{0:T(1024)S(1)}) all-reduce(f32[2048]{0:T(1024)S(1)} %reduce_sum.31, f32[8192]{0:T(1024)S(1)} %get-tuple-element.41), channel_id=1, replica_groups=mesh['mem'=16,'cell'=8] {'mem'}, use_global_device_ids=true, to_apply=%region_3.0 | all-reduce | flops 10240 | bytes 81920 | tf_op jit(solution)/shard_map/psum | solution.py:81
  112.8 67.3 %all-gather.4.cloned.1.call-done = f32[1024,2048]{1,0:T(8,128)} async-done(((f32[64,2048]{1,0:T(8,128)}), f32[1024,2048]{1,0:T(8,128)}) %all-gather.4.cloned.1.call-update) | async-done | bytes 8388624 | tf_op jit(solution)/shard_map/all_gather | solution.py:94
  180.1 12.0 %fusion.19 = f32[1024,128]{0,1:T(8,128)} fusion(f32[1024,2048]{1,0:T(8,128)} %all-gather.4.cloned.1.call-done, f32[64,2048]{1,0:T(8,128)S(1)} %get-tuple-element.43, f32[64,2048]{1,0:T(8,128)S(1)} %get-tuple-element.33), kind=kOutput, calls=%fused_computation.62 | convolution fusion | flops 3221487616 | bytes 9961472 | tf_op jit(solution)/shard_map/dot_general | solution.py:56
  192.1 64.9 %psum.28 = f32[]{:T(128)} all-reduce(f32[]{:T(128)} %get-tuple-element.13), channel_id=1, replica_groups=mesh['mem'=16,'cell'=8] {'mem','cell'}, use_global_device_ids=true, to_apply=%region_1.0 | all-reduce | flops 1 | bytes 8 | tf_op jit(solution)/shard_map/psum | solution.py:90
  261.2 47.2 %all-gather.6.cloned.1.call-done = f32[1024,1024]{0,1:T(8,128)} async-done(((f32[1024,64]{0,1:T(8,128)}), f32[1024,1024]{0,1:T(8,128)}) %all-gather.6.cloned.1.call-update) | async-done | bytes 4194320 | tf_op jit(solution)/shard_map/all_gather | solution.py:96
  326.9 11.7 %cholesky.223 = f32[128,128]{1,0:T(8,128)S(1)} custom-call(f32[128,128]{1,0:T(8,128)S(1)} %cholesky.580), custom_call_target="Cholesky" | custom-call | tf_op jit(solution)/shard_map/jit(cholesky)/cholesky | solution.py:48
  341.1 9.8 %custom-call.64 = f32[1,128,128]{1,2,0:T(8,128)S(1)} custom-call(f32[1,128,128]{2,1,0:T(8,128)S(1)} %get-tuple-element.75), custom_call_target="InvertDiagBlocksLowerTriangular" | custom-call | tf_op jit(solution)/shard_map/jit(cholesky)/cholesky | solution.py:48
  354.8 11.8 %cholesky.244 = f32[128,128]{1,0:T(8,128)S(1)} custom-call(f32[128,128]{1,0:T(8,128)S(1)} %cholesky.584), custom_call_target="Cholesky" | custom-call | tf_op jit(solution)/shard_map/jit(cholesky)/cholesky | solution.py:48
  367.3 9.8 %custom-call.65 = f32[1,128,128]{1,2,0:T(8,128)S(1)} custom-call(f32[1,128,128]{2,1,0:T(8,128)S(1)} %get-tuple-element.72), custom_call_target="InvertDiagBlocksLowerTriangular" | custom-call | tf_op jit(solution)/shard_map/jit(cholesky)/cholesky | solution.py:48
  380.5 11.7 %cholesky.468 = f32[128,128]{1,0:T(8,128)S(1)} custom-call(f32[128,128]{1,0:T(8,128)S(1)} %cholesky.589), custom_call_target="Cholesky" | custom-call | tf_op jit(solution)/shard_map/jit(cholesky)/cholesky | solution.py:48
  392.9 9.8 %custom-call.66 = f32[1,128,128]{1,2,0:T(8,128)S(1)} custom-call(f32[1,128,128]{2,1,0:T(8,128)S(1)} %get-tuple-element.69), custom_call_target="InvertDiagBlocksLowerTriangular" | custom-call | tf_op jit(solution)/shard_map/jit(cholesky)/cholesky | solution.py:48
  406.2 11.9 %cholesky.487 = f32[128,128]{1,0:T(8,128)S(1)} custom-call(f32[128,128]{1,0:T(8,128)S(1)} %cholesky.594), custom_call_target="Cholesky" | custom-call | tf_op jit(solution)/shard_map/jit(cholesky)/cholesky | solution.py:48
  418.7 9.8 %custom-call.67 = f32[1,128,128]{1,2,0:T(8,128)S(1)} custom-call(f32[1,128,128]{2,1,0:T(8,128)S(1)} %get-tuple-element.66), custom_call_target="InvertDiagBlocksLowerTriangular" | custom-call | tf_op jit(solution)/shard_map/jit(cholesky)/cholesky | solution.py:48
  432.1 11.7 %cholesky.506 = f32[128,128]{1,0:T(8,128)S(1)} custom-call(f32[128,128]{1,0:T(8,128)S(1)} %cholesky.599), custom_call_target="Cholesky" | custom-call | tf_op jit(solution)/shard_map/jit(cholesky)/cholesky | solution.py:48
  444.4 10.2 %custom-call.68 = f32[1,128,128]{1,2,0:T(8,128)S(1)} custom-call(f32[1,128,128]{2,1,0:T(8,128)S(1)} %get-tuple-element.63), custom_call_target="InvertDiagBlocksLowerTriangular" | custom-call | tf_op jit(solution)/shard_map/jit(cholesky)/cholesky | solution.py:48
  458.0 11.7 %cholesky.526 = f32[128,128]{1,0:T(8,128)S(1)} custom-call(f32[128,128]{1,0:T(8,128)S(1)} %cholesky.604), custom_call_target="Cholesky" | custom-call | tf_op jit(solution)/shard_map/jit(cholesky)/cholesky | solution.py:48
  470.4 9.8 %custom-call.69 = f32[1,128,128]{1,2,0:T(8,128)S(1)} custom-call(f32[1,128,128]{2,1,0:T(8,128)S(1)} %get-tuple-element.60), custom_call_target="InvertDiagBlocksLowerTriangular" | custom-call | tf_op jit(solution)/shard_map/jit(cholesky)/cholesky | solution.py:48
  483.2 11.9 %cholesky.546 = f32[128,128]{1,0:T(8,128)S(1)} custom-call(f32[128,128]{1,0:T(8,128)S(1)} %cholesky.609), custom_call_target="Cholesky" | custom-call | tf_op jit(solution)/shard_map/jit(cholesky)/cholesky | solution.py:48
  495.7 9.8 %custom-call.70 = f32[1,128,128]{1,2,0:T(8,128)S(1)} custom-call(f32[1,128,128]{2,1,0:T(8,128)S(1)} %get-tuple-element.57), custom_call_target="InvertDiagBlocksLowerTriangular" | custom-call | tf_op jit(solution)/shard_map/jit(cholesky)/cholesky | solution.py:48
  508.2 11.7 %cholesky.564 = f32[128,128]{1,0:T(8,128)S(1)} custom-call(f32[128,128]{1,0:T(8,128)S(1)} %convolution_subtract_fusion.6), custom_call_target="Cholesky" | custom-call | tf_op jit(solution)/shard_map/jit(cholesky)/cholesky | solution.py:48
  535.7 22.4 %while.1 = (s32[]{:T(128)}, f32[1024,1024]{1,0:T(8,128)}, s32[8,2]{0,1:T(2,128)S(1)}, f32[8,128,128]{2,1,0:T(8,128)S(1)}, s32[]{:T(128)}) while((s32[]{:T(128)}, f32[1024,1024]{1,0:T(8,128)}, s32[8,2]{0,1:T(2,128)S(1)}, f32[8,128,128]{2,1,0:T(8,128)S(1)}, s32[]{:T(128)}) %tuple.76), condition=%wide.while_cond, body=%wide.while_body.sunk | while | flops 2 | bytes 131181 | solution.py:50
  558.1 78.8 %custom-call.71 = f32[8,128,128]{1,2,0:T(8,128)S(1)} custom-call(f32[8,128,128]{2,1,0:T(8,128)S(1)} %get-tuple-element.12), custom_call_target="InvertDiagBlocksLowerTriangular" | custom-call | tf_op jit(solution)/shard_map/triangular_solve | solution.py:50
  659.3 25.5 %convolution_add_fusion = f32[64,8192]{1,0:T(8,128)} fusion(f32[64,8192]{1,0:T(8,128)S(1)} %copy-done, f32[1024,64]{0,1:T(8,128)S(1)} %constant_dynamic-update-slice_fusion.36, f32[1024,8192]{1,0:T(8,128)} %all-gather.8.cloned.1.call-done), kind=kOutput, calls=%fused_computation.2 | convolution fusion | flops 6442975232 | bytes 38010880 | tf_op jit(solution)/shard_map/kj,kc->jc/dot_general | solution.py:101
  (165 shorter events, 126.7 us)
Async XLA Ops:
  6.5 173.5 %all-gather.4.cloned.1.call-start = ((), (), s32[]{:S(2)}) async-start(), calls=%async_computation | async-start | bytes 8912896 | tf_op jit(solution)/shard_map/all_gather | solution.py:94
  24.5 86.3 %copy-start.2 = (f32[2048]{0:T(1024)S(1)}, f32[2048]{0:T(1024)}, u32[]{:S(2)}) copy-start(f32[2048]{0:T(1024)} %param.20) | copy-start | bytes 24580
  24.5 86.3 %copy-start.3 = (f32[2048]{0:T(1024)S(1)}, f32[2048]{0:T(1024)}, u32[]{:S(2)}) copy-start(f32[2048]{0:T(1024)} %param.19) | copy-start | bytes 24580
  112.8 145.0 %all-reduce.4.cloned.1.call-start = ((), (), s32[]{:S(2)}) async-start(), calls=%async_computation.1 | async-start | bytes 1048576 | tf_op jit(solution)/shard_map/psum | solution.py:95
  180.1 79.6 %copy-start = (f32[64,8192]{1,0:T(8,128)S(1)}, f32[64,8192]{1,0:T(8,128)}, u32[]{:S(2)}) copy-start(f32[64,8192]{1,0:T(8,128)} %param.11) | copy-start | bytes 6291460
  192.1 116.3 %all-gather.6.cloned.1.call-start = ((), (), s32[]{:S(2)}) async-start(), calls=%async_computation.2 | async-start | bytes 4456448 | tf_op jit(solution)/shard_map/all_gather | solution.py:96
  259.6 399.7 %all-gather.8.cloned.1.call-start = ((), (), s32[]{:S(2)}) async-start(), calls=%async_computation.3 | async-start | bytes 35651584 | tf_op jit(solution)/shard_map/all_gather | solution.py:104
  324.8 2.0 copy-start.1
Sparse Core Ops, SparseCore 0:
  112.9 67.1 all-gather.3
  192.2 60.2 all-reduce.3
  259.7 48.6 all-gather.5
  310.6 197.4 all-gather.7
where the time goes:
time: 701 us; the launch traced here: 692 us
  other arithmetic  282 us (40%)
  blocking collectives  141 us (20%)
  waiting for transfers between devices  115 us (16%)
  matrix products  92.4 us (13%)
  local copies, waits for them, and re-layouts  41.4 us (6%)
  between operations  20.1 us (3%)
    another operation x30, other arithmetic, spd_solve(): factor = jnp.linalg.cholesky(matrix)  173 us
    another operation x3, other arithmetic, spd_solve(): lax.linalg.triangular_solve(factor, halfway, left_side=True, lower=True,...  83.7 us
    psum x1, blocking collectives, body(): lax.psum((jnp.sum(turnover_effect, axis=0), jnp.sum(predicted, axis=0)),...  76 us
    all_gather x1, waiting for transfers between devices, body(): lax.all_gather(pred_anomaly, 'mem', axis=0, tiled=True)  67.3 us
    psum x1, blocking collectives, body(): misfit_sum = lax.psum(misfit_local, ('mem', 'cell'))  64.9 us
    all_gather x1, waiting for transfers between devices, body(): gram = lax.all_gather(summed[:, :local_members], 'mem', axis=1, tiled=True)  47.2 us
    dot_general x1, matrix products, body(): jnp.einsum('kj,kc->jc', local_solve, lax.all_gather(anomaly, 'mem', axis=...  25.5 us
    another operation x14, matrix products, spd_solve(): factor = jnp.linalg.cholesky(matrix)  23.3 us
  transfers between devices with their start and end apart: 4, of which 2 were waited for; matrix products, arithmetic and copies ran while one was open for 50% of the time, Pallas kernels for 0%

commit v1 on v0

v1 whole, which is shorter than its diff:
```python
import math

import jax
import jax.numpy as jnp
from jax import lax
from jax.experimental import pallas as pl
from jax.experimental.pallas import tpu as pltpu
from jax.sharding import Mesh, PartitionSpec as P

STEPS = 6
BLOCK = 128
TAPS = 4
Z = 4
Y = 4
X = 4
LANES = 128
HALF = 128
TILE = 256
CHUNK = 1024
f32 = jnp.float32

ANY_VMEM = pl.BlockSpec(memory_space=pltpu.VMEM)
ANY_SMEM = pl.BlockSpec(memory_space=pltpu.SMEM)


def mm(left, right):
    return jnp.dot(left, right, precision=lax.Precision.HIGHEST, preferred_element_type=f32)


def mm_last(left, right):
    return lax.dot_general(
        left, right, (((1,), (1,)), ((), ())),
        precision=lax.Precision.HIGHEST, preferred_element_type=f32,
    )


def forward_kernel(
    effect, base, fast, slow, init, fall, taps, weights, observed, var, pred, small, resp, coef
):
    step = pl.program_id(0)
    members, cells = effect.shape
    w = slow[...]
    f = fast[...]
    left_slow = [jnp.zeros_like(w)]
    left_fast = [jnp.zeros_like(w)]
    for _ in range(STEPS):
        left_fast.append(0.7 * f + 0.3 * f * left_slow[-1] + (1.0 - f) * left_fast[-1])
        left_slow.append(w + (1.0 - w) * left_slow[-1])
    share = [0.6 + 0.4 * left_fast[STEPS - 1 - t] for t in range(STEPS)]
    for power in range(STEPS):
        total = share[power] * init[0:1, :]
        for t in range(power + 1, STEPS):
            total = total + share[t] * fall[t - 1 - power : t - power, :]
        coef[power : power + 1, :] = total
    coef[6:7, :] = init[1:2, :] * left_fast[STEPS] + init[2:3, :] * left_slow[STEPS]
    coef[7:8, :] = -base[...]

    def rows(i, _):
        at = pl.ds(pl.multiple_of(i * 8, 8), 8)
        kept = jnp.exp(coef[7:8, :] * jnp.exp(effect[at, :]))
        total = coef[5:6, :]
        for power in range(4, -1, -1):
            total = total * kept + coef[power : power + 1, :]
        resp[at, :] = coef[6:7, :] + (1.0 - kept) * total
        return 0

    lax.fori_loop(0, members // 8, rows, 0)
    position = lax.broadcasted_iota(jnp.int32, (BLOCK, LANES), 0)
    owner = lax.broadcasted_iota(jnp.int32, (members, LANES), 1) // 32
    spread = jnp.zeros((1, LANES), f32)
    for group in range(cells // (4 * BLOCK)):
        lanes = slice(group * LANES, (group + 1) * LANES)
        table = jnp.zeros((BLOCK, LANES), f32)
        for k in range(TAPS):
            table = table + jnp.where(taps[k : k + 1, lanes] == position, weights[k : k + 1, lanes], 0.0)
        stacked = jnp.concatenate(
            [resp[:, (4 * group + b) * BLOCK : (4 * group + b + 1) * BLOCK] for b in range(4)], axis=0
        )
        product = mm(stacked, table)
        out = product[:members]
        for b in range(1, 4):
            out = jnp.where(owner == b, product[b * members : (b + 1) * members], out)
        pred[:, lanes] = out
        small[0:1, pl.ds(pl.multiple_of(step * (cells // 4) + group * LANES, LANES), LANES)] = jnp.sum(
            out, axis=0, keepdims=True
        )
        residual = observed[:, lanes] - out
        spread = spread + jnp.sum(residual * residual, axis=0, keepdims=True) / var[:, lanes]
    spread = jnp.broadcast_to(jnp.sum(spread, axis=1, keepdims=True), (1, LANES))
    tail = pl.ds(small.shape[1] - LANES, LANES)

    @pl.when(step == 0)
    def _():
        small[0:1, tail] = spread

    @pl.when(step > 0)
    def _():
        small[0:1, tail] = small[0:1, tail] + spread


def forward(effect, base, fast, slow, init, fall, taps, weights, observed, var):
    members, cells = effect.shape
    obs = taps.shape[1]
    obs_chunk = CHUNK // 4

    def wide(rows, width):
        return pl.BlockSpec((rows, width), lambda i: (0, i))

    return pl.pallas_call(
        forward_kernel,
        grid=(cells // CHUNK,),
        in_specs=[
            wide(members, CHUNK), wide(1, CHUNK), wide(1, CHUNK), wide(1, CHUNK),
            wide(3, CHUNK), wide(STEPS, CHUNK), wide(TAPS, obs_chunk), wide(TAPS, obs_chunk),
            wide(1, obs_chunk), wide(1, obs_chunk),
        ],
        out_specs=[wide(members, obs_chunk), pl.BlockSpec((1, obs + LANES), lambda i: (0, 0))],
        out_shape=[
            jax.ShapeDtypeStruct((members, obs), f32),
            jax.ShapeDtypeStruct((1, obs + LANES), f32),
        ],
        scratch_shapes=[pltpu.VMEM((members, CHUNK), f32), pltpu.VMEM((8, CHUNK), f32)],
        name="forward",
    )(effect, base, fast, slow, init, fall, taps, weights, observed, var)


def gram_kernel(
    where, p0, p1, p2, p3, c1, c2, c3, n0, n1, n2, n3, observed, var, sums, misfit, out,
    left, right, total,
):
    step = pl.program_id(0)
    zid, yid = where[0], where[1]
    members = p0.shape[0]
    member_count = members * Z * Y
    inv_root = 1.0 / math.sqrt(member_count - 1)
    mean = sums[...] / member_count
    inv_var = 1.0 / var[...]
    root_var = jnp.sqrt(var[...])
    for a, (p, n) in enumerate(((p0, n0), (p1, n1), (p2, n2), (p3, n3))):
        at = pl.multiple_of((yid ^ a) * members, members)
        left[pl.ds(at, members), :] = (p[...] - mean) * inv_root
        left[pl.ds(at + Y * members, members), :] = observed[...] + root_var * n[...] - p[...]
    for b, c in enumerate((p0, c1, c2, c3)):
        at = pl.multiple_of((zid ^ b) * members, members)
        right[pl.ds(at, members), :] = (c[...] - mean) * inv_root * inv_var

    product = mm_last(left[...], right[...])

    @pl.when(step == 0)
    def _():
        total[...] = product

    @pl.when(step > 0)
    def _():
        total[...] = total[...] + product

    @pl.when(step == pl.num_programs(0) - 1)
    def _():
        for c in range(8):
            out[c, 0:32, 0:TILE] = total[c * 32 : c * 32 + 32, :]
            out[c, 0:32, TILE : 2 * TILE] = total[TILE + c * 32 : TILE + c * 32 + 32, :]
            out[c, 32:40, :] = jnp.broadcast_to(misfit[0:1, 0:1], (8, 2 * TILE))


def gram_block(where, rows, columns, noises, observed, var, sums, misfit):
    members, obs = rows[0].shape
    width = 512

    def chunk(n):
        return pl.BlockSpec((n, width), lambda i: (0, i))

    return pl.pallas_call(
        gram_kernel,
        grid=(obs // width,),
        in_specs=[ANY_SMEM] + [chunk(members)] * 11 + [chunk(1)] * 3
        + [pl.BlockSpec((1, LANES), lambda i: (0, 0))],
        out_specs=pl.BlockSpec((8, 40, 2 * TILE), lambda i: (0, 0, 0)),
        out_shape=jax.ShapeDtypeStruct((8, 40, 2 * TILE), f32),
        scratch_shapes=[
            pltpu.VMEM((2 * TILE, width), f32),
            pltpu.VMEM((TILE, width), f32),
            pltpu.VMEM((2 * TILE, TILE), f32),
        ],
        name="gram",
    )(where, *rows, *columns, *noises, observed, var, sums, misfit)


def invert_block(rows):
    width = HALF
    count = width // 8
    rows = list(rows)
    lane = lax.broadcasted_iota(jnp.int32, (8, width), 1)
    sub = lax.broadcasted_iota(jnp.int32, (8, width), 0)

    def row(value, r):
        return jnp.broadcast_to(value[r : r + 1, :], (8, width))

    for block in range(count):
        low = 8 * block
        panel = rows[block]
        inside = (lane >= low) & (lane < low + 8)
        pivots = [jnp.broadcast_to(panel[:, low + p : low + p + 1], (8, width)) for p in range(8)]
        for r in range(8):
            heads = [row(pivots[p], r) for p in range(8)]
            inverse = 1.0 / heads[r]
            here = sub == r
            column = jnp.where(here, 0.0, pivots[r])
            for p in range(8):
                if p != r:
                    scaled = heads[p] * inverse
                    pivots[p] = jnp.where(here, scaled, pivots[p] - column * scaled)
            pivots[r] = jnp.where(here, inverse, -column * inverse)
        panel = jnp.where(inside, jnp.where(lane - low == sub, 1.0, 0.0), panel)
        terms = [pivots[p] * row(panel, p) for p in range(8)]
        while len(terms) > 1:
            terms = [terms[i] + terms[i + 1] for i in range(0, len(terms), 2)]
        solved = terms[0]
        heads = [row(solved, p) for p in range(8)]
        for step in range(1, count):
            i = (block + step) % count
            terms = [
                jnp.broadcast_to(rows[i][:, low + p : low + p + 1], (8, width)) * heads[p]
                for p in range(8)
            ]
            while len(terms) > 1:
                terms = [terms[j] + terms[j + 1] for j in range(0, len(terms), 2)]
            rows[i] = jnp.where(inside, 0.0, rows[i]) - terms[0]
        rows[block] = solved
    return rows


def factor_kernel(where, mine, other, misfit, system, inverses, halves, ahead, behind):
    core = where[2]
    scale = (f32(1024 * 16384) / misfit[0:1, 0:1])
    for z in range(Z):
        for y in range(Y):
            for x in range(X):
                piece = slice(((z * Y + y) * X + x) * 32, ((z * Y + y) * X + x) * 32 + 32)
                at = x * TILE + z * 64
                lanes = slice(y * TILE, (y + 1) * TILE)
                system[pl.ds(pl.multiple_of(at + core * 32, 32), 32), lanes] = mine[piece, :] * scale
                system[pl.ds(pl.multiple_of(at + 32 - core * 32, 32), 32), lanes] = other[piece, :] * scale
    eye = jnp.where(
        lax.broadcasted_iota(jnp.int32, (HALF, HALF), 0) == lax.broadcasted_iota(jnp.int32, (HALF, HALF), 1),
        1.0, 0.0,
    )
    for d in range(system.shape[0] // HALF):
        at = slice(d * HALF, (d + 1) * HALF)
        system[at, at] = system[at, at] + eye
    tiles = system.shape[0] // TILE

    def outer(k, _):
        top = pl.multiple_of(k * TILE, TILE)
        low = pl.multiple_of(k * TILE + HALF, HALF)

        def half(h, _):
            at = pl.multiple_of(top + h * HALF, HALF)
            block = [system[pl.ds(at + 8 * j, 8), pl.ds(at, HALF)] for j in range(HALF // 8)]
            block = invert_block(block)
            for j in range(HALF // 8):
                halves[pl.ds(pl.multiple_of(h * HALF + 8 * j, 8), 8), :] = block[j]

            @pl.when(h == 0)
            def _():
                first = halves[0:HALF, :]
                upper = system[pl.ds(top, HALF), pl.ds(low, HALF)]
                ahead[...] = mm(first, upper)
                behind[...] = mm(system[pl.ds(low, HALF), pl.ds(top, HALF)], first)
                system[pl.ds(low, HALF), pl.ds(low, HALF)] = (
                    system[pl.ds(low, HALF), pl.ds(low, HALF)] - mm(behind[...], upper)
                )

            return 0

        lax.fori_loop(0, 2, half, 0)
        second = halves[HALF:, :]
        corner = mm(second, behind[...])
        inverses[pl.ds(top, HALF), 0:HALF] = halves[0:HALF, :] + mm(ahead[...], corner)
        inverses[pl.ds(top, HALF), HALF:] = -mm(ahead[...], second)
        inverses[pl.ds(low, HALF), 0:HALF] = -corner
        inverses[pl.ds(low, HALF), HALF:] = second

        def across(t, _):
            lanes = pl.ds(pl.multiple_of(t * TILE, TILE), TILE)
            solved = mm(inverses[pl.ds(top, TILE), :], system[pl.ds(top, TILE), lanes])
            system[pl.ds(top, TILE), lanes] = solved

            def down(i, _):
                at = pl.ds(pl.multiple_of(i * TILE, TILE), TILE)
                system[at, lanes] = system[at, lanes] - mm(
                    system[at, pl.ds(top, TILE)], system[pl.ds(top, TILE), lanes]
                )
                return 0

            lax.fori_loop(k + 1, tiles, down, 0)
            return 0

        lax.fori_loop(k + 1, tiles, across, 0)
        return 0

    lax.fori_loop(0, tiles, outer, 0)


def factor(where, mine, other, misfit):
    n = TILE * Y
    return pl.pallas_call(
        factor_kernel,
        in_specs=[ANY_SMEM, ANY_VMEM, ANY_VMEM, ANY_VMEM],
        out_specs=[ANY_VMEM, ANY_VMEM],
        out_shape=[jax.ShapeDtypeStruct((n, n), f32), jax.ShapeDtypeStruct((n, TILE), f32)],
        scratch_shapes=[
            pltpu.VMEM((TILE, HALF), f32), pltpu.VMEM((HALF, HALF), f32), pltpu.VMEM((HALF, HALF), f32),
        ],
        cost_estimate=pl.CostEstimate(flops=int(2e10), bytes_accessed=int(1e7), transcendentals=0),
        name="factor",
    )(where, mine, other, misfit)


def update_kernel(where, system, inverses, rhs, misfit, *refs):
    blocks, out, value, work = refs[:4], refs[4], refs[5], refs[6]
    zid, yid = where[0], where[1]
    n = system.shape[0]
    tiles = n // TILE
    scale = (f32(1024 * 16384) / misfit[0:1, 0:1])
    for a in range(Y):
        for b in range(Z):
            at = pl.multiple_of((yid ^ a) * TILE + (zid ^ b) * 64, 64)
            value[pl.ds(at, 64), :] = blocks[a][b * 64 : (b + 1) * 64, :]
    mean = jnp.sum(value[...], axis=0, keepdims=True) / n
    inv_root = 1.0 / math.sqrt(n - 1)
    work[...] = (value[...] - mean) * inv_root
    for k in range(tiles):
        at = slice(k * TILE, (k + 1) * TILE)
        work[at, :] = mm(inverses[at, :], work[at, :])
        for i in range(k + 1, tiles):
            down = slice(i * TILE, (i + 1) * TILE)
            work[down, :] = work[down, :] - mm(system[down, at], work[at, :])
    for k in range(tiles - 2, -1, -1):
        at = slice(k * TILE, (k + 1) * TILE)
        rest = slice((k + 1) * TILE, n)
        work[at, :] = work[at, :] - mm(system[at, rest], work[rest, :])
    for z in range(Z):
        total = mm(rhs[z * Y * TILE : (z * Y + 1) * TILE, :], work[0:TILE, :])
        for y in range(1, Y):
            total = total + mm(
                rhs[(z * Y + y) * TILE : (z * Y + y + 1) * TILE, :], work[y * TILE : (y + 1) * TILE, :]
            )
        for y in range(Y):
            out[z * TILE + y * 64 : z * TILE + (y + 1) * 64, :] = (
                value[y * TILE + z * 64 : y * TILE + (z + 1) * 64, :] + scale * total[y * 64 : (y + 1) * 64, :]
            )


def update(where, system, inverses, rhs, misfit, blocks):
    n = system.shape[0]
    width = blocks[0].shape[1]
    return pl.pallas_call(
        update_kernel,
        in_specs=[ANY_SMEM] + [ANY_VMEM] * 8,
        out_specs=ANY_VMEM,
        out_shape=jax.ShapeDtypeStruct((n, width), f32),
        scratch_shapes=[pltpu.VMEM((n, width), f32), pltpu.VMEM((n, width), f32)],
        cost_estimate=pl.CostEstimate(flops=int(1e10), bytes_accessed=int(1e7), transcendentals=0),
        name="update",
    )(where, system, inverses, rhs, misfit, *blocks)


def swap(value, axis, size, bit):
    return lax.ppermute(value, axis, [(i, i ^ bit) for i in range(size)])


def body(
    turnover_effect,
    base_rate,
    fast_rate,
    slow_rate,
    init_pools,
    litterfall,
    obs_taps,
    obs_weights,
    observed,
    obs_var,
    obs_noise,
):
    members, cells = turnover_effect.shape
    obs = obs_taps.shape[0]
    zid, yid, core = lax.axis_index("z"), lax.axis_index("y"), lax.axis_index("core")
    where = jnp.stack([zid, yid, core]).astype(jnp.int32)
    observed = observed[None, :]
    obs_var = obs_var[None, :]
    noises = [obs_noise] + [swap(obs_noise, "y", Y, a) for a in range(1, Y)]
    predicted, small = forward(
        turnover_effect, base_rate[None, :], fast_rate[None, :], slow_rate[None, :],
        init_pools, litterfall, obs_taps.T, obs_weights.T, observed, obs_var,
    )
    rows = [predicted] + [swap(predicted, "y", Y, a) for a in range(1, Y)]
    columns = [swap(predicted, "z", Z, b) for b in range(1, Z)]
    for axis in ("y", "z"):
        for bit in (1, 2):
            small = small + swap(small, axis, 4, bit)
    block = gram_block(where, rows, columns, noises, observed, obs_var, small[:, :obs], small[:, obs:])
    effect, block = lax.optimization_barrier((turnover_effect, block))
    wide = cells // Z
    strip = [lax.dynamic_slice_in_dim(effect, (zid ^ b) * wide, wide, 1) for b in range(Z)]
    strip = jnp.concatenate([strip[0]] + [swap(strip[b], "z", Z, b) for b in range(1, Z)], axis=0)
    shared = jnp.sum(lax.all_to_all(block, ("x", "core"), 0, 0, tiled=False), axis=0)
    piece, right, misfit = shared[:32, :TILE], shared[:32, TILE:], shared[32:, :LANES]
    rhs = lax.all_gather(right, ("z", "y", "x", "core"), axis=0, tiled=True)
    mine = lax.all_to_all(
        jnp.broadcast_to(piece[None], (Z * Y * X, 32, TILE)), ("z", "y", "x"), 0, 0, tiled=True
    ).reshape(Z * Y * X * 32, TILE)
    other = swap(mine, "core", 2, 1)
    strip, other = lax.optimization_barrier((strip, other))
    narrow = wide // Y
    cut = [lax.dynamic_slice_in_dim(strip, (yid ^ a) * narrow, narrow, 1) for a in range(Y)]
    cut = [cut[0]] + [swap(cut[a], "y", Y, a) for a in range(1, Y)]
    system, inverses = factor(where, mine, other, misfit)
    changed = update(where, system, inverses, rhs, misfit, cut)
    return lax.all_to_all(changed, ("z", "y"), 0, 1, tiled=True)


def solution(mesh):
    grid = Mesh(mesh.devices.reshape(Z, Y, X, 2), ("z", "y", "x", "core"))
    mem, cell = ("z", "y"), ("x", "core")
    in_specs = (
        P(mem, cell),
        P(cell),
        P(cell),
        P(cell),
        P(None, cell),
        P(None, cell),
        P(cell, None),
        P(cell, None),
        P(cell),
        P(cell),
        P(mem, cell),
    )
    return jax.shard_map(
        body, mesh=grid, in_specs=in_specs, out_specs=P(mem, cell), check_vma=False
    )
```

time: 701 us -> 294 us (0.42); the launches traced: 692 us -> 294 us
  other arithmetic: 282 us -> 1.56 us
  matrix products: 92.4 us -> 0 us
  Pallas kernels: 0 us -> 85.7 us
  blocking collectives: 141 us -> 83.1 us
  waiting for transfers between devices: 115 us -> 67.2 us
  starting transfers between devices: 0.13 us -> 35.3 us
  local copies, waits for them, and re-layouts: 41.4 us -> 7.4 us
    another operation x33 -> x1, other arithmetic: 256 us -> 0.64 us  [body(): where = jnp.stack([zid, yid, core]).astype(jnp.int32)]
    psum x2 -> x0, blocking collectives: 141 us -> none  [the longest x1 76 us: body(): lax.psum((jnp.sum(turnover_effect, axis=0), jnp.sum(predicted, axis=0)),...]
    all_gather x3 -> x1, waiting for transfers between devices: 114 us -> 0.02 us  [body(): rhs = lax.all_gather(right, ('z', 'y', 'x', 'core'), axis=0, tiled=True)]
    pallas_call x0 -> x4, Pallas kernels: none -> 85.7 us  [the longest x1 48 us: factor(): pl.pallas_call(factor_kernel, in_specs=[ANY_SMEM, ANY_VMEM, ANY_VMEM, ANY...]
    all_to_all x0 -> x3, blocking collectives: none -> 83.1 us  [the longest x1 35.6 us: body(): lax.all_to_all(jnp.broadcast_to(piece[None], (Z * Y * X, 32, TILE)), ('z'...]
    ppermute x0 -> x20, waiting for transfers between devices: none -> 67.2 us  [swap(): return lax.ppermute(value, axis, [(i, i ^ bit) for i in range(size)])]
    dot_general x3 -> x0, matrix products: 47.3 us -> none  [the longest x1 25.5 us: body(): jnp.einsum('kj,kc->jc', local_solve, lax.all_gather(anomaly, 'mem', axis=...]
    another operation x44 -> x0, matrix products: 45.1 us -> none  [the longest x14 23.3 us: spd_solve(): factor = jnp.linalg.cholesky(matrix)]
  transfers between devices with their start and end apart: 4 -> 21, of which waited for: 2 -> 11; matrix products, arithmetic and copies ran while one was open for 50% -> 2% of each run, Pallas kernels for 0% -> 16%
where the time goes in v1:
time: 294 us
  Pallas kernels  85.7 us (29%)
  blocking collectives  83.1 us (28%)
  waiting for transfers between devices  67.2 us (23%)
  starting transfers between devices  35.3 us (12%)
  between operations  13.5 us (5%)
  local copies, waits for them, and re-layouts  7.4 us (3%)
    ppermute x20, waiting for transfers between devices, swap(): return lax.ppermute(value, axis, [(i, i ^ bit) for i in range(size)])  67.2 us
    pallas_call x1, Pallas kernels, factor(): pl.pallas_call(factor_kernel, in_specs=[ANY_SMEM, ANY_VMEM, ANY_VMEM, ANY...  48 us
    all_to_all x1, blocking collectives, body(): lax.all_to_all(jnp.broadcast_to(piece[None], (Z * Y * X, 32, TILE)), ('z'...  35.6 us
    ppermute x20, starting transfers between devices, swap(): return lax.ppermute(value, axis, [(i, i ^ bit) for i in range(size)])  35.3 us
    all_to_all x1, blocking collectives, body(): return lax.all_to_all(changed, ('z', 'y'), 0, 1, tiled=True)  31.5 us
    pallas_call x1, Pallas kernels, update(): pl.pallas_call(update_kernel, in_specs=[ANY_SMEM] + [ANY_VMEM] * 8, out_s...  20.6 us
    all_to_all x1, blocking collectives, body(): lax.all_to_all(block, ('x', 'core'), 0, 0, tiled=False)  16.1 us
    pallas_call x1, Pallas kernels, forward(): pl.pallas_call(forward_kernel, grid=(cells // CHUNK,), in_specs=[wide(mem...  9.25 us
  transfers between devices with their start and end apart: 21, of which 11 were waited for; matrix products, arithmetic and copies ran while one was open for 2% of the time, Pallas kernels for 16%

profile of v1, /device:TPU:0, one launch (start us, length us, event | category | flops | bytes accessed | tf_op | source)
XLA Modules:
  0.0 293.8 jit_solution(4404610063500384783)
XLA Ops:
  6.5 9.3 %forward.1 = (f32[64,2048]{1,0:T(8,128)}, f32[1,2176]{1,0:T(1,128)}) custom-call(f32[64,8192]{1,0:T(8,128)} %effect.1, f32[1,8192]{1,0:T(1,128)} %bitcast.21, f32[1,8192]{1,0:T(1,128)} %bitcast.22, f32[1,8192]{1,0:T(1,128)} %bitcast.23, f32[3,8192]{1,0:T(4,128)} %init.1, f32[6,8192]{1,0:T(8,128)} %fall.1, s32[4,2048]{1,0:T(4,128)} %bitcast.24, ...), custom_call_target="tpu_custom_call" | custom-call | tf_op jit(solution)/shard_map/forward/pallas_call | solution.py:109
  17.5 2.9 collective-permute-start.1
  20.6 2.0 collective-permute-start.3
  22.9 18.2 %collective-permute-done.9 = f32[1,2176]{1,0:T(1,128)S(1)} collective-permute-done((f32[1,2176]{1,0:T(1,128)}, f32[1,2176]{1,0:T(1,128)S(1)}, u32[]{:S(2)}, u32[]{:S(2)}) %collective-permute-start.9) | collective-permute-done | bytes 8736 | tf_op jit(solution)/shard_map/ppermute | solution.py:369
  41.8 3.4 %collective-permute-start.10 = (f32[1,2176]{1,0:T(1,128)S(1)}, f32[1,2176]{1,0:T(1,128)S(1)}, u32[]{:S(2)}, u32[]{:S(2)}) collective-permute-start(f32[1,2176]{1,0:T(1,128)S(1)} %add.36), channel_id=1, source_target_pairs={{0,16},{8,24},{16,0},{24,8},{1,17},{9,25},{17,1},{25,9},{2,18},{10... | collective-permute-start | bytes 26120 | tf_op jit(solution)/shard_map/ppermute | solution.py:369
  47.1 2.2 collective-permute-start.11
  50.9 4.1 %collective-permute-start.12 = (f32[1,2176]{1,0:T(1,128)S(1)}, f32[1,2176]{1,0:T(1,128)S(1)}, u32[]{:S(2)}, u32[]{:S(2)}) collective-permute-start(f32[1,2176]{1,0:T(1,128)S(1)} %add.38), channel_id=1, source_target_pairs={{0,64},{32,96},{64,0},{96,32},{1,65},{33,97},{65,1},{97,33},{2,66}... | collective-permute-start | bytes 26120 | tf_op jit(solution)/shard_map/ppermute | solution.py:369
  56.6 3.7 %collective-permute-start.4 = (f32[64,2048]{1,0:T(8,128)}, f32[64,2048]{1,0:T(8,128)S(1)}, u32[]{:S(2)}, u32[]{:S(2)}) collective-permute-start(f32[64,2048]{1,0:T(8,128)} %get-tuple-element.13.p0), channel_id=1, source_target_pairs={{0,64},{32,96},{64,0},{96,32},{1,65},{33,97},{65,1},{97,33},{2,66}... | collective-permute-start | bytes 1572872 | tf_op jit(solution)/shard_map/ppermute | solution.py:369
  62.6 2.9 collective-permute-start.7
  68.2 11.2 %collective-permute-done.5.c3 = f32[64,2048]{1,0:T(8,128)} collective-permute-done((f32[64,2048]{1,0:T(8,128)}, f32[64,2048]{1,0:T(8,128)}, u32[]{:S(2)}, u32[]{:S(2)}) %collective-permute-start.5) | collective-permute-done | bytes 524320 | tf_op jit(solution)/shard_map/ppermute | solution.py:369
  79.4 4.2 %collective-permute-done.7.n2 = f32[64,2048]{1,0:T(8,128)} collective-permute-done((f32[64,2048]{1,0:T(8,128)S(1)}, f32[64,2048]{1,0:T(8,128)}, u32[]{:S(2)}, u32[]{:S(2)}) %collective-permute-start.7) | collective-permute-done | bytes 524320 | tf_op jit(solution)/shard_map/ppermute | solution.py:369
  83.6 2.6 collective-permute-done.8.n3
  86.2 7.8 %gram.1 = f32[8,40,512]{2,1,0:T(8,128)} custom-call(s32[3]{0:T(128)} %pad_add_fusion.where, f32[64,2048]{1,0:T(8,128)} %get-tuple-element.13.p0, f32[64,2048]{1,0:T(8,128)} %copy-done.2, f32[64,2048]{1,0:T(8,128)} %copy-done.3, f32[64,2048]{1,0:T(8,128)} %copy-done.4, f32[64,2048]{1,0:T(8,128)} %copy-done.5, f32[64,2048]{1,0:T(8,128)} %copy-done.6, ...), custom_call_target="tpu_custom_call" | custom-call | tf_op jit(solution)/shard_map/gram/pallas_call | solution.py:172
  94.1 16.1 %all_to_all.29 = f32[8,40,512]{2,1,0:T(8,128)S(1)} all-to-all(f32[8,40,512]{2,1,0:T(8,128)} %gram.1), channel_id=1, replica_groups=mesh['z'=4,'y'=4,'x'=4,'core'=2] {'x','core'}, dimensions={0} | all-to-all | bytes 1310720 | tf_op jit(solution)/shard_map/all_to_all | solution.py:406
  111.1 35.6 %all_to_all.30 = f32[64,32,256]{2,1,0:T(8,128)} all-to-all(f32[64,32,256]{2,1,0:T(8,128)S(1)} %broadcast_in_dim.26), channel_id=1, replica_groups=mesh['z'=4,'y'=4,'x'=4,'core'=2] {'z','y','x'}, dimensions={0} | all-to-all | bytes 4194304 | tf_op jit(solution)/shard_map/all_to_all | solution.py:409
  148.1 2.0 collective-permute-start.14
  150.1 2.5 collective-permute-start.15
  152.6 11.4 %collective-permute-done.13 = f32[64,2048]{1,0:T(8,128)S(1)} collective-permute-done((f32[64,2048]{1,0:T(8,128)}, f32[64,2048]{1,0:T(8,128)S(1)}, u32[]{:S(2)}, u32[]{:S(2)}) %collective-permute-start.13) | collective-permute-done | bytes 524320 | tf_op jit(solution)/shard_map/ppermute | solution.py:369
  164.0 11.4 %collective-permute-done.14 = f32[64,2048]{1,0:T(8,128)S(1)} collective-permute-done((f32[64,2048]{1,0:T(8,128)}, f32[64,2048]{1,0:T(8,128)S(1)}, u32[]{:S(2)}, u32[]{:S(2)}) %collective-permute-start.14) | collective-permute-done | bytes 524320 | tf_op jit(solution)/shard_map/ppermute | solution.py:369
  175.4 2.4 collective-permute-done.15
  181.8 2.4 collective-permute-start.19
  184.2 48.0 %factor.1 = (f32[1024,1024]{1,0:T(8,128)}, f32[1024,256]{1,0:T(8,128)}) custom-call(s32[3]{0:T(128)} %pad_add_fusion.where, f32[2048,256]{1,0:T(8,128)} %bitcast.10.mine, f32[2048,256]{1,0:T(8,128)} %collective-permute-done.16.other, f32[8,128]{1,0:T(8,128)} %slice.23.misfit), custom_call_target="tpu_custom_call" | custom-call | flops 20000000000 | bytes 10000000 | tf_op jit(solution)/shard_map/factor/pallas_call | solution.py:306
  233.3 20.6 %update.1 = f32[1024,512]{1,0:T(8,128)} custom-call(s32[3]{0:T(128)} %pad_add_fusion.where, f32[1024,1024]{1,0:T(8,128)} %get-tuple-element.18.system, f32[1024,256]{1,0:T(8,128)} %get-tuple-element.19.inverses, f32[4096,256]{1,0:T(8,128)} %all-gather.2.cloned.1.call-done.rhs, f32[8,128]{1,0:T(8,128)} %slice.23.misfit, ...), custom_call_target="tpu_custom_call" | custom-call | flops 10000000000 | bytes 10000000 | tf_op jit(solution)/shard_map/update/pallas_call | solution.py:357
  253.9 31.5 %all_to_all.31 = f32[16,64,512]{2,1,0:T(8,128)S(1)} all-to-all(f32[16,64,512]{2,1,0:T(8,128)} %bitcast.16), channel_id=1, replica_groups=mesh['z'=4,'y'=4,'x'=4,'core'=2] {'z','y'}, dimensions={0} | all-to-all | bytes 4194304 | tf_op jit(solution)/shard_map/all_to_all | solution.py:419
  (61 shorter events, 22.0 us)
Async XLA Ops:
  6.5 54.4 %copy-start.1 = (f32[64,2048]{1,0:T(8,128)S(1)}, f32[64,2048]{1,0:T(8,128)}, u32[]{:S(2)}) copy-start(f32[64,2048]{1,0:T(8,128)} %n0.1) | copy-start | bytes 1572868
  6.5 225.7 %all-gather.2.cloned.1.call-start = ((), (), s32[]{:S(2)}) async-start(), calls=%async_computation.3 | async-start | bytes 4227072 | tf_op jit(solution)/shard_map/all_gather | solution.py:408
  15.8 44.5 %collective-permute-start = (f32[64,2048]{1,0:T(8,128)}, f32[64,2048]{1,0:T(8,128)S(1)}, u32[]{:S(2)}, u32[]{:S(2)}) collective-permute-start(f32[64,2048]{1,0:T(8,128)} %get-tuple-element.13.p0), channel_id=1, source_target_pairs={{0,8},{8,0},{16,24},{24,16},{1,9},{9,1},{17,25},{25,17},{2,10},{10... | collective-permute-start | bytes 1572872 | tf_op jit(solution)/shard_map/ppermute | solution.py:369
  17.5 43.4 %collective-permute-start.1 = (f32[64,2048]{1,0:T(8,128)}, f32[64,2048]{1,0:T(8,128)S(1)}, u32[]{:S(2)}, u32[]{:S(2)}) collective-permute-start(f32[64,2048]{1,0:T(8,128)} %get-tuple-element.13.p0), channel_id=1, source_target_pairs={{0,16},{8,24},{16,0},{24,8},{1,17},{9,25},{17,1},{25,9},{2,18},{10... | collective-permute-start | bytes 1572872 | tf_op jit(solution)/shard_map/ppermute | solution.py:369
  20.4 42.2 %collective-permute-start.2 = (f32[64,2048]{1,0:T(8,128)}, f32[64,2048]{1,0:T(8,128)S(1)}, u32[]{:S(2)}, u32[]{:S(2)}) collective-permute-start(f32[64,2048]{1,0:T(8,128)} %get-tuple-element.13.p0), channel_id=1, source_target_pairs={{0,24},{8,16},{16,8},{24,0},{1,25},{9,17},{17,9},{25,1},{2,26},{10... | collective-permute-start | bytes 1572872 | tf_op jit(solution)/shard_map/ppermute | solution.py:369
  20.6 44.9 %collective-permute-start.3 = (f32[64,2048]{1,0:T(8,128)}, f32[64,2048]{1,0:T(8,128)S(1)}, u32[]{:S(2)}, u32[]{:S(2)}) collective-permute-start(f32[64,2048]{1,0:T(8,128)} %get-tuple-element.13.p0), channel_id=1, source_target_pairs={{0,32},{32,0},{64,96},{96,64},{1,33},{33,1},{65,97},{97,65},{2,34}... | collective-permute-start | bytes 1572872 | tf_op jit(solution)/shard_map/ppermute | solution.py:369
  22.6 18.6 %collective-permute-start.9 = (f32[1,2176]{1,0:T(1,128)}, f32[1,2176]{1,0:T(1,128)S(1)}, u32[]{:S(2)}, u32[]{:S(2)}) collective-permute-start(f32[1,2176]{1,0:T(1,128)} %get-tuple-element.14), channel_id=1, source_target_pairs={{0,8},{8,0},{16,24},{24,16},{1,9},{9,1},{17,25},{25,17},{2,10},{10... | collective-permute-start | bytes 26120 | tf_op jit(solution)/shard_map/ppermute | solution.py:369
  41.8 5.2 %collective-permute-start.10 = (f32[1,2176]{1,0:T(1,128)S(1)}, f32[1,2176]{1,0:T(1,128)S(1)}, u32[]{:S(2)}, u32[]{:S(2)}) collective-permute-start(f32[1,2176]{1,0:T(1,128)S(1)} %add.36), channel_id=1, source_target_pairs={{0,16},{8,24},{16,0},{24,8},{1,17},{9,25},{17,1},{25,9},{2,18},{10... | collective-permute-start | bytes 26120 | tf_op jit(solution)/shard_map/ppermute | solution.py:369
  47.1 3.8 %collective-permute-start.11 = (f32[1,2176]{1,0:T(1,128)S(1)}, f32[1,2176]{1,0:T(1,128)S(1)}, u32[]{:S(2)}, u32[]{:S(2)}) collective-permute-start(f32[1,2176]{1,0:T(1,128)S(1)} %add.37), channel_id=1, source_target_pairs={{0,32},{32,0},{64,96},{96,64},{1,33},{33,1},{65,97},{97,65},{2,34}... | collective-permute-start | bytes 26120 | tf_op jit(solution)/shard_map/ppermute | solution.py:369
  50.9 5.7 %collective-permute-start.12 = (f32[1,2176]{1,0:T(1,128)S(1)}, f32[1,2176]{1,0:T(1,128)S(1)}, u32[]{:S(2)}, u32[]{:S(2)}) collective-permute-start(f32[1,2176]{1,0:T(1,128)S(1)} %add.38), channel_id=1, source_target_pairs={{0,64},{32,96},{64,0},{96,32},{1,65},{33,97},{65,1},{97,33},{2,66}... | collective-permute-start | bytes 26120 | tf_op jit(solution)/shard_map/ppermute | solution.py:369
  56.6 11.6 %collective-permute-start.4 = (f32[64,2048]{1,0:T(8,128)}, f32[64,2048]{1,0:T(8,128)S(1)}, u32[]{:S(2)}, u32[]{:S(2)}) collective-permute-start(f32[64,2048]{1,0:T(8,128)} %get-tuple-element.13.p0), channel_id=1, source_target_pairs={{0,64},{32,96},{64,0},{96,32},{1,65},{33,97},{65,1},{97,33},{2,66}... | collective-permute-start | bytes 1572872 | tf_op jit(solution)/shard_map/ppermute | solution.py:369
  60.3 25.9 %copy-start.2 = (f32[64,2048]{1,0:T(8,128)}, f32[64,2048]{1,0:T(8,128)S(1)}, u32[]{:S(2)}) copy-start(f32[64,2048]{1,0:T(8,128)S(1)} %collective-permute-done.p1) | copy-start | bytes 1572868
  60.3 19.1 %collective-permute-start.5 = (f32[64,2048]{1,0:T(8,128)}, f32[64,2048]{1,0:T(8,128)}, u32[]{:S(2)}, u32[]{:S(2)}) collective-permute-start(f32[64,2048]{1,0:T(8,128)} %get-tuple-element.13.p0), channel_id=1, source_target_pairs={{0,96},{32,64},{64,32},{96,0},{1,97},{33,65},{65,33},{97,1},{2,98}... | collective-permute-start | bytes 1572872 | tf_op jit(solution)/shard_map/ppermute | solution.py:369
  60.9 18.5 %collective-permute-start.6 = (f32[64,2048]{1,0:T(8,128)S(1)}, f32[64,2048]{1,0:T(8,128)}, u32[]{:S(2)}, u32[]{:S(2)}) collective-permute-start(f32[64,2048]{1,0:T(8,128)S(1)} %copy-done.1), channel_id=1, source_target_pairs={{0,8},{8,0},{16,24},{24,16},{1,9},{9,1},{17,25},{25,17},{2,10},{10... | collective-permute-start | bytes 1572872 | tf_op jit(solution)/shard_map/ppermute | solution.py:369
  62.6 21.0 %collective-permute-start.7 = (f32[64,2048]{1,0:T(8,128)S(1)}, f32[64,2048]{1,0:T(8,128)}, u32[]{:S(2)}, u32[]{:S(2)}) collective-permute-start(f32[64,2048]{1,0:T(8,128)S(1)} %copy-done.1), channel_id=1, source_target_pairs={{0,16},{8,24},{16,0},{24,8},{1,17},{9,25},{17,1},{25,9},{2,18},{10... | collective-permute-start | bytes 1572872 | tf_op jit(solution)/shard_map/ppermute | solution.py:369
  65.5 20.7 %collective-permute-start.8 = (f32[64,2048]{1,0:T(8,128)S(1)}, f32[64,2048]{1,0:T(8,128)}, u32[]{:S(2)}, u32[]{:S(2)}) collective-permute-start(f32[64,2048]{1,0:T(8,128)S(1)} %copy-done.1), channel_id=1, source_target_pairs={{0,24},{8,16},{16,8},{24,0},{1,25},{9,17},{17,9},{25,1},{2,26},{10... | collective-permute-start | bytes 1572872 | tf_op jit(solution)/shard_map/ppermute | solution.py:369
  111.1 35.6 %copy-start = (f32[64,8192]{1,0:T(8,128)S(1)}, f32[64,8192]{1,0:T(8,128)}, u32[]{:S(2)}) copy-start(f32[64,8192]{1,0:T(8,128)} %effect.1) | copy-start | bytes 6291460
  146.7 31.8 %collective-permute-start.16 = (f32[2048,256]{1,0:T(8,128)}, f32[2048,256]{1,0:T(8,128)}, u32[]{:S(2)}, u32[]{:S(2)}) collective-permute-start(f32[2048,256]{1,0:T(8,128)} %bitcast.10.mine), channel_id=1, source_target_pairs={{0,1},{1,0},{2,3},{3,2},{4,5},{5,4},{6,7},{7,6},{8,9},{9,8},{10,11... | collective-permute-start | bytes 6291464 | tf_op jit(solution)/shard_map/ppermute | solution.py:369
  147.9 16.1 %collective-permute-start.13 = (f32[64,2048]{1,0:T(8,128)}, f32[64,2048]{1,0:T(8,128)S(1)}, u32[]{:S(2)}, u32[]{:S(2)}) collective-permute-start(f32[64,2048]{1,0:T(8,128)} %get-tuple-element.28), channel_id=1, source_target_pairs={{0,32},{32,0},{64,96},{96,64},{1,33},{33,1},{65,97},{97,65},{2,34}... | collective-permute-start | bytes 1572872 | tf_op jit(solution)/shard_map/ppermute | solution.py:369
  148.1 27.3 %collective-permute-start.14 = (f32[64,2048]{1,0:T(8,128)}, f32[64,2048]{1,0:T(8,128)S(1)}, u32[]{:S(2)}, u32[]{:S(2)}) collective-permute-start(f32[64,2048]{1,0:T(8,128)} %get-tuple-element.27), channel_id=1, source_target_pairs={{0,64},{32,96},{64,0},{96,32},{1,65},{33,97},{65,1},{97,33},{2,66}... | collective-permute-start | bytes 1572872 | tf_op jit(solution)/shard_map/ppermute | solution.py:369
  150.1 27.7 %collective-permute-start.15 = (f32[64,2048]{1,0:T(8,128)S(1)}, f32[64,2048]{1,0:T(8,128)S(1)}, u32[]{:S(2)}, u32[]{:S(2)}) collective-permute-start(f32[64,2048]{1,0:T(8,128)S(1)} %get-tuple-element.26), channel_id=1, source_target_pairs={{0,96},{32,64},{64,32},{96,0},{1,97},{33,65},{65,33},{97,1},{2,98}... | collective-permute-start | bytes 1572872 | tf_op jit(solution)/shard_map/ppermute | solution.py:369
  179.5 52.7 %collective-permute-start.17 = (f32[256,512]{1,0:T(8,128)S(1)}, f32[256,512]{1,0:T(8,128)S(1)}, u32[]{:S(2)}, u32[]{:S(2)}) collective-permute-start(f32[256,512]{1,0:T(8,128)S(1)} %get-tuple-element.23), channel_id=1, source_target_pairs={{0,8},{8,0},{16,24},{24,16},{1,9},{9,1},{17,25},{25,17},{2,10},{10... | collective-permute-start | bytes 1572872 | tf_op jit(solution)/shard_map/ppermute | solution.py:369
  180.1 52.1 %collective-permute-start.18 = (f32[256,512]{1,0:T(8,128)S(1)}, f32[256,512]{1,0:T(8,128)S(1)}, u32[]{:S(2)}, u32[]{:S(2)}) collective-permute-start(f32[256,512]{1,0:T(8,128)S(1)} %get-tuple-element.22), channel_id=1, source_target_pairs={{0,16},{8,24},{16,0},{24,8},{1,17},{9,25},{17,1},{25,9},{2,18},{10... | collective-permute-start | bytes 1572872 | tf_op jit(solution)/shard_map/ppermute | solution.py:369
  181.8 50.4 %collective-permute-start.19 = (f32[256,512]{1,0:T(8,128)S(1)}, f32[256,512]{1,0:T(8,128)S(1)}, u32[]{:S(2)}, u32[]{:S(2)}) collective-permute-start(f32[256,512]{1,0:T(8,128)S(1)} %get-tuple-element.21), channel_id=1, source_target_pairs={{0,24},{8,16},{16,8},{24,0},{1,25},{9,17},{17,9},{25,1},{2,26},{10... | collective-permute-start | bytes 1572872 | tf_op jit(solution)/shard_map/ppermute | solution.py:369
  (7 other events, 90.6 us)
Sparse Core Ops, SparseCore 0:
  111.0 100.5 all-gather.1

commit v2 on v1

--- a/solution.py
+++ b/solution.py
@@ -125,7 +125,7 @@
 
 
 def gram_kernel(
-    where, p0, p1, p2, p3, c1, c2, c3, n0, n1, n2, n3, observed, var, sums, misfit, out,
+    where, p0, p1, p2, p3, c1, c2, c3, noise, observed, var, sums, misfit, out,
     left, right, total,
 ):
     step = pl.program_id(0)
@@ -136,10 +136,12 @@
     mean = sums[...] / member_count
     inv_var = 1.0 / var[...]
     root_var = jnp.sqrt(var[...])
-    for a, (p, n) in enumerate(((p0, n0), (p1, n1), (p2, n2), (p3, n3))):
+    for a, p in enumerate((p0, p1, p2, p3)):
         at = pl.multiple_of((yid ^ a) * members, members)
         left[pl.ds(at, members), :] = (p[...] - mean) * inv_root
-        left[pl.ds(at + Y * members, members), :] = observed[...] + root_var * n[...] - p[...]
+        left[pl.ds(at + Y * members, members), :] = (
+            observed[...] + root_var * noise[pl.ds(at, members), :] - p[...]
+        )
     for b, c in enumerate((p0, c1, c2, c3)):
         at = pl.multiple_of((zid ^ b) * members, members)
         right[pl.ds(at, members), :] = (c[...] - mean) * inv_root * inv_var
@@ -162,7 +164,7 @@
             out[c, 32:40, :] = jnp.broadcast_to(misfit[0:1, 0:1], (8, 2 * TILE))
 
 
-def gram_block(where, rows, columns, noises, observed, var, sums, misfit):
+def gram_block(where, rows, columns, noise, observed, var, sums, misfit):
     members, obs = rows[0].shape
     width = 512
 
@@ -172,7 +174,7 @@
     return pl.pallas_call(
         gram_kernel,
         grid=(obs // width,),
-        in_specs=[ANY_SMEM] + [chunk(members)] * 11 + [chunk(1)] * 3
+        in_specs=[ANY_SMEM] + [chunk(members)] * 7 + [chunk(members * Y)] + [chunk(1)] * 3
         + [pl.BlockSpec((1, LANES), lambda i: (0, 0))],
         out_specs=pl.BlockSpec((8, 40, 2 * TILE), lambda i: (0, 0, 0)),
         out_shape=jax.ShapeDtypeStruct((8, 40, 2 * TILE), f32),
@@ -182,7 +184,7 @@
             pltpu.VMEM((2 * TILE, TILE), f32),
         ],
         name="gram",
-    )(where, *rows, *columns, *noises, observed, var, sums, misfit)
+    )(where, *rows, *columns, noise, observed, var, sums, misfit)
 
 
 def invert_block(rows):
@@ -229,7 +231,7 @@
     return rows
 
 
-def factor_kernel(where, mine, other, misfit, system, inverses, halves, ahead, behind):
+def begin_kernel(where, mine, other, misfit, system, inverses, halves, ahead, behind):
     core = where[2]
     scale = (f32(1024 * 16384) / misfit[0:1, 0:1])
     for z in range(Z):
@@ -247,9 +249,21 @@
     for d in range(system.shape[0] // HALF):
         at = slice(d * HALF, (d + 1) * HALF)
         system[at, at] = system[at, at] + eye
+    eliminate(system, inverses, 0, halves, ahead, behind, 0, 1)
+
+
+def finish_kernel(before, system, inverses, halves, ahead, behind, arrived):
+    copy = pltpu.make_async_copy(before, system, arrived)
+    copy.start()
+    copy.wait()
+    eliminate(system, inverses, TILE, halves, ahead, behind, 1, system.shape[0] // TILE)
+
+
+def eliminate(system, inverses, offset, halves, ahead, behind, start, stop):
     tiles = system.shape[0] // TILE
 
     def outer(k, _):
+        kept = pl.multiple_of(k * TILE - offset, TILE)
         top = pl.multiple_of(k * TILE, TILE)
         low = pl.multiple_of(k * TILE + HALF, HALF)
 
@@ -275,14 +289,14 @@
         lax.fori_loop(0, 2, half, 0)
         second = halves[HALF:, :]
         corner = mm(second, behind[...])
-        inverses[pl.ds(top, HALF), 0:HALF] = halves[0:HALF, :] + mm(ahead[...], corner)
-        inverses[pl.ds(top, HALF), HALF:] = -mm(ahead[...], second)
-        inverses[pl.ds(low, HALF), 0:HALF] = -corner
-        inverses[pl.ds(low, HALF), HALF:] = second
+        inverses[pl.ds(kept, HALF), 0:HALF] = halves[0:HALF, :] + mm(ahead[...], corner)
+        inverses[pl.ds(kept, HALF), HALF:] = -mm(ahead[...], second)
+        inverses[pl.ds(kept + HALF, HALF), 0:HALF] = -corner
+        inverses[pl.ds(kept + HALF, HALF), HALF:] = second
 
         def across(t, _):
             lanes = pl.ds(pl.multiple_of(t * TILE, TILE), TILE)
-            solved = mm(inverses[pl.ds(top, TILE), :], system[pl.ds(top, TILE), lanes])
+            solved = mm(inverses[pl.ds(kept, TILE), :], system[pl.ds(top, TILE), lanes])
             system[pl.ds(top, TILE), lanes] = solved
 
             def down(i, _):
@@ -298,25 +312,45 @@
         lax.fori_loop(k + 1, tiles, across, 0)
         return 0
 
-    lax.fori_loop(0, tiles, outer, 0)
-
-
-def factor(where, mine, other, misfit):
+    lax.fori_loop(start, stop, outer, 0)
+
+
+FACTOR_SCRATCH = [
+    pltpu.VMEM((TILE, HALF), f32), pltpu.VMEM((HALF, HALF), f32), pltpu.VMEM((HALF, HALF), f32),
+]
+
+
+def cost(flops):
+    return pl.CostEstimate(flops=int(flops), bytes_accessed=int(1e7), transcendentals=0)
+
+
+def factor_begin(where, mine, other, misfit):
     n = TILE * Y
     return pl.pallas_call(
-        factor_kernel,
+        begin_kernel,
         in_specs=[ANY_SMEM, ANY_VMEM, ANY_VMEM, ANY_VMEM],
         out_specs=[ANY_VMEM, ANY_VMEM],
-        out_shape=[jax.ShapeDtypeStruct((n, n), f32), jax.ShapeDtypeStruct((n, TILE), f32)],
-        scratch_shapes=[
-            pltpu.VMEM((TILE, HALF), f32), pltpu.VMEM((HALF, HALF), f32), pltpu.VMEM((HALF, HALF), f32),
-        ],
-        cost_estimate=pl.CostEstimate(flops=int(2e10), bytes_accessed=int(1e7), transcendentals=0),
-        name="factor",
+        out_shape=[jax.ShapeDtypeStruct((n, n), f32), jax.ShapeDtypeStruct((TILE, TILE), f32)],
+        scratch_shapes=FACTOR_SCRATCH,
+        cost_estimate=cost(2e10),
+        name="factor_begin",
     )(where, mine, other, misfit)
 
 
-def update_kernel(where, system, inverses, rhs, misfit, *refs):
+def factor_finish(system):
+    n = system.shape[0]
+    return pl.pallas_call(
+        finish_kernel,
+        in_specs=[pl.BlockSpec(memory_space=pl.ANY)],
+        out_specs=[ANY_VMEM, ANY_VMEM],
+        out_shape=[jax.ShapeDtypeStruct((n, n), f32), jax.ShapeDtypeStruct((n - TILE, TILE), f32)],
+        scratch_shapes=FACTOR_SCRATCH + [pltpu.SemaphoreType.DMA],
+        cost_estimate=cost(3e10),
+        name="factor_finish",
+    )(system)
+
+
+def update_kernel(where, system, inverse, inverses, rhs, misfit, *refs):
     blocks, out, value, work = refs[:4], refs[4], refs[5], refs[6]
     zid, yid = where[0], where[1]
     n = system.shape[0]
@@ -331,7 +365,8 @@
     work[...] = (value[...] - mean) * inv_root
     for k in range(tiles):
         at = slice(k * TILE, (k + 1) * TILE)
-        work[at, :] = mm(inverses[at, :], work[at, :])
+        block = inverse[...] if k == 0 else inverses[(k - 1) * TILE : k * TILE, :]
+        work[at, :] = mm(block, work[at, :])
         for i in range(k + 1, tiles):
             down = slice(i * TILE, (i + 1) * TILE)
             work[down, :] = work[down, :] - mm(system[down, at], work[at, :])
@@ -339,30 +374,33 @@
         at = slice(k * TILE, (k + 1) * TILE)
         rest = slice((k + 1) * TILE, n)
         work[at, :] = work[at, :] - mm(system[at, rest], work[rest, :])
-    for z in range(Z):
-        total = mm(rhs[z * Y * TILE : (z * Y + 1) * TILE, :], work[0:TILE, :])
+    def combine(z, _):
+        at = pl.multiple_of(z * (Y * TILE), Y * TILE)
+        total = mm(rhs[pl.ds(at, TILE), :], work[0:TILE, :])
         for y in range(1, Y):
-            total = total + mm(
-                rhs[(z * Y + y) * TILE : (z * Y + y + 1) * TILE, :], work[y * TILE : (y + 1) * TILE, :]
+            total = total + mm(rhs[pl.ds(at + y * TILE, TILE), :], work[y * TILE : (y + 1) * TILE, :])
+        for y in range(Y):
+            out[pl.ds(pl.multiple_of(z * TILE + y * 64, 64), 64), :] = (
+                value[pl.ds(pl.multiple_of(y * TILE + z * 64, 64), 64), :]
+                + scale * total[y * 64 : (y + 1) * 64, :]
             )
-        for y in range(Y):
-            out[z * TILE + y * 64 : z * TILE + (y + 1) * 64, :] = (
-                value[y * TILE + z * 64 : y * TILE + (z + 1) * 64, :] + scale * total[y * 64 : (y + 1) * 64, :]
-            )
-
-
-def update(where, system, inverses, rhs, misfit, blocks):
+        return 0
+
+    lax.fori_loop(0, Z, combine, 0)
+
+
+def update(where, system, inverse, inverses, rhs, misfit, blocks):
     n = system.shape[0]
     width = blocks[0].shape[1]
     return pl.pallas_call(
         update_kernel,
-        in_specs=[ANY_SMEM] + [ANY_VMEM] * 8,
+        in_specs=[ANY_SMEM] + [ANY_VMEM] * 9,
         out_specs=ANY_VMEM,
         out_shape=jax.ShapeDtypeStruct((n, width), f32),
         scratch_shapes=[pltpu.VMEM((n, width), f32), pltpu.VMEM((n, width), f32)],
-        cost_estimate=pl.CostEstimate(flops=int(1e10), bytes_accessed=int(1e7), transcendentals=0),
+        cost_estimate=cost(1e10),
         name="update",
-    )(where, system, inverses, rhs, misfit, *blocks)
+    )(where, system, inverse, inverses, rhs, misfit, *blocks)
 
 
 def swap(value, axis, size, bit):
@@ -388,34 +426,41 @@
     where = jnp.stack([zid, yid, core]).astype(jnp.int32)
     observed = observed[None, :]
     obs_var = obs_var[None, :]
-    noises = [obs_noise] + [swap(obs_noise, "y", Y, a) for a in range(1, Y)]
+    noise = lax.all_gather(obs_noise, "y", axis=0, tiled=True)
     predicted, small = forward(
         turnover_effect, base_rate[None, :], fast_rate[None, :], slow_rate[None, :],
         init_pools, litterfall, obs_taps.T, obs_weights.T, observed, obs_var,
     )
+    small = small + sum(swap(small, "y", Y, a) for a in range(1, Y))
+    small, predicted = lax.optimization_barrier((small, predicted))
     rows = [predicted] + [swap(predicted, "y", Y, a) for a in range(1, Y)]
-    columns = [swap(predicted, "z", Z, b) for b in range(1, Z)]
-    for axis in ("y", "z"):
-        for bit in (1, 2):
-            small = small + swap(small, axis, 4, bit)
-    block = gram_block(where, rows, columns, noises, observed, obs_var, small[:, :obs], small[:, obs:])
-    effect, block = lax.optimization_barrier((turnover_effect, block))
-    wide = cells // Z
-    strip = [lax.dynamic_slice_in_dim(effect, (zid ^ b) * wide, wide, 1) for b in range(Z)]
-    strip = jnp.concatenate([strip[0]] + [swap(strip[b], "z", Z, b) for b in range(1, Z)], axis=0)
+    small = small + sum(swap(small, "z", Z, b) for b in range(1, Z))
+    small, ready = lax.optimization_barrier((small, predicted))
+    columns = [swap(ready, "z", Z, b) for b in range(1, Z)]
+    block = gram_block(where, rows, columns, noise, observed, obs_var, small[:, :obs], small[:, obs:])
     shared = jnp.sum(lax.all_to_all(block, ("x", "core"), 0, 0, tiled=False), axis=0)
     piece, right, misfit = shared[:32, :TILE], shared[:32, TILE:], shared[32:, :LANES]
     rhs = lax.all_gather(right, ("z", "y", "x", "core"), axis=0, tiled=True)
     mine = lax.all_to_all(
         jnp.broadcast_to(piece[None], (Z * Y * X, 32, TILE)), ("z", "y", "x"), 0, 0, tiled=True
     ).reshape(Z * Y * X * 32, TILE)
+    effect, mine = lax.optimization_barrier((turnover_effect, mine))
     other = swap(mine, "core", 2, 1)
-    strip, other = lax.optimization_barrier((strip, other))
+    wide = cells // Z
+    strip = [lax.dynamic_slice_in_dim(effect, (zid ^ b) * wide, wide, 1) for b in range(Z)]
+    strip = [strip[0]] + [swap(strip[b], "z", Z, b) for b in range(1, Z)]
+    system, inverse = factor_begin(where, mine, other, misfit)
+    strip, system = lax.optimization_barrier((strip, system))
     narrow = wide // Y
-    cut = [lax.dynamic_slice_in_dim(strip, (yid ^ a) * narrow, narrow, 1) for a in range(Y)]
+    cut = [
+        jnp.concatenate(
+            [lax.dynamic_slice_in_dim(part, (yid ^ a) * narrow, narrow, 1) for part in strip], axis=0
+        )
+        for a in range(Y)
+    ]
     cut = [cut[0]] + [swap(cut[a], "y", Y, a) for a in range(1, Y)]
-    system, inverses = factor(where, mine, other, misfit)
-    changed = update(where, system, inverses, rhs, misfit, cut)
+    system, inverses = factor_finish(system)
+    changed = update(where, system, inverse, inverses, rhs, misfit, cut)
     return lax.all_to_all(changed, ("z", "y"), 0, 1, tiled=True)
 
 

time: 294 us -> 265 us (0.901)
  blocking collectives: 83.1 us -> 48 us
  Pallas kernels: 85.7 us -> 91 us
  waiting for transfers between devices: 67.2 us -> 63.7 us
    all_to_all x1 -> x0, blocking collectives: 35.6 us -> none  [body(): lax.all_to_all(jnp.broadcast_to(piece[None], (Z * Y * X, 32, TILE)), ('z'...]
    ppermute x20 -> x19, waiting for transfers between devices: 67.2 us -> 33.2 us  [swap(): return lax.ppermute(value, axis, [(i, i ^ bit) for i in range(size)])]
    all_to_all x0 -> x1, waiting for transfers between devices: none -> 29 us  [body(): lax.all_to_all(jnp.broadcast_to(piece[None], (Z * Y * X, 32, TILE)), ('z'...]
    all_to_all x0 -> x1, starting transfers between devices: none -> 8.24 us  [body(): lax.all_to_all(jnp.broadcast_to(piece[None], (Z * Y * X, 32, TILE)), ('z'...]
    ppermute x20 -> x19, starting transfers between devices: 35.3 us -> 29 us  [swap(): return lax.ppermute(value, axis, [(i, i ^ bit) for i in range(size)])]
    pallas_call x2 -> x3, Pallas kernels: 68.6 us -> 74 us  [the longest x1 34.3 us: factor_finish(): pl.pallas_call(finish_kernel, in_specs=[pl.BlockSpec(memory_space=pl.ANY)...]
  transfers between devices with their start and end apart: 21 -> 22, of which waited for: 11 -> 9; matrix products, arithmetic and copies ran while one was open for 2% -> 2% of each run, Pallas kernels for 16% -> 23%
where the time goes in v2:
time: 265 us; the launch traced here: 264 us
  Pallas kernels  91 us (34%)
  waiting for transfers between devices  63.7 us (24%)
  blocking collectives  48 us (18%)
  starting transfers between devices  37.3 us (14%)
  between operations  13.5 us (5%)
  local copies, waits for them, and re-layouts  8.51 us (3%)
    pallas_call x1, Pallas kernels, factor_finish(): pl.pallas_call(finish_kernel, in_specs=[pl.BlockSpec(memory_space=pl.ANY)...  34.3 us
    ppermute x19, waiting for transfers between devices, swap(): return lax.ppermute(value, axis, [(i, i ^ bit) for i in range(size)])  33.2 us
    all_to_all x1, blocking collectives, body(): return lax.all_to_all(changed, ('z', 'y'), 0, 1, tiled=True)  32 us
    ppermute x19, starting transfers between devices, swap(): return lax.ppermute(value, axis, [(i, i ^ bit) for i in range(size)])  29 us
    all_to_all x1, waiting for transfers between devices, body(): lax.all_to_all(jnp.broadcast_to(piece[None], (Z * Y * X, 32, TILE)), ('z'...  29 us
    pallas_call x1, Pallas kernels, update(): pl.pallas_call(update_kernel, in_specs=[ANY_SMEM] + [ANY_VMEM] * 9, out_s...  21.6 us
    pallas_call x1, Pallas kernels, factor_begin(): pl.pallas_call(begin_kernel, in_specs=[ANY_SMEM, ANY_VMEM, ANY_VMEM, ANY_...  18.1 us
    all_to_all x1, blocking collectives, body(): lax.all_to_all(block, ('x', 'core'), 0, 0, tiled=False)  16.1 us
  transfers between devices with their start and end apart: 22, of which 9 were waited for; matrix products, arithmetic and copies ran while one was open for 2% of the time, Pallas kernels for 23%

profile of v2, /device:TPU:0, one launch (start us, length us, event | category | flops | bytes accessed | tf_op | source)
XLA Modules:
  0.0 264.5 jit_solution(4448338345340876054)
XLA Ops:
  7.3 9.2 %forward.1 = (f32[64,2048]{1,0:T(8,128)}, f32[1,2176]{1,0:T(1,128)}) custom-call(f32[64,8192]{1,0:T(8,128)} %effect.1, f32[1,8192]{1,0:T(1,128)} %bitcast.21, f32[1,8192]{1,0:T(1,128)} %bitcast.22, f32[1,8192]{1,0:T(1,128)} %bitcast.23, f32[3,8192]{1,0:T(4,128)} %init.1, f32[6,8192]{1,0:T(8,128)} %fall.1, s32[4,2048]{1,0:T(4,128)} %bitcast.24, ...), custom_call_target="tpu_custom_call" | custom-call | tf_op jit(solution)/shard_map/forward/pallas_call | solution.py:109
  16.5 1.7 collective-permute-start
  18.2 2.9 %collective-permute-start.1 = (f32[1,2176]{1,0:T(1,128)}, f32[1,2176]{1,0:T(1,128)S(1)}, u32[]{:S(2)}, u32[]{:S(2)}) collective-permute-start(f32[1,2176]{1,0:T(1,128)} %get-tuple-element.22), channel_id=1, source_target_pairs={{0,16},{8,24},{16,0},{24,8},{1,17},{9,25},{17,1},{25,9},{2,18},{10... | collective-permute-start | bytes 26120 | tf_op jit(solution)/shard_map/ppermute | solution.py:407
  21.2 2.3 collective-permute-done.1
  23.6 2.6 collective-permute-done.2
  26.9 2.0 collective-permute-start.6
  28.9 3.7 %collective-permute-start.7 = (f32[1,2176]{1,0:T(1,128)S(1)}, f32[1,2176]{1,0:T(1,128)S(1)}, u32[]{:S(2)}, u32[]{:S(2)}) collective-permute-start(f32[1,2176]{1,0:T(1,128)S(1)} %add_add_fusion.1), channel_id=1, source_target_pairs={{0,64},{32,96},{64,0},{96,32},{1,65},{33,97},{65,1},{97,33},{2,66}... | collective-permute-start | bytes 26120 | tf_op jit(solution)/shard_map/ppermute | solution.py:407
  34.2 3.2 %collective-permute-start.5 = (f32[64,2048]{1,0:T(8,128)}, f32[64,2048]{1,0:T(8,128)S(1)}, u32[]{:S(2)}, u32[]{:S(2)}) collective-permute-start(f32[64,2048]{1,0:T(8,128)} %get-tuple-element.26.p0), channel_id=1, source_target_pairs={{0,24},{8,16},{16,8},{24,0},{1,25},{9,17},{17,9},{25,1},{2,26},{10... | collective-permute-start | bytes 1572872 | tf_op jit(solution)/shard_map/ppermute | solution.py:407
  37.5 1.7 collective-permute-start.10
  40.8 12.5 %collective-permute-done.3.p1 = f32[64,2048]{1,0:T(8,128)S(1)} collective-permute-done((f32[64,2048]{1,0:T(8,128)}, f32[64,2048]{1,0:T(8,128)S(1)}, u32[]{:S(2)}, u32[]{:S(2)}) %collective-permute-start.3) | collective-permute-done | bytes 524320 | tf_op jit(solution)/shard_map/ppermute | solution.py:407
  56.6 8.1 %collective-permute-done.4.p2 = f32[64,2048]{1,0:T(8,128)S(1)} collective-permute-done((f32[64,2048]{1,0:T(8,128)}, f32[64,2048]{1,0:T(8,128)S(1)}, u32[]{:S(2)}, u32[]{:S(2)}) %collective-permute-start.4) | collective-permute-done | bytes 524320 | tf_op jit(solution)/shard_map/ppermute | solution.py:407
  66.2 7.8 %gram.1 = f32[8,40,512]{2,1,0:T(8,128)} custom-call(s32[3]{0:T(128)} %pad_add_fusion.where, f32[64,2048]{1,0:T(8,128)} %get-tuple-element.26.p0, f32[64,2048]{1,0:T(8,128)} %copy-done.1, f32[64,2048]{1,0:T(8,128)} %copy-done.2, f32[64,2048]{1,0:T(8,128)} %copy-done.3, f32[64,2048]{1,0:T(8,128)} %copy-done.6, f32[64,2048]{1,0:T(8,128)} %copy-done.4, ...), custom_call_target="tpu_custom_call" | custom-call | tf_op jit(solution)/shard_map/gram/pallas_call | solution.py:174
  74.0 16.1 %all_to_all.29 = f32[8,40,512]{2,1,0:T(8,128)S(1)} all-to-all(f32[8,40,512]{2,1,0:T(8,128)} %gram.1), channel_id=1, replica_groups=mesh['z'=4,'y'=4,'x'=4,'core'=2] {'x','core'}, dimensions={0} | all-to-all | bytes 1310720 | tf_op jit(solution)/shard_map/all_to_all | solution.py:441
  92.3 8.2 %all-to-all-start.1 = ((f32[64,32,256]{2,1,0:T(8,128)}), f32[64,32,256]{2,1,0:T(8,128)}, u32[]{:S(2)}, u32[]{:S(2)}) async-start(f32[64,32,256]{2,1,0:T(8,128)} %broadcast_in_dim.26), calls=%async_computation.1 | async-start | bytes 4194304 | tf_op jit(solution)/shard_map/all_to_all | solution.py:444
  101.3 29.0 %all-to-all-done.1 = f32[64,32,256]{2,1,0:T(8,128)} async-done(((f32[64,32,256]{2,1,0:T(8,128)}), f32[64,32,256]{2,1,0:T(8,128)}, u32[]{:S(2)}, u32[]{:S(2)}) %all-to-all-start.1) | async-done | bytes 2097184 | tf_op jit(solution)/shard_map/all_to_all | solution.py:444
  132.3 2.0 collective-permute-start.13
  134.3 2.5 collective-permute-start.14
  136.8 18.1 %factor_begin.1 = (f32[1024,1024]{1,0:T(8,128)}, f32[256,256]{1,0:T(8,128)}) custom-call(s32[3]{0:T(128)} %pad_add_fusion.where, f32[2048,256]{1,0:T(8,128)} %bitcast.10.mine, f32[2048,256]{1,0:T(8,128)} %collective-permute-done.15.other, f32[8,128]{1,0:T(8,128)} %slice.21.misfit), custom_call_target="tpu_custom_call" | custom-call | flops 20000000000 | bytes 10000000 | tf_op jit(solution)/shard_map/factor_begin/pallas_call | solution.py:329
  154.9 4.5 %collective-permute-done.13 = f32[64,2048]{1,0:T(8,128)S(1)} collective-permute-done((f32[64,2048]{1,0:T(8,128)}, f32[64,2048]{1,0:T(8,128)S(1)}, u32[]{:S(2)}, u32[]{:S(2)}) %collective-permute-start.13) | collective-permute-done | bytes 524320 | tf_op jit(solution)/shard_map/ppermute | solution.py:407
  159.3 2.4 collective-permute-done.14
  163.0 1.9 collective-permute-start.17
  166.4 34.3 %factor_finish.1 = (f32[1024,1024]{1,0:T(8,128)}, f32[768,256]{1,0:T(8,128)}) custom-call(f32[1024,1024]{1,0:T(8,128)} %get-tuple-element.31.before), custom_call_target="tpu_custom_call" | custom-call | flops 30000001024 | bytes 10000000 | tf_op jit(solution)/shard_map/factor_finish/pallas_call | solution.py:342
  202.5 21.6 %update.1 = f32[1024,512]{1,0:T(8,128)} custom-call(s32[3]{0:T(128)} %pad_add_fusion.where, f32[1024,1024]{1,0:T(8,128)} %get-tuple-element.32.system, f32[256,256]{1,0:T(8,128)} %get-tuple-element.33.inverse, f32[768,256]{1,0:T(8,128)} %get-tuple-element.34.inverses, f32[4096,256]{1,0:T(8,128)} %all-gather.5.cloned.1.call-done.rhs, f32[8,128]{1,0:T(8,128)} %slice.21.misfit, ...), custom_call_target="tpu_custom_call" | custom-call | flops 10000000000 | bytes 10000000 | tf_op jit(solution)/shard_map/update/pallas_call | solution.py:395
  224.1 32.0 %all_to_all.30 = f32[16,64,512]{2,1,0:T(8,128)S(1)} all-to-all(f32[16,64,512]{2,1,0:T(8,128)} %bitcast.16), channel_id=1, replica_groups=mesh['z'=4,'y'=4,'x'=4,'core'=2] {'z','y'}, dimensions={0} | all-to-all | bytes 4194304 | tf_op jit(solution)/shard_map/all_to_all | solution.py:464
  (64 shorter events, 20.7 us)
Async XLA Ops:
  6.5 58.9 %all-gather.3.cloned.1.call-start = ((), (), s32[]{:S(2)}) async-start(), calls=%async_computation.3 | async-start | bytes 2621440 | tf_op jit(solution)/shard_map/all_gather | solution.py:429
  16.5 4.8 %collective-permute-start = (f32[1,2176]{1,0:T(1,128)}, f32[1,2176]{1,0:T(1,128)S(1)}, u32[]{:S(2)}, u32[]{:S(2)}) collective-permute-start(f32[1,2176]{1,0:T(1,128)} %get-tuple-element.22), channel_id=1, source_target_pairs={{0,8},{8,0},{16,24},{24,16},{1,9},{9,1},{17,25},{25,17},{2,10},{10... | collective-permute-start | bytes 26120 | tf_op jit(solution)/shard_map/ppermute | solution.py:407
  18.2 5.4 %collective-permute-start.1 = (f32[1,2176]{1,0:T(1,128)}, f32[1,2176]{1,0:T(1,128)S(1)}, u32[]{:S(2)}, u32[]{:S(2)}) collective-permute-start(f32[1,2176]{1,0:T(1,128)} %get-tuple-element.22), channel_id=1, source_target_pairs={{0,16},{8,24},{16,0},{24,8},{1,17},{9,25},{17,1},{25,9},{2,18},{10... | collective-permute-start | bytes 26120 | tf_op jit(solution)/shard_map/ppermute | solution.py:407
  21.1 5.1 %collective-permute-start.2 = (f32[1,2176]{1,0:T(1,128)}, f32[1,2176]{1,0:T(1,128)S(1)}, u32[]{:S(2)}, u32[]{:S(2)}) collective-permute-start(f32[1,2176]{1,0:T(1,128)} %get-tuple-element.22), channel_id=1, source_target_pairs={{0,24},{8,16},{16,8},{24,0},{1,25},{9,17},{17,9},{25,1},{2,26},{10... | collective-permute-start | bytes 26120 | tf_op jit(solution)/shard_map/ppermute | solution.py:407
  26.9 7.3 %collective-permute-start.6 = (f32[1,2176]{1,0:T(1,128)S(1)}, f32[1,2176]{1,0:T(1,128)S(1)}, u32[]{:S(2)}, u32[]{:S(2)}) collective-permute-start(f32[1,2176]{1,0:T(1,128)S(1)} %add_add_fusion.1), channel_id=1, source_target_pairs={{0,32},{32,0},{64,96},{96,64},{1,33},{33,1},{65,97},{97,65},{2,34}... | collective-permute-start | bytes 26120 | tf_op jit(solution)/shard_map/ppermute | solution.py:407
  28.9 8.4 %collective-permute-start.7 = (f32[1,2176]{1,0:T(1,128)S(1)}, f32[1,2176]{1,0:T(1,128)S(1)}, u32[]{:S(2)}, u32[]{:S(2)}) collective-permute-start(f32[1,2176]{1,0:T(1,128)S(1)} %add_add_fusion.1), channel_id=1, source_target_pairs={{0,64},{32,96},{64,0},{96,32},{1,65},{33,97},{65,1},{97,33},{2,66}... | collective-permute-start | bytes 26120 | tf_op jit(solution)/shard_map/ppermute | solution.py:407
  32.6 4.9 %collective-permute-start.8 = (f32[1,2176]{1,0:T(1,128)S(1)}, f32[1,2176]{1,0:T(1,128)S(1)}, u32[]{:S(2)}, u32[]{:S(2)}) collective-permute-start(f32[1,2176]{1,0:T(1,128)S(1)} %add_add_fusion.1), channel_id=1, source_target_pairs={{0,96},{32,64},{64,32},{96,0},{1,97},{33,65},{65,33},{97,1},{2,98}... | collective-permute-start | bytes 26120 | tf_op jit(solution)/shard_map/ppermute | solution.py:407
  32.6 20.6 %collective-permute-start.3 = (f32[64,2048]{1,0:T(8,128)}, f32[64,2048]{1,0:T(8,128)S(1)}, u32[]{:S(2)}, u32[]{:S(2)}) collective-permute-start(f32[64,2048]{1,0:T(8,128)} %get-tuple-element.26.p0), channel_id=1, source_target_pairs={{0,8},{8,0},{16,24},{24,16},{1,9},{9,1},{17,25},{25,17},{2,10},{10... | collective-permute-start | bytes 1572872 | tf_op jit(solution)/shard_map/ppermute | solution.py:407
  32.6 32.1 %collective-permute-start.4 = (f32[64,2048]{1,0:T(8,128)}, f32[64,2048]{1,0:T(8,128)S(1)}, u32[]{:S(2)}, u32[]{:S(2)}) collective-permute-start(f32[64,2048]{1,0:T(8,128)} %get-tuple-element.26.p0), channel_id=1, source_target_pairs={{0,16},{8,24},{16,0},{24,8},{1,17},{9,25},{17,1},{25,9},{2,18},{10... | collective-permute-start | bytes 1572872 | tf_op jit(solution)/shard_map/ppermute | solution.py:407
  34.2 30.5 %collective-permute-start.5 = (f32[64,2048]{1,0:T(8,128)}, f32[64,2048]{1,0:T(8,128)S(1)}, u32[]{:S(2)}, u32[]{:S(2)}) collective-permute-start(f32[64,2048]{1,0:T(8,128)} %get-tuple-element.26.p0), channel_id=1, source_target_pairs={{0,24},{8,16},{16,8},{24,0},{1,25},{9,17},{17,9},{25,1},{2,26},{10... | collective-permute-start | bytes 1572872 | tf_op jit(solution)/shard_map/ppermute | solution.py:407
  37.5 27.2 %collective-permute-start.10 = (f32[64,2048]{1,0:T(8,128)}, f32[64,2048]{1,0:T(8,128)S(1)}, u32[]{:S(2)}, u32[]{:S(2)}) collective-permute-start(f32[64,2048]{1,0:T(8,128)} %get-tuple-element.26.p0), channel_id=1, source_target_pairs={{0,64},{32,96},{64,0},{96,32},{1,65},{33,97},{65,1},{97,33},{2,66}... | collective-permute-start | bytes 1572872 | tf_op jit(solution)/shard_map/ppermute | solution.py:407
  39.2 25.5 %collective-permute-start.11 = (f32[64,2048]{1,0:T(8,128)}, f32[64,2048]{1,0:T(8,128)S(1)}, u32[]{:S(2)}, u32[]{:S(2)}) collective-permute-start(f32[64,2048]{1,0:T(8,128)} %get-tuple-element.26.p0), channel_id=1, source_target_pairs={{0,96},{32,64},{64,32},{96,0},{1,97},{33,65},{65,33},{97,1},{2,98}... | collective-permute-start | bytes 1572872 | tf_op jit(solution)/shard_map/ppermute | solution.py:407
  53.3 12.1 %copy-start.1 = (f32[64,2048]{1,0:T(8,128)}, f32[64,2048]{1,0:T(8,128)S(1)}, u32[]{:S(2)}) copy-start(f32[64,2048]{1,0:T(8,128)S(1)} %collective-permute-done.3.p1) | copy-start | bytes 1572868
  53.3 12.1 %collective-permute-start.9 = (f32[64,2048]{1,0:T(8,128)}, f32[64,2048]{1,0:T(8,128)S(1)}, u32[]{:S(2)}, u32[]{:S(2)}) collective-permute-start(f32[64,2048]{1,0:T(8,128)} %get-tuple-element.26.p0), channel_id=1, source_target_pairs={{0,32},{32,0},{64,96},{96,64},{1,33},{33,1},{65,97},{97,65},{2,34}... | collective-permute-start | bytes 1572872 | tf_op jit(solution)/shard_map/ppermute | solution.py:407
  92.3 38.6 %copy-start = (f32[64,8192]{1,0:T(8,128)S(1)}, f32[64,8192]{1,0:T(8,128)}, u32[]{:S(2)}) copy-start(f32[64,8192]{1,0:T(8,128)} %effect.1) | copy-start | bytes 6291460
  92.3 38.0 %all-to-all-start.1 = ((f32[64,32,256]{2,1,0:T(8,128)}), f32[64,32,256]{2,1,0:T(8,128)}, u32[]{:S(2)}, u32[]{:S(2)}) async-start(f32[64,32,256]{2,1,0:T(8,128)} %broadcast_in_dim.26), calls=%async_computation.1 | async-start | bytes 4194304 | tf_op jit(solution)/shard_map/all_to_all | solution.py:444
  100.5 101.1 %all-gather.5.cloned.1.call-start = ((), (), s32[]{:S(2)}) async-start(), calls=%async_computation.4 | async-start | bytes 4227072 | tf_op jit(solution)/shard_map/all_gather | solution.py:443
  130.3 6.5 %collective-permute-start.15 = (f32[2048,256]{1,0:T(8,128)}, f32[2048,256]{1,0:T(8,128)}, u32[]{:S(2)}, u32[]{:S(2)}) collective-permute-start(f32[2048,256]{1,0:T(8,128)} %bitcast.10.mine), channel_id=1, source_target_pairs={{0,1},{1,0},{2,3},{3,2},{4,5},{5,4},{6,7},{7,6},{8,9},{9,8},{10,11... | collective-permute-start | bytes 6291464 | tf_op jit(solution)/shard_map/ppermute | solution.py:407
  132.1 22.8 %collective-permute-start.12 = (f32[64,2048]{1,0:T(8,128)}, f32[64,2048]{1,0:T(8,128)S(1)}, u32[]{:S(2)}, u32[]{:S(2)}) collective-permute-start(f32[64,2048]{1,0:T(8,128)} %get-tuple-element.41), channel_id=1, source_target_pairs={{0,32},{32,0},{64,96},{96,64},{1,33},{33,1},{65,97},{97,65},{2,34}... | collective-permute-start | bytes 1572872 | tf_op jit(solution)/shard_map/ppermute | solution.py:407
  132.3 27.0 %collective-permute-start.13 = (f32[64,2048]{1,0:T(8,128)}, f32[64,2048]{1,0:T(8,128)S(1)}, u32[]{:S(2)}, u32[]{:S(2)}) collective-permute-start(f32[64,2048]{1,0:T(8,128)} %get-tuple-element.40), channel_id=1, source_target_pairs={{0,64},{32,96},{64,0},{96,32},{1,65},{33,97},{65,1},{97,33},{2,66}... | collective-permute-start | bytes 1572872 | tf_op jit(solution)/shard_map/ppermute | solution.py:407
  134.3 27.5 %collective-permute-start.14 = (f32[64,2048]{1,0:T(8,128)S(1)}, f32[64,2048]{1,0:T(8,128)S(1)}, u32[]{:S(2)}, u32[]{:S(2)}) collective-permute-start(f32[64,2048]{1,0:T(8,128)S(1)} %get-tuple-element.39), channel_id=1, source_target_pairs={{0,96},{32,64},{64,32},{96,0},{1,97},{33,65},{65,33},{97,1},{2,98}... | collective-permute-start | bytes 1572872 | tf_op jit(solution)/shard_map/ppermute | solution.py:407
  162.0 39.6 %collective-permute-start.18 = (f32[256,512]{1,0:T(8,128)S(1)}, f32[256,512]{1,0:T(8,128)S(1)}, u32[]{:S(2)}, u32[]{:S(2)}) collective-permute-start(f32[256,512]{1,0:T(8,128)S(1)} %pad_maximum_fusion.3), channel_id=1, source_target_pairs={{0,24},{8,16},{16,8},{24,0},{1,25},{9,17},{17,9},{25,1},{2,26},{10... | collective-permute-start | bytes 1572872 | tf_op jit(solution)/shard_map/ppermute | solution.py:407
  163.0 38.5 %collective-permute-start.17 = (f32[256,512]{1,0:T(8,128)S(1)}, f32[256,512]{1,0:T(8,128)S(1)}, u32[]{:S(2)}, u32[]{:S(2)}) collective-permute-start(f32[256,512]{1,0:T(8,128)S(1)} %pad_maximum_fusion.2), channel_id=1, source_target_pairs={{0,16},{8,24},{16,0},{24,8},{1,17},{9,25},{17,1},{25,9},{2,18},{10... | collective-permute-start | bytes 1572872 | tf_op jit(solution)/shard_map/ppermute | solution.py:407
  164.9 36.7 %collective-permute-start.16 = (f32[256,512]{1,0:T(8,128)S(1)}, f32[256,512]{1,0:T(8,128)}, u32[]{:S(2)}, u32[]{:S(2)}) collective-permute-start(f32[256,512]{1,0:T(8,128)S(1)} %pad_maximum_fusion.1), channel_id=1, source_target_pairs={{0,8},{8,0},{16,24},{24,16},{1,9},{9,1},{17,25},{25,17},{2,10},{10... | collective-permute-start | bytes 1572872 | tf_op jit(solution)/shard_map/ppermute | solution.py:407
  (7 other events, 6.8 us)
Sparse Core Ops, SparseCore 0:
  9.0 39.2 all-gather.2
  104.5 91.0 all-gather.4

commit v3 on v2

--- a/solution.py
+++ b/solution.py
@@ -125,26 +125,26 @@
 
 
 def gram_kernel(
-    where, p0, p1, p2, p3, c1, c2, c3, noise, observed, var, sums, misfit, out,
-    left, right, total,
+    where, p1, p2, p3, e0, e1, e2, e3, noise, observed, var, out, left, right, total
 ):
     step = pl.program_id(0)
     zid, yid = where[0], where[1]
-    members = p0.shape[0]
+    members = p1.shape[0]
     member_count = members * Z * Y
     inv_root = 1.0 / math.sqrt(member_count - 1)
-    mean = sums[...] / member_count
+    tails = e0[members:, :] + e1[members:, :] + e2[members:, :] + e3[members:, :]
+    mean = tails[0:1, :] / member_count
     inv_var = 1.0 / var[...]
     root_var = jnp.sqrt(var[...])
-    for a, p in enumerate((p0, p1, p2, p3)):
+    for a, p in enumerate((e0, p1, p2, p3)):
         at = pl.multiple_of((yid ^ a) * members, members)
-        left[pl.ds(at, members), :] = (p[...] - mean) * inv_root
+        left[pl.ds(at, members), :] = (p[0:members, :] - mean) * inv_root
         left[pl.ds(at + Y * members, members), :] = (
-            observed[...] + root_var * noise[pl.ds(at, members), :] - p[...]
+            observed[...] + root_var * noise[pl.ds(at, members), :] - p[0:members, :]
         )
-    for b, c in enumerate((p0, c1, c2, c3)):
+    for b, e in enumerate((e0, e1, e2, e3)):
         at = pl.multiple_of((zid ^ b) * members, members)
-        right[pl.ds(at, members), :] = (c[...] - mean) * inv_root * inv_var
+        right[pl.ds(at, members), :] = (e[0:members, :] - mean) * inv_root * inv_var
 
     product = mm_last(left[...], right[...])
 
@@ -161,10 +161,10 @@
         for c in range(8):
             out[c, 0:32, 0:TILE] = total[c * 32 : c * 32 + 32, :]
             out[c, 0:32, TILE : 2 * TILE] = total[TILE + c * 32 : TILE + c * 32 + 32, :]
-            out[c, 32:40, :] = jnp.broadcast_to(misfit[0:1, 0:1], (8, 2 * TILE))
-
-
-def gram_block(where, rows, columns, noise, observed, var, sums, misfit):
+            out[c, 32:40, :] = jnp.broadcast_to(tails[1:2, 0:1], (8, 2 * TILE))
+
+
+def gram_block(where, rows, columns, noise, observed, var):
     members, obs = rows[0].shape
     width = 512
 
@@ -174,8 +174,8 @@
     return pl.pallas_call(
         gram_kernel,
         grid=(obs // width,),
-        in_specs=[ANY_SMEM] + [chunk(members)] * 7 + [chunk(members * Y)] + [chunk(1)] * 3
-        + [pl.BlockSpec((1, LANES), lambda i: (0, 0))],
+        in_specs=[ANY_SMEM] + [chunk(members)] * 3 + [chunk(members + 8)] * 4
+        + [chunk(members * Y)] + [chunk(1)] * 2,
         out_specs=pl.BlockSpec((8, 40, 2 * TILE), lambda i: (0, 0, 0)),
         out_shape=jax.ShapeDtypeStruct((8, 40, 2 * TILE), f32),
         scratch_shapes=[
@@ -183,8 +183,13 @@
             pltpu.VMEM((TILE, width), f32),
             pltpu.VMEM((2 * TILE, TILE), f32),
         ],
+        cost_estimate=cost(8e9),
         name="gram",
-    )(where, *rows, *columns, noise, observed, var, sums, misfit)
+    )(where, *rows, *columns, noise, observed, var)
+
+
+def cost(flops):
+    return pl.CostEstimate(flops=int(flops), bytes_accessed=int(1e7), transcendentals=0)
 
 
 def invert_block(rows):
@@ -201,6 +206,10 @@
         low = 8 * block
         panel = rows[block]
         inside = (lane >= low) & (lane < low + 8)
+        early = {
+            i: [jnp.broadcast_to(rows[i][:, low + p : low + p + 1], (8, width)) for p in range(8)]
+            for i in range(block + 1, min(block + 3, count))
+        }
         pivots = [jnp.broadcast_to(panel[:, low + p : low + p + 1], (8, width)) for p in range(8)]
         for r in range(8):
             heads = [row(pivots[p], r) for p in range(8)]
@@ -218,22 +227,28 @@
             terms = [terms[i] + terms[i + 1] for i in range(0, len(terms), 2)]
         solved = terms[0]
         heads = [row(solved, p) for p in range(8)]
-        for step in range(1, count):
-            i = (block + step) % count
-            terms = [
-                jnp.broadcast_to(rows[i][:, low + p : low + p + 1], (8, width)) * heads[p]
-                for p in range(8)
-            ]
-            while len(terms) > 1:
-                terms = [terms[j] + terms[j + 1] for j in range(0, len(terms), 2)]
-            rows[i] = jnp.where(inside, 0.0, rows[i]) - terms[0]
-        rows[block] = solved
+        zero = jnp.zeros((8, width), f32)
+        masked = [
+            zero if block <= i <= block + 2 else jnp.where(inside, rows[i], 0.0) for i in range(count)
+        ]
+        spread = [solved if i == block else zero for i in range(count)]
+        product = mm(jnp.concatenate(masked, axis=0), jnp.concatenate(spread, axis=0))
+        for i in range(count):
+            if i == block:
+                rows[i] = solved
+            elif i in early:
+                terms = [early[i][p] * heads[p] for p in range(8)]
+                while len(terms) > 1:
+                    terms = [terms[j] + terms[j + 1] for j in range(0, len(terms), 2)]
+                rows[i] = jnp.where(inside, 0.0, rows[i]) - terms[0]
+            else:
+                rows[i] = jnp.where(inside, 0.0, rows[i]) - product[8 * i : 8 * i + 8]
     return rows
 
 
-def begin_kernel(where, mine, other, misfit, system, inverses, halves, ahead, behind):
+def begin_kernel(where, mine, other, misfit, system, inverses, last, halves, ahead, behind):
     core = where[2]
-    scale = (f32(1024 * 16384) / misfit[0:1, 0:1])
+    scale = f32(1024 * 16384) / misfit[0:1, 0:1]
     for z in range(Z):
         for y in range(Y):
             for x in range(X):
@@ -249,21 +264,44 @@
     for d in range(system.shape[0] // HALF):
         at = slice(d * HALF, (d + 1) * HALF)
         system[at, at] = system[at, at] + eye
-    eliminate(system, inverses, 0, halves, ahead, behind, 0, 1)
-
-
-def finish_kernel(before, system, inverses, halves, ahead, behind, arrived):
+    eliminate(system, inverses, 0, last, halves, ahead, behind)
+
+
+def finish_kernel(before, earlier, system, inverses, last, halves, ahead, behind, arrived):
     copy = pltpu.make_async_copy(before, system, arrived)
     copy.start()
+    last[...] = earlier[TILE:, :]
     copy.wait()
-    eliminate(system, inverses, TILE, halves, ahead, behind, 1, system.shape[0] // TILE)
-
-
-def eliminate(system, inverses, offset, halves, ahead, behind, start, stop):
+    eliminate(system, inverses, 2, last, halves, ahead, behind)
+
+
+def eliminate(system, inverses, start, last, halves, ahead, behind):
     tiles = system.shape[0] // TILE
 
-    def outer(k, _):
-        kept = pl.multiple_of(k * TILE - offset, TILE)
+    def spread(k):
+        top = pl.multiple_of(k * TILE, TILE)
+
+        def across(t, _):
+            lanes = pl.ds(pl.multiple_of(t * TILE, TILE), TILE)
+            system[pl.ds(top, TILE), lanes] = mm(last[...], system[pl.ds(top, TILE), lanes])
+
+            def down(i, _):
+                at = pl.ds(pl.multiple_of(i * TILE, TILE), TILE)
+                system[at, lanes] = system[at, lanes] - mm(
+                    system[at, pl.ds(top, TILE)], system[pl.ds(top, TILE), lanes]
+                )
+                return 0
+
+            lax.fori_loop(k + 1, tiles, down, 0)
+            return 0
+
+        lax.fori_loop(k + 1, tiles, across, 0)
+
+    def stage(k, _):
+        @pl.when(k > 0)
+        def _():
+            spread(k - 1)
+
         top = pl.multiple_of(k * TILE, TILE)
         low = pl.multiple_of(k * TILE + HALF, HALF)
 
@@ -289,39 +327,20 @@
         lax.fori_loop(0, 2, half, 0)
         second = halves[HALF:, :]
         corner = mm(second, behind[...])
-        inverses[pl.ds(kept, HALF), 0:HALF] = halves[0:HALF, :] + mm(ahead[...], corner)
-        inverses[pl.ds(kept, HALF), HALF:] = -mm(ahead[...], second)
-        inverses[pl.ds(kept + HALF, HALF), 0:HALF] = -corner
-        inverses[pl.ds(kept + HALF, HALF), HALF:] = second
-
-        def across(t, _):
-            lanes = pl.ds(pl.multiple_of(t * TILE, TILE), TILE)
-            solved = mm(inverses[pl.ds(kept, TILE), :], system[pl.ds(top, TILE), lanes])
-            system[pl.ds(top, TILE), lanes] = solved
-
-            def down(i, _):
-                at = pl.ds(pl.multiple_of(i * TILE, TILE), TILE)
-                system[at, lanes] = system[at, lanes] - mm(
-                    system[at, pl.ds(top, TILE)], system[pl.ds(top, TILE), lanes]
-                )
-                return 0
-
-            lax.fori_loop(k + 1, tiles, down, 0)
-            return 0
-
-        lax.fori_loop(k + 1, tiles, across, 0)
+        last[0:HALF, 0:HALF] = halves[0:HALF, :] + mm(ahead[...], corner)
+        last[0:HALF, HALF:] = -mm(ahead[...], second)
+        last[HALF:, 0:HALF] = -corner
+        last[HALF:, HALF:] = second
+        inverses[pl.ds(pl.multiple_of((k - start) * TILE, TILE), TILE), :] = last[...]
         return 0
 
-    lax.fori_loop(start, stop, outer, 0)
+    lax.fori_loop(start, start + 2, stage, 0)
 
 
 FACTOR_SCRATCH = [
-    pltpu.VMEM((TILE, HALF), f32), pltpu.VMEM((HALF, HALF), f32), pltpu.VMEM((HALF, HALF), f32),
+    pltpu.VMEM((TILE, TILE), f32), pltpu.VMEM((TILE, HALF), f32), pltpu.VMEM((HALF, HALF), f32),
+    pltpu.VMEM((HALF, HALF), f32),
 ]
-
-
-def cost(flops):
-    return pl.CostEstimate(flops=int(flops), bytes_accessed=int(1e7), transcendentals=0)
 
 
 def factor_begin(where, mine, other, misfit):
@@ -330,43 +349,41 @@
         begin_kernel,
         in_specs=[ANY_SMEM, ANY_VMEM, ANY_VMEM, ANY_VMEM],
         out_specs=[ANY_VMEM, ANY_VMEM],
-        out_shape=[jax.ShapeDtypeStruct((n, n), f32), jax.ShapeDtypeStruct((TILE, TILE), f32)],
+        out_shape=[jax.ShapeDtypeStruct((n, n), f32), jax.ShapeDtypeStruct((2 * TILE, TILE), f32)],
         scratch_shapes=FACTOR_SCRATCH,
         cost_estimate=cost(2e10),
         name="factor_begin",
     )(where, mine, other, misfit)
 
 
-def factor_finish(system):
+def factor_finish(system, earlier):
     n = system.shape[0]
     return pl.pallas_call(
         finish_kernel,
-        in_specs=[pl.BlockSpec(memory_space=pl.ANY)],
+        in_specs=[pl.BlockSpec(memory_space=pl.ANY), ANY_VMEM],
         out_specs=[ANY_VMEM, ANY_VMEM],
-        out_shape=[jax.ShapeDtypeStruct((n, n), f32), jax.ShapeDtypeStruct((n - TILE, TILE), f32)],
+        out_shape=[jax.ShapeDtypeStruct((n, n), f32), jax.ShapeDtypeStruct((2 * TILE, TILE), f32)],
         scratch_shapes=FACTOR_SCRATCH + [pltpu.SemaphoreType.DMA],
-        cost_estimate=cost(3e10),
+        cost_estimate=cost(2e10),
         name="factor_finish",
-    )(system)
-
-
-def update_kernel(where, system, inverse, inverses, rhs, misfit, *refs):
-    blocks, out, value, work = refs[:4], refs[4], refs[5], refs[6]
+    )(system, earlier)
+
+
+def solve_kernel(where, system, earlier, later, b0, b1, b2, b3, work):
     zid, yid = where[0], where[1]
     n = system.shape[0]
     tiles = n // TILE
-    scale = (f32(1024 * 16384) / misfit[0:1, 0:1])
-    for a in range(Y):
+    for a, block in enumerate((b0, b1, b2, b3)):
         for b in range(Z):
             at = pl.multiple_of((yid ^ a) * TILE + (zid ^ b) * 64, 64)
-            value[pl.ds(at, 64), :] = blocks[a][b * 64 : (b + 1) * 64, :]
-    mean = jnp.sum(value[...], axis=0, keepdims=True) / n
+            work[pl.ds(at, 64), :] = block[b * 64 : (b + 1) * 64, :]
+    mean = jnp.sum(work[...], axis=0, keepdims=True) / n
     inv_root = 1.0 / math.sqrt(n - 1)
-    work[...] = (value[...] - mean) * inv_root
+    work[...] = (work[...] - mean) * inv_root
     for k in range(tiles):
         at = slice(k * TILE, (k + 1) * TILE)
-        block = inverse[...] if k == 0 else inverses[(k - 1) * TILE : k * TILE, :]
-        work[at, :] = mm(block, work[at, :])
+        source = earlier if k < 2 else later
+        work[at, :] = mm(source[(k % 2) * TILE : (k % 2 + 1) * TILE, :], work[at, :])
         for i in range(k + 1, tiles):
             down = slice(i * TILE, (i + 1) * TILE)
             work[down, :] = work[down, :] - mm(system[down, at], work[at, :])
@@ -374,33 +391,40 @@
         at = slice(k * TILE, (k + 1) * TILE)
         rest = slice((k + 1) * TILE, n)
         work[at, :] = work[at, :] - mm(system[at, rest], work[rest, :])
-    def combine(z, _):
-        at = pl.multiple_of(z * (Y * TILE), Y * TILE)
-        total = mm(rhs[pl.ds(at, TILE), :], work[0:TILE, :])
-        for y in range(1, Y):
-            total = total + mm(rhs[pl.ds(at + y * TILE, TILE), :], work[y * TILE : (y + 1) * TILE, :])
-        for y in range(Y):
-            out[pl.ds(pl.multiple_of(z * TILE + y * 64, 64), 64), :] = (
-                value[pl.ds(pl.multiple_of(y * TILE + z * 64, 64), 64), :]
-                + scale * total[y * 64 : (y + 1) * 64, :]
-            )
-        return 0
-
-    lax.fori_loop(0, Z, combine, 0)
-
-
-def update(where, system, inverse, inverses, rhs, misfit, blocks):
-    n = system.shape[0]
-    width = blocks[0].shape[1]
+
+
+def solve(where, system, earlier, later, blocks):
     return pl.pallas_call(
-        update_kernel,
-        in_specs=[ANY_SMEM] + [ANY_VMEM] * 9,
+        solve_kernel,
+        in_specs=[ANY_SMEM] + [ANY_VMEM] * 7,
         out_specs=ANY_VMEM,
+        out_shape=jax.ShapeDtypeStruct((system.shape[0], blocks[0].shape[1]), f32),
+        cost_estimate=cost(5e9),
+        name="solve",
+    )(where, system, earlier, later, *blocks)
+
+
+def combine_kernel(rhs, work, misfit, out):
+    scale = f32(1024 * 16384) / misfit[0:1, 0:1]
+    total = mm(rhs[0:TILE, :], work[0:TILE, :])
+    for y in range(1, Y):
+        total = total + mm(rhs[y * TILE : (y + 1) * TILE, :], work[y * TILE : (y + 1) * TILE, :])
+    out[...] = scale * total
+
+
+def combine(rhs, work, misfit):
+    n, width = work.shape
+    return pl.pallas_call(
+        combine_kernel,
+        grid=(Z,),
+        in_specs=[
+            pl.BlockSpec((Y * TILE, TILE), lambda z: (z, 0)), ANY_VMEM, ANY_VMEM,
+        ],
+        out_specs=pl.BlockSpec((TILE, width), lambda z: (z, 0)),
         out_shape=jax.ShapeDtypeStruct((n, width), f32),
-        scratch_shapes=[pltpu.VMEM((n, width), f32), pltpu.VMEM((n, width), f32)],
-        cost_estimate=cost(1e10),
-        name="update",
-    )(where, system, inverse, inverses, rhs, misfit, *blocks)
+        cost_estimate=cost(6e9),
+        name="combine",
+    )(rhs, work, misfit)
 
 
 def swap(value, axis, size, bit):
@@ -433,11 +457,12 @@
     )
     small = small + sum(swap(small, "y", Y, a) for a in range(1, Y))
     small, predicted = lax.optimization_barrier((small, predicted))
-    rows = [predicted] + [swap(predicted, "y", Y, a) for a in range(1, Y)]
-    small = small + sum(swap(small, "z", Z, b) for b in range(1, Z))
-    small, ready = lax.optimization_barrier((small, predicted))
-    columns = [swap(ready, "z", Z, b) for b in range(1, Z)]
-    block = gram_block(where, rows, columns, noise, observed, obs_var, small[:, :obs], small[:, obs:])
+    rows = [swap(predicted, "y", Y, a) for a in range(1, Y)]
+    extended = jnp.concatenate(
+        [predicted, small[:, :obs], jnp.broadcast_to(small[:, obs : obs + 1], (7, obs))], axis=0
+    )
+    columns = [extended] + [swap(extended, "z", Z, b) for b in range(1, Z)]
+    block = gram_block(where, rows, columns, noise, observed, obs_var)
     shared = jnp.sum(lax.all_to_all(block, ("x", "core"), 0, 0, tiled=False), axis=0)
     piece, right, misfit = shared[:32, :TILE], shared[:32, TILE:], shared[32:, :LANES]
     rhs = lax.all_gather(right, ("z", "y", "x", "core"), axis=0, tiled=True)
@@ -459,9 +484,10 @@
         for a in range(Y)
     ]
     cut = [cut[0]] + [swap(cut[a], "y", Y, a) for a in range(1, Y)]
-    system, inverses = factor_finish(system)
-    changed = update(where, system, inverse, inverses, rhs, misfit, cut)
-    return lax.all_to_all(changed, ("z", "y"), 0, 1, tiled=True)
+    system, later = factor_finish(system, inverse)
+    work = solve(where, system, inverse, later, cut)
+    change = combine(rhs, work, misfit)
+    return turnover_effect + lax.all_to_all(change, ("z", "y"), 0, 1, tiled=True)
 
 
 def solution(mesh):

time: 265 us -> 271 us (1.023)
  waiting for transfers between devices: 63.7 us -> 73.4 us
  starting transfers between devices: 37.3 us -> 28.3 us
  other arithmetic: 2.42 us -> 6.73 us
    ppermute x19 -> x16, waiting for transfers between devices: 33.2 us -> 43 us  [swap(): return lax.ppermute(value, axis, [(i, i ^ bit) for i in range(size)])]
    pallas_call x1, Pallas kernels: 34.3 us -> 24.7 us  [factor_finish(): pl.pallas_call(finish_kernel, in_specs=[pl.BlockSpec(memory_space=pl.ANY)...]
    ppermute x19 -> x16, starting transfers between devices: 29 us -> 20.5 us  [swap(): return lax.ppermute(value, axis, [(i, i ^ bit) for i in range(size)])]
    pallas_call x1, Pallas kernels: 18.1 us -> 25.3 us  [factor_begin(): pl.pallas_call(begin_kernel, in_specs=[ANY_SMEM, ANY_VMEM, ANY_VMEM, ANY_...]
    dynamic_slice x2, local copies, waits for them, and re-layouts: 0.18 us -> 3.06 us  [body(): lax.dynamic_slice_in_dim(part, (yid ^ a) * narrow, narrow, 1)]
    pallas_call x1 -> x2, Pallas kernels: 21.6 us -> 23.7 us  [the longest x1 13.3 us: solve(): pl.pallas_call(solve_kernel, in_specs=[ANY_SMEM] + [ANY_VMEM] * 7, out_sp...]
  transfers between devices with their start and end apart: 22 -> 19, of which waited for: 9 -> 7; matrix products, arithmetic and copies ran while one was open for 2% -> 4% of each run, Pallas kernels for 23% -> 27%
where the time goes in v3:
time: 271 us
  Pallas kernels  90.6 us (33%)
  waiting for transfers between devices  73.4 us (27%)
  blocking collectives  48.2 us (18%)
  starting transfers between devices  28.3 us (10%)
  between operations  13.6 us (5%)
  local copies, waits for them, and re-layouts  9.72 us (4%)
  other arithmetic  6.73 us (2%)
    ppermute x16, waiting for transfers between devices, swap(): return lax.ppermute(value, axis, [(i, i ^ bit) for i in range(size)])  43 us
    all_to_all x1, blocking collectives, body(): lax.all_to_all(change, ('z', 'y'), 0, 1, tiled=True)  32.1 us
    all_to_all x1, waiting for transfers between devices, body(): lax.all_to_all(jnp.broadcast_to(piece[None], (Z * Y * X, 32, TILE)), ('z'...  29 us
    pallas_call x1, Pallas kernels, factor_begin(): pl.pallas_call(begin_kernel, in_specs=[ANY_SMEM, ANY_VMEM, ANY_VMEM, ANY_...  25.3 us
    pallas_call x1, Pallas kernels, factor_finish(): pl.pallas_call(finish_kernel, in_specs=[pl.BlockSpec(memory_space=pl.ANY)...  24.7 us
    ppermute x16, starting transfers between devices, swap(): return lax.ppermute(value, axis, [(i, i ^ bit) for i in range(size)])  20.5 us
    all_to_all x1, blocking collectives, body(): lax.all_to_all(block, ('x', 'core'), 0, 0, tiled=False)  16.1 us
    pallas_call x1, Pallas kernels, solve(): pl.pallas_call(solve_kernel, in_specs=[ANY_SMEM] + [ANY_VMEM] * 7, out_sp...  13.3 us
  transfers between devices with their start and end apart: 19, of which 7 were waited for; matrix products, arithmetic and copies ran while one was open for 4% of the time, Pallas kernels for 27%

profile of v3, /device:TPU:0, one launch (start us, length us, event | category | flops | bytes accessed | tf_op | source)
XLA Modules:
  0.0 270.5 jit_solution(17698716424856917010)
XLA Ops:
  7.3 9.2 %forward.1 = (f32[64,2048]{1,0:T(8,128)}, f32[1,2176]{1,0:T(1,128)}) custom-call(f32[64,8192]{1,0:T(8,128)} %effect.1, f32[1,8192]{1,0:T(1,128)} %bitcast.19, f32[1,8192]{1,0:T(1,128)} %bitcast.20, f32[1,8192]{1,0:T(1,128)} %bitcast.21, f32[3,8192]{1,0:T(4,128)} %init.1, f32[6,8192]{1,0:T(8,128)} %fall.1, s32[4,2048]{1,0:T(4,128)} %bitcast.22, ...), custom_call_target="tpu_custom_call" | custom-call | tf_op jit(solution)/shard_map/forward/pallas_call | solution.py:109
  16.5 1.7 collective-permute-start
  18.2 2.9 %collective-permute-start.1 = (f32[1,2176]{1,0:T(1,128)}, f32[1,2176]{1,0:T(1,128)S(1)}, u32[]{:S(2)}, u32[]{:S(2)}) collective-permute-start(f32[1,2176]{1,0:T(1,128)} %get-tuple-element.20), channel_id=1, source_target_pairs={{0,16},{8,24},{16,0},{24,8},{1,17},{9,25},{17,1},{25,9},{2,18},{10... | collective-permute-start | bytes 26120 | tf_op jit(solution)/shard_map/ppermute | solution.py:431
  21.2 2.3 collective-permute-done.1
  23.6 2.6 collective-permute-done.2
  29.4 2.0 collective-permute-start.6
  31.4 3.7 %collective-permute-start.7 = (f32[72,2048]{1,0:T(8,128)S(1)}, f32[72,2048]{1,0:T(8,128)S(1)}, u32[]{:S(2)}, u32[]{:S(2)}) collective-permute-start(f32[72,2048]{1,0:T(8,128)S(1)} %maximum_maximum_fusion.e0), channel_id=1, source_target_pairs={{0,64},{32,96},{64,0},{96,32},{1,65},{33,97},{65,1},{97,33},{2,66}... | collective-permute-start | bytes 1769480 | tf_op jit(solution)/shard_map/ppermute | solution.py:431
  36.7 16.5 %collective-permute-done.3.p1 = f32[64,2048]{1,0:T(8,128)S(1)} collective-permute-done((f32[64,2048]{1,0:T(8,128)}, f32[64,2048]{1,0:T(8,128)S(1)}, u32[]{:S(2)}, u32[]{:S(2)}) %collective-permute-start.3) | collective-permute-done | bytes 524320 | tf_op jit(solution)/shard_map/ppermute | solution.py:431
  54.5 10.4 %collective-permute-done.4.p2 = f32[64,2048]{1,0:T(8,128)} collective-permute-done((f32[64,2048]{1,0:T(8,128)}, f32[64,2048]{1,0:T(8,128)}, u32[]{:S(2)}, u32[]{:S(2)}) %collective-permute-start.4) | collective-permute-done | bytes 524320 | tf_op jit(solution)/shard_map/ppermute | solution.py:431
  64.9 10.5 %collective-permute-done.5.p3 = f32[64,2048]{1,0:T(8,128)} collective-permute-done((f32[64,2048]{1,0:T(8,128)}, f32[64,2048]{1,0:T(8,128)}, u32[]{:S(2)}, u32[]{:S(2)}) %collective-permute-start.5) | collective-permute-done | bytes 524320 | tf_op jit(solution)/shard_map/ppermute | solution.py:431
  76.6 7.7 %gram.1 = f32[8,40,512]{2,1,0:T(8,128)} custom-call(s32[3]{0:T(128)} %pad_add_fusion.where, f32[64,2048]{1,0:T(8,128)} %copy-done.5, f32[64,2048]{1,0:T(8,128)} %collective-permute-done.4.p2, f32[64,2048]{1,0:T(8,128)} %collective-permute-done.5.p3, f32[72,2048]{1,0:T(8,128)} %copy-done.1, f32[72,2048]{1,0:T(8,128)} %copy-done.2, f32[72,2048]{1,0:T(8,128)} %copy-done.3, ...), custom_call_target="tpu_custom_call" | custom-call | flops 8000000000 | bytes 10000000 | tf_op jit(solution)/shard_map/gram/pallas_call | solution.py:174
  84.4 16.1 %all_to_all.29 = f32[8,40,512]{2,1,0:T(8,128)S(1)} all-to-all(f32[8,40,512]{2,1,0:T(8,128)} %gram.1), channel_id=1, replica_groups=mesh['z'=4,'y'=4,'x'=4,'core'=2] {'x','core'}, dimensions={0} | all-to-all | bytes 1310720 | tf_op jit(solution)/shard_map/all_to_all | solution.py:466
  102.7 7.8 %all-to-all-start.1 = ((f32[64,32,256]{2,1,0:T(8,128)}), f32[64,32,256]{2,1,0:T(8,128)}, u32[]{:S(2)}, u32[]{:S(2)}) async-start(f32[64,32,256]{2,1,0:T(8,128)} %broadcast_in_dim.35), calls=%async_computation.1 | async-start | bytes 4194304 | tf_op jit(solution)/shard_map/all_to_all | solution.py:469
  111.3 29.0 %all-to-all-done.1 = f32[64,32,256]{2,1,0:T(8,128)} async-done(((f32[64,32,256]{2,1,0:T(8,128)}), f32[64,32,256]{2,1,0:T(8,128)}, u32[]{:S(2)}, u32[]{:S(2)}) %all-to-all-start.1) | async-done | bytes 2097184 | tf_op jit(solution)/shard_map/all_to_all | solution.py:469
  142.7 2.3 collective-permute-start.11
  145.6 25.3 %factor_begin.1 = (f32[1024,1024]{1,0:T(8,128)}, f32[512,256]{1,0:T(8,128)}) custom-call(s32[3]{0:T(128)} %pad_add_fusion.where, f32[2048,256]{1,0:T(8,128)} %bitcast.11.mine, f32[2048,256]{1,0:T(8,128)} %collective-permute-done.12.other, f32[8,128]{1,0:T(8,128)} %slice.22.misfit), custom_call_target="tpu_custom_call" | custom-call | flops 20000000000 | bytes 10000000 | tf_op jit(solution)/shard_map/factor_begin/pallas_call | solution.py:348
  172.0 1.9 constant_dynamic-slice_fusion
  174.6 2.2 collective-permute-start.14
  179.1 24.7 %factor_finish.1 = (f32[1024,1024]{1,0:T(8,128)}, f32[512,256]{1,0:T(8,128)}) custom-call(f32[1024,1024]{1,0:T(8,128)} %get-tuple-element.27.before, f32[512,256]{1,0:T(8,128)} %get-tuple-element.28.earlier), custom_call_target="tpu_custom_call" | custom-call | flops 20000000000 | bytes 10000000 | tf_op jit(solution)/shard_map/factor_finish/pallas_call | solution.py:361
  203.7 1.8 pad_maximum_fusion.b0
  206.1 13.3 %solve.1.work = f32[1024,512]{1,0:T(8,128)} custom-call(s32[3]{0:T(128)} %pad_add_fusion.where, f32[1024,1024]{1,0:T(8,128)} %get-tuple-element.29.system, f32[512,256]{1,0:T(8,128)} %get-tuple-element.28.earlier, f32[512,256]{1,0:T(8,128)} %get-tuple-element.30.later, f32[256,512]{1,0:T(8,128)} %pad_maximum_fusion.b0, ...), custom_call_target="tpu_custom_call" | custom-call | flops 5000000000 | bytes 10000000 | tf_op jit(solution)/shard_map/solve/pallas_call | solution.py:397
  219.3 10.4 %combine.1 = f32[1024,512]{1,0:T(8,128)} custom-call(f32[4096,256]{1,0:T(8,128)} %all-gather.5.cloned.1.call-done.rhs, f32[1024,512]{1,0:T(8,128)} %solve.1.work, f32[8,128]{1,0:T(8,128)} %slice.22.misfit), custom_call_target="tpu_custom_call" | custom-call | flops 6000000000 | bytes 10000000 | tf_op jit(solution)/shard_map/combine/pallas_call | solution.py:417
  229.7 32.1 %all_to_all.30 = f32[16,64,512]{2,1,0:T(8,128)S(1)} all-to-all(f32[16,64,512]{2,1,0:T(8,128)} %bitcast.18), channel_id=1, replica_groups=mesh['z'=4,'y'=4,'x'=4,'core'=2] {'z','y'}, dimensions={0} | all-to-all | bytes 4194304 | tf_op jit(solution)/shard_map/all_to_all | solution.py:490
  262.1 1.6 add.59
  (56 shorter events, 18.9 us)
Async XLA Ops:
  6.5 68.9 %all-gather.3.cloned.1.call-start = ((), (), s32[]{:S(2)}) async-start(), calls=%async_computation.3 | async-start | bytes 2621440 | tf_op jit(solution)/shard_map/all_gather | solution.py:453
  16.5 4.8 %collective-permute-start = (f32[1,2176]{1,0:T(1,128)}, f32[1,2176]{1,0:T(1,128)S(1)}, u32[]{:S(2)}, u32[]{:S(2)}) collective-permute-start(f32[1,2176]{1,0:T(1,128)} %get-tuple-element.20), channel_id=1, source_target_pairs={{0,8},{8,0},{16,24},{24,16},{1,9},{9,1},{17,25},{25,17},{2,10},{10... | collective-permute-start | bytes 26120 | tf_op jit(solution)/shard_map/ppermute | solution.py:431
  18.2 5.4 %collective-permute-start.1 = (f32[1,2176]{1,0:T(1,128)}, f32[1,2176]{1,0:T(1,128)S(1)}, u32[]{:S(2)}, u32[]{:S(2)}) collective-permute-start(f32[1,2176]{1,0:T(1,128)} %get-tuple-element.20), channel_id=1, source_target_pairs={{0,16},{8,24},{16,0},{24,8},{1,17},{9,25},{17,1},{25,9},{2,18},{10... | collective-permute-start | bytes 26120 | tf_op jit(solution)/shard_map/ppermute | solution.py:431
  21.1 5.1 %collective-permute-start.2 = (f32[1,2176]{1,0:T(1,128)}, f32[1,2176]{1,0:T(1,128)S(1)}, u32[]{:S(2)}, u32[]{:S(2)}) collective-permute-start(f32[1,2176]{1,0:T(1,128)} %get-tuple-element.20), channel_id=1, source_target_pairs={{0,24},{8,16},{16,8},{24,0},{1,25},{9,17},{17,9},{25,1},{2,26},{10... | collective-permute-start | bytes 26120 | tf_op jit(solution)/shard_map/ppermute | solution.py:431
  27.5 25.7 %collective-permute-start.3 = (f32[64,2048]{1,0:T(8,128)}, f32[64,2048]{1,0:T(8,128)S(1)}, u32[]{:S(2)}, u32[]{:S(2)}) collective-permute-start(f32[64,2048]{1,0:T(8,128)} %get-tuple-element.22), channel_id=1, source_target_pairs={{0,8},{8,0},{16,24},{24,16},{1,9},{9,1},{17,25},{25,17},{2,10},{10... | collective-permute-start | bytes 1572872 | tf_op jit(solution)/shard_map/ppermute | solution.py:431
  29.4 46.1 %copy-start.1 = (f32[72,2048]{1,0:T(8,128)}, f32[72,2048]{1,0:T(8,128)S(1)}, u32[]{:S(2)}) copy-start(f32[72,2048]{1,0:T(8,128)S(1)} %maximum_maximum_fusion.e0) | copy-start | bytes 1769476
  29.4 46.0 %collective-permute-start.6 = (f32[72,2048]{1,0:T(8,128)S(1)}, f32[72,2048]{1,0:T(8,128)S(1)}, u32[]{:S(2)}, u32[]{:S(2)}) collective-permute-start(f32[72,2048]{1,0:T(8,128)S(1)} %maximum_maximum_fusion.e0), channel_id=1, source_target_pairs={{0,32},{32,0},{64,96},{96,64},{1,33},{33,1},{65,97},{97,65},{2,34}... | collective-permute-start | bytes 1769480 | tf_op jit(solution)/shard_map/ppermute | solution.py:431
  31.4 44.0 %collective-permute-start.7 = (f32[72,2048]{1,0:T(8,128)S(1)}, f32[72,2048]{1,0:T(8,128)S(1)}, u32[]{:S(2)}, u32[]{:S(2)}) collective-permute-start(f32[72,2048]{1,0:T(8,128)S(1)} %maximum_maximum_fusion.e0), channel_id=1, source_target_pairs={{0,64},{32,96},{64,0},{96,32},{1,65},{33,97},{65,1},{97,33},{2,66}... | collective-permute-start | bytes 1769480 | tf_op jit(solution)/shard_map/ppermute | solution.py:431
  35.1 40.3 %collective-permute-start.8 = (f32[72,2048]{1,0:T(8,128)S(1)}, f32[72,2048]{1,0:T(8,128)S(1)}, u32[]{:S(2)}, u32[]{:S(2)}) collective-permute-start(f32[72,2048]{1,0:T(8,128)S(1)} %maximum_maximum_fusion.e0), channel_id=1, source_target_pairs={{0,96},{32,64},{64,32},{96,0},{1,97},{33,65},{65,33},{97,1},{2,98}... | collective-permute-start | bytes 1769480 | tf_op jit(solution)/shard_map/ppermute | solution.py:431
  35.1 29.7 %collective-permute-start.4 = (f32[64,2048]{1,0:T(8,128)}, f32[64,2048]{1,0:T(8,128)}, u32[]{:S(2)}, u32[]{:S(2)}) collective-permute-start(f32[64,2048]{1,0:T(8,128)} %get-tuple-element.22), channel_id=1, source_target_pairs={{0,16},{8,24},{16,0},{24,8},{1,17},{9,25},{17,1},{25,9},{2,18},{10... | collective-permute-start | bytes 1572872 | tf_op jit(solution)/shard_map/ppermute | solution.py:431
  53.2 22.3 %copy-start.5 = (f32[64,2048]{1,0:T(8,128)}, f32[64,2048]{1,0:T(8,128)S(1)}, u32[]{:S(2)}) copy-start(f32[64,2048]{1,0:T(8,128)S(1)} %collective-permute-done.3.p1) | copy-start | bytes 1572868
  53.2 22.2 %collective-permute-start.5 = (f32[64,2048]{1,0:T(8,128)}, f32[64,2048]{1,0:T(8,128)}, u32[]{:S(2)}, u32[]{:S(2)}) collective-permute-start(f32[64,2048]{1,0:T(8,128)} %get-tuple-element.22), channel_id=1, source_target_pairs={{0,24},{8,16},{16,8},{24,0},{1,25},{9,17},{17,9},{25,1},{2,26},{10... | collective-permute-start | bytes 1572872 | tf_op jit(solution)/shard_map/ppermute | solution.py:431
  75.4 1.0 copy-start.3
  75.4 1.2 copy-start.4
  102.7 38.1 %copy-start = (f32[64,8192]{1,0:T(8,128)S(1)}, f32[64,8192]{1,0:T(8,128)}, u32[]{:S(2)}) copy-start(f32[64,8192]{1,0:T(8,128)} %effect.1) | copy-start | bytes 6291460
  102.7 37.5 %all-to-all-start.1 = ((f32[64,32,256]{2,1,0:T(8,128)}), f32[64,32,256]{2,1,0:T(8,128)}, u32[]{:S(2)}, u32[]{:S(2)}) async-start(f32[64,32,256]{2,1,0:T(8,128)} %broadcast_in_dim.35), calls=%async_computation.1 | async-start | bytes 4194304 | tf_op jit(solution)/shard_map/all_to_all | solution.py:469
  110.5 108.8 %all-gather.5.cloned.1.call-start = ((), (), s32[]{:S(2)}) async-start(), calls=%async_computation.4 | async-start | bytes 4227072 | tf_op jit(solution)/shard_map/all_gather | solution.py:468
  140.3 5.3 %collective-permute-start.12 = (f32[2048,256]{1,0:T(8,128)}, f32[2048,256]{1,0:T(8,128)}, u32[]{:S(2)}, u32[]{:S(2)}) collective-permute-start(f32[2048,256]{1,0:T(8,128)} %bitcast.11.mine), channel_id=1, source_target_pairs={{0,1},{1,0},{2,3},{3,2},{4,5},{5,4},{6,7},{7,6},{8,9},{9,8},{10,11... | collective-permute-start | bytes 6291464 | tf_op jit(solution)/shard_map/ppermute | solution.py:431
  142.1 28.8 %collective-permute-start.10 = (f32[64,2048]{1,0:T(8,128)}, f32[64,2048]{1,0:T(8,128)S(1)}, u32[]{:S(2)}, u32[]{:S(2)}) collective-permute-start(f32[64,2048]{1,0:T(8,128)} %get-tuple-element.36), channel_id=1, source_target_pairs={{0,64},{32,96},{64,0},{96,32},{1,65},{33,97},{65,1},{97,33},{2,66}... | collective-permute-start | bytes 1572872 | tf_op jit(solution)/shard_map/ppermute | solution.py:431
  142.7 28.1 %collective-permute-start.11 = (f32[64,2048]{1,0:T(8,128)}, f32[64,2048]{1,0:T(8,128)}, u32[]{:S(2)}, u32[]{:S(2)}) collective-permute-start(f32[64,2048]{1,0:T(8,128)} %get-tuple-element.35), channel_id=1, source_target_pairs={{0,96},{32,64},{64,32},{96,0},{1,97},{33,65},{65,33},{97,1},{2,98}... | collective-permute-start | bytes 1572872 | tf_op jit(solution)/shard_map/ppermute | solution.py:431
  145.0 25.8 %collective-permute-start.9 = (f32[64,2048]{1,0:T(8,128)}, f32[64,2048]{1,0:T(8,128)}, u32[]{:S(2)}, u32[]{:S(2)}) collective-permute-start(f32[64,2048]{1,0:T(8,128)} %get-tuple-element.37), channel_id=1, source_target_pairs={{0,32},{32,0},{64,96},{96,64},{1,33},{33,1},{65,97},{97,65},{2,34}... | collective-permute-start | bytes 1572872 | tf_op jit(solution)/shard_map/ppermute | solution.py:431
  173.9 31.6 %collective-permute-start.15 = (f32[256,512]{1,0:T(8,128)S(1)}, f32[256,512]{1,0:T(8,128)}, u32[]{:S(2)}, u32[]{:S(2)}) collective-permute-start(f32[256,512]{1,0:T(8,128)S(1)} %pad_maximum_fusion.3), channel_id=1, source_target_pairs={{0,24},{8,16},{16,8},{24,0},{1,25},{9,17},{17,9},{25,1},{2,26},{10... | collective-permute-start | bytes 1572872 | tf_op jit(solution)/shard_map/ppermute | solution.py:431
  174.6 30.9 %collective-permute-start.14 = (f32[256,512]{1,0:T(8,128)S(1)}, f32[256,512]{1,0:T(8,128)}, u32[]{:S(2)}, u32[]{:S(2)}) collective-permute-start(f32[256,512]{1,0:T(8,128)S(1)} %pad_maximum_fusion.2), channel_id=1, source_target_pairs={{0,16},{8,24},{16,0},{24,8},{1,17},{9,25},{17,1},{25,9},{2,18},{10... | collective-permute-start | bytes 1572872 | tf_op jit(solution)/shard_map/ppermute | solution.py:431
  177.6 28.4 %collective-permute-start.13 = (f32[256,512]{1,0:T(8,128)}, f32[256,512]{1,0:T(8,128)}, u32[]{:S(2)}, u32[]{:S(2)}) collective-permute-start(f32[256,512]{1,0:T(8,128)} %pad_maximum_fusion.1), channel_id=1, source_target_pairs={{0,8},{8,0},{16,24},{24,16},{1,9},{9,1},{17,25},{25,17},{2,10},{10... | collective-permute-start | bytes 1572872 | tf_op jit(solution)/shard_map/ppermute | solution.py:431
  (1 other events, 0.8 us)
Sparse Core Ops, SparseCore 0:
  9.0 44.2 all-gather.2
  114.5 88.2 all-gather.4

commit v4 on v3

--- a/solution.py
+++ b/solution.py
@@ -125,7 +125,7 @@
 
 
 def gram_kernel(
-    where, p1, p2, p3, e0, e1, e2, e3, noise, observed, var, out, left, right, total
+    where, p1, p2, p3, e0, e1, e2, e3, noise, observed, var, keep, send, left, right, total
 ):
     step = pl.program_id(0)
     zid, yid = where[0], where[1]
@@ -136,15 +136,15 @@
     mean = tails[0:1, :] / member_count
     inv_var = 1.0 / var[...]
     root_var = jnp.sqrt(var[...])
-    for a, p in enumerate((e0, p1, p2, p3)):
+    for a, e in enumerate((e0, e1, e2, e3)):
         at = pl.multiple_of((yid ^ a) * members, members)
-        left[pl.ds(at, members), :] = (p[0:members, :] - mean) * inv_root
+        left[pl.ds(at, members), :] = (e[0:members, :] - mean) * inv_root
         left[pl.ds(at + Y * members, members), :] = (
-            observed[...] + root_var * noise[pl.ds(at, members), :] - p[0:members, :]
+            observed[...] + root_var * noise[pl.ds(at, members), :] - e[0:members, :]
         )
-    for b, e in enumerate((e0, e1, e2, e3)):
+    for b, p in enumerate((e0, p1, p2, p3)):
         at = pl.multiple_of((zid ^ b) * members, members)
-        right[pl.ds(at, members), :] = (e[0:members, :] - mean) * inv_root * inv_var
+        right[pl.ds(at, members), :] = (p[0:members, :] - mean) * inv_root * inv_var
 
     product = mm_last(left[...], right[...])
 
@@ -158,14 +158,17 @@
 
     @pl.when(step == pl.num_programs(0) - 1)
     def _():
-        for c in range(8):
-            out[c, 0:32, 0:TILE] = total[c * 32 : c * 32 + 32, :]
-            out[c, 0:32, TILE : 2 * TILE] = total[TILE + c * 32 : TILE + c * 32 + 32, :]
-            out[c, 32:40, :] = jnp.broadcast_to(tails[1:2, 0:1], (8, 2 * TILE))
+        core, xid = where[2], where[3]
+        for part, offset in ((keep, core * 32), (send, 32 - core * 32)):
+            for a in range(X):
+                at = pl.multiple_of((xid ^ a) * 64 + offset, 32)
+                part[a, 0:32, 0:TILE] = total[pl.ds(at, 32), :]
+                part[a, 0:32, TILE : 2 * TILE] = total[pl.ds(at + TILE, 32), :]
+                part[a, 32:40, :] = jnp.broadcast_to(tails[1:2, 0:1], (8, 2 * TILE))
 
 
 def gram_block(where, rows, columns, noise, observed, var):
-    members, obs = rows[0].shape
+    members, obs = columns[0].shape
     width = 512
 
     def chunk(n):
@@ -176,8 +179,8 @@
         grid=(obs // width,),
         in_specs=[ANY_SMEM] + [chunk(members)] * 3 + [chunk(members + 8)] * 4
         + [chunk(members * Y)] + [chunk(1)] * 2,
-        out_specs=pl.BlockSpec((8, 40, 2 * TILE), lambda i: (0, 0, 0)),
-        out_shape=jax.ShapeDtypeStruct((8, 40, 2 * TILE), f32),
+        out_specs=[pl.BlockSpec((X, 40, 2 * TILE), lambda i: (0, 0, 0))] * 2,
+        out_shape=[jax.ShapeDtypeStruct((X, 40, 2 * TILE), f32)] * 2,
         scratch_shapes=[
             pltpu.VMEM((2 * TILE, width), f32),
             pltpu.VMEM((TILE, width), f32),
@@ -185,7 +188,7 @@
         ],
         cost_estimate=cost(8e9),
         name="gram",
-    )(where, *rows, *columns, noise, observed, var)
+    )(where, *columns, *rows, noise, observed, var)
 
 
 def cost(flops):
@@ -447,7 +450,7 @@
     members, cells = turnover_effect.shape
     obs = obs_taps.shape[0]
     zid, yid, core = lax.axis_index("z"), lax.axis_index("y"), lax.axis_index("core")
-    where = jnp.stack([zid, yid, core]).astype(jnp.int32)
+    where = jnp.stack([zid, yid, core, lax.axis_index("x")]).astype(jnp.int32)
     observed = observed[None, :]
     obs_var = obs_var[None, :]
     noise = lax.all_gather(obs_noise, "y", axis=0, tiled=True)
@@ -455,15 +458,16 @@
         turnover_effect, base_rate[None, :], fast_rate[None, :], slow_rate[None, :],
         init_pools, litterfall, obs_taps.T, obs_weights.T, observed, obs_var,
     )
-    small = small + sum(swap(small, "y", Y, a) for a in range(1, Y))
+    small = small + sum(swap(small, "z", Z, b) for b in range(1, Z))
     small, predicted = lax.optimization_barrier((small, predicted))
-    rows = [swap(predicted, "y", Y, a) for a in range(1, Y)]
+    columns = [swap(predicted, "z", Z, b) for b in range(1, Z)]
     extended = jnp.concatenate(
         [predicted, small[:, :obs], jnp.broadcast_to(small[:, obs : obs + 1], (7, obs))], axis=0
     )
-    columns = [extended] + [swap(extended, "z", Z, b) for b in range(1, Z)]
-    block = gram_block(where, rows, columns, noise, observed, obs_var)
-    shared = jnp.sum(lax.all_to_all(block, ("x", "core"), 0, 0, tiled=False), axis=0)
+    rows = [extended] + [swap(extended, "y", Y, a) for a in range(1, Y)]
+    keep, send = gram_block(where, rows, columns, noise, observed, obs_var)
+    part = keep + swap(send, "core", 2, 1)
+    shared = part[0] + sum(swap(part[a], "x", X, a) for a in range(1, X))
     piece, right, misfit = shared[:32, :TILE], shared[:32, TILE:], shared[32:, :LANES]
     rhs = lax.all_gather(right, ("z", "y", "x", "core"), axis=0, tiled=True)
     mine = lax.all_to_all(

time: 271 us -> 260 us (0.959)
  blocking collectives: 48.2 us -> 31.3 us
  starting transfers between devices: 28.3 us -> 32.8 us
    all_to_all x1 -> x0, blocking collectives: 16.1 us -> none  [body(): lax.all_to_all(block, ('x', 'core'), 0, 0, tiled=False)]
    ppermute x16 -> x20, starting transfers between devices: 20.5 us -> 25.8 us  [swap(): return lax.ppermute(value, axis, [(i, i ^ bit) for i in range(size)])]
    ppermute x16 -> x20, waiting for transfers between devices: 43 us -> 43.4 us  [swap(): return lax.ppermute(value, axis, [(i, i ^ bit) for i in range(size)])]
  transfers between devices with their start and end apart: 19 -> 23, of which waited for: 7 -> 12; matrix products, arithmetic and copies ran while one was open for 4% -> 4% of each run, Pallas kernels for 27% -> 28%
where the time goes in v4:
time: 260 us; the launch traced here: 259 us
  Pallas kernels  90.3 us (35%)
  waiting for transfers between devices  74 us (28%)
  starting transfers between devices  32.8 us (13%)
  blocking collectives  31.3 us (12%)
  between operations  13.6 us (5%)
  local copies, waits for them, and re-layouts  9.45 us (4%)
  other arithmetic  7.85 us (3%)
    ppermute x20, waiting for transfers between devices, swap(): return lax.ppermute(value, axis, [(i, i ^ bit) for i in range(size)])  43.4 us
    all_to_all x1, blocking collectives, body(): lax.all_to_all(change, ('z', 'y'), 0, 1, tiled=True)  31.3 us
    all_to_all x1, waiting for transfers between devices, body(): lax.all_to_all(jnp.broadcast_to(piece[None], (Z * Y * X, 32, TILE)), ('z'...  29.2 us
    ppermute x20, starting transfers between devices, swap(): return lax.ppermute(value, axis, [(i, i ^ bit) for i in range(size)])  25.8 us
    pallas_call x1, Pallas kernels, factor_begin(): pl.pallas_call(begin_kernel, in_specs=[ANY_SMEM, ANY_VMEM, ANY_VMEM, ANY_...  25.3 us
    pallas_call x1, Pallas kernels, factor_finish(): pl.pallas_call(finish_kernel, in_specs=[pl.BlockSpec(memory_space=pl.ANY)...  24.3 us
    pallas_call x1, Pallas kernels, solve(): pl.pallas_call(solve_kernel, in_specs=[ANY_SMEM] + [ANY_VMEM] * 7, out_sp...  13.3 us
    pallas_call x1, Pallas kernels, combine(): pl.pallas_call(combine_kernel, grid=(Z,), in_specs=[pl.BlockSpec((Y * TIL...  10.4 us
  transfers between devices with their start and end apart: 23, of which 12 were waited for; matrix products, arithmetic and copies ran while one was open for 4% of the time, Pallas kernels for 28%

profile of v4, /device:TPU:0, one launch (start us, length us, event | category | flops | bytes accessed | tf_op | source)
XLA Modules:
  0.0 259.4 jit_solution(5202350705021240003)
XLA Ops:
  7.3 9.2 %forward.1 = (f32[64,2048]{1,0:T(8,128)}, f32[1,2176]{1,0:T(1,128)}) custom-call(f32[64,8192]{1,0:T(8,128)} %effect.1, f32[1,8192]{1,0:T(1,128)} %bitcast.30, f32[1,8192]{1,0:T(1,128)} %bitcast.31, f32[1,8192]{1,0:T(1,128)} %bitcast.32, f32[3,8192]{1,0:T(4,128)} %init.1, f32[6,8192]{1,0:T(8,128)} %fall.1, s32[4,2048]{1,0:T(4,128)} %bitcast.33, ...), custom_call_target="tpu_custom_call" | custom-call | tf_op jit(solution)/shard_map/forward/pallas_call | solution.py:109
  16.5 2.1 collective-permute-start
  18.5 3.6 %collective-permute-start.1 = (f32[1,2176]{1,0:T(1,128)}, f32[1,2176]{1,0:T(1,128)S(1)}, u32[]{:S(2)}, u32[]{:S(2)}) collective-permute-start(f32[1,2176]{1,0:T(1,128)} %get-tuple-element.22), channel_id=1, source_target_pairs={{0,64},{32,96},{64,0},{96,32},{1,65},{33,97},{65,1},{97,33},{2,66}... | collective-permute-start | bytes 26120 | tf_op jit(solution)/shard_map/ppermute | solution.py:434
  22.1 1.9 collective-permute-done.1
  24.1 3.1 %collective-permute-done.2 = f32[1,2176]{1,0:T(1,128)S(1)} collective-permute-done((f32[1,2176]{1,0:T(1,128)}, f32[1,2176]{1,0:T(1,128)S(1)}, u32[]{:S(2)}, u32[]{:S(2)}) %collective-permute-start.2) | collective-permute-done | bytes 8736 | tf_op jit(solution)/shard_map/ppermute | solution.py:434
  32.0 2.9 %collective-permute-start.7 = (f32[72,2048]{1,0:T(8,128)S(1)}, f32[72,2048]{1,0:T(8,128)S(1)}, u32[]{:S(2)}, u32[]{:S(2)}) collective-permute-start(f32[72,2048]{1,0:T(8,128)S(1)} %maximum_maximum_fusion.e0), channel_id=1, source_target_pairs={{0,16},{8,24},{16,0},{24,8},{1,17},{9,25},{17,1},{25,9},{2,18},{10... | collective-permute-start | bytes 1769480 | tf_op jit(solution)/shard_map/ppermute | solution.py:434
  36.6 6.9 %collective-permute-done.3.p1 = f32[64,2048]{1,0:T(8,128)S(1)} collective-permute-done((f32[64,2048]{1,0:T(8,128)}, f32[64,2048]{1,0:T(8,128)S(1)}, u32[]{:S(2)}, u32[]{:S(2)}) %collective-permute-start.3) | collective-permute-done | bytes 524320 | tf_op jit(solution)/shard_map/ppermute | solution.py:434
  44.3 7.5 %collective-permute-done.4.p2 = f32[64,2048]{1,0:T(8,128)} collective-permute-done((f32[64,2048]{1,0:T(8,128)}, f32[64,2048]{1,0:T(8,128)}, u32[]{:S(2)}, u32[]{:S(2)}) %collective-permute-start.4) | collective-permute-done | bytes 524320 | tf_op jit(solution)/shard_map/ppermute | solution.py:434
  51.8 10.6 %collective-permute-done.5.p3 = f32[64,2048]{1,0:T(8,128)} collective-permute-done((f32[64,2048]{1,0:T(8,128)}, f32[64,2048]{1,0:T(8,128)}, u32[]{:S(2)}, u32[]{:S(2)}) %collective-permute-start.5) | collective-permute-done | bytes 524320 | tf_op jit(solution)/shard_map/ppermute | solution.py:434
  62.4 5.1 %collective-permute-done.7.e2 = f32[72,2048]{1,0:T(8,128)S(1)} collective-permute-done((f32[72,2048]{1,0:T(8,128)S(1)}, f32[72,2048]{1,0:T(8,128)S(1)}, u32[]{:S(2)}, u32[]{:S(2)}) %collective-permute-start.7) | collective-permute-done | bytes 589856 | tf_op jit(solution)/shard_map/ppermute | solution.py:434
  68.5 7.8 %gram.1 = (f32[4,40,512]{2,1,0:T(8,128)}, f32[4,40,512]{2,1,0:T(8,128)}) custom-call(s32[4]{0:T(128)} %pad_add_fusion.where, f32[64,2048]{1,0:T(8,128)} %copy-done.5, f32[64,2048]{1,0:T(8,128)} %collective-permute-done.4.p2, f32[64,2048]{1,0:T(8,128)} %collective-permute-done.5.p3, f32[72,2048]{1,0:T(8,128)} %copy-done.1, f32[72,2048]{1,0:T(8,128)} %copy-done.2, ...), custom_call_target="tpu_custom_call" | custom-call | flops 8000000000 | bytes 10000000 | tf_op jit(solution)/shard_map/gram/pallas_call | solution.py:177
  80.8 2.7 %collective-permute-start.11 = (f32[40,512]{1,0:T(8,128)S(1)}, f32[40,512]{1,0:T(8,128)S(1)}, u32[]{:S(2)}, u32[]{:S(2)}) collective-permute-start(f32[40,512]{1,0:T(8,128)S(1)} %get-tuple-element.59), channel_id=1, source_target_pairs={{0,4},{2,6},{4,0},{6,2},{1,5},{3,7},{5,1},{7,3},{8,12},{10,14},{12... | collective-permute-start | bytes 245768 | tf_op jit(solution)/shard_map/ppermute | solution.py:434
  84.1 3.8 %collective-permute-done.11 = f32[40,512]{1,0:T(8,128)S(1)} collective-permute-done((f32[40,512]{1,0:T(8,128)S(1)}, f32[40,512]{1,0:T(8,128)S(1)}, u32[]{:S(2)}, u32[]{:S(2)}) %collective-permute-start.11) | collective-permute-done | bytes 81952 | tf_op jit(solution)/shard_map/ppermute | solution.py:434
  91.7 7.0 %all-to-all-start = ((f32[64,32,256]{2,1,0:T(8,128)}), f32[64,32,256]{2,1,0:T(8,128)}, u32[]{:S(2)}, u32[]{:S(2)}) async-start(f32[64,32,256]{2,1,0:T(8,128)} %broadcast_in_dim.35), calls=%async_computation | async-start | bytes 4194304 | tf_op jit(solution)/shard_map/all_to_all | solution.py:473
  99.5 29.2 %all-to-all-done = f32[64,32,256]{2,1,0:T(8,128)} async-done(((f32[64,32,256]{2,1,0:T(8,128)}), f32[64,32,256]{2,1,0:T(8,128)}, u32[]{:S(2)}, u32[]{:S(2)}) %all-to-all-start) | async-done | bytes 2097184 | tf_op jit(solution)/shard_map/all_to_all | solution.py:473
  130.8 1.9 collective-permute-start.14
  132.7 2.5 collective-permute-start.15
  135.2 25.3 %factor_begin.1 = (f32[1024,1024]{1,0:T(8,128)}, f32[512,256]{1,0:T(8,128)}) custom-call(s32[4]{0:T(128)} %pad_add_fusion.where, f32[2048,256]{1,0:T(8,128)} %bitcast.16.mine, f32[2048,256]{1,0:T(8,128)} %collective-permute-done.16.other, f32[8,128]{1,0:T(8,128)} %slice.42.misfit), custom_call_target="tpu_custom_call" | custom-call | flops 20000000000 | bytes 10000000 | tf_op jit(solution)/shard_map/factor_begin/pallas_call | solution.py:351
  161.7 1.9 constant_dynamic-slice_fusion
  164.6 1.9 collective-permute-start.18
  168.7 24.3 %factor_finish.1 = (f32[1024,1024]{1,0:T(8,128)}, f32[512,256]{1,0:T(8,128)}) custom-call(f32[1024,1024]{1,0:T(8,128)} %get-tuple-element.31.before, f32[512,256]{1,0:T(8,128)} %get-tuple-element.32.earlier), custom_call_target="tpu_custom_call" | custom-call | flops 20000000000 | bytes 10000000 | tf_op jit(solution)/shard_map/factor_finish/pallas_call | solution.py:364
  195.7 13.3 %solve.1.work = f32[1024,512]{1,0:T(8,128)} custom-call(s32[4]{0:T(128)} %pad_add_fusion.where, f32[1024,1024]{1,0:T(8,128)} %get-tuple-element.33.system, f32[512,256]{1,0:T(8,128)} %get-tuple-element.32.earlier, f32[512,256]{1,0:T(8,128)} %get-tuple-element.34.later, f32[256,512]{1,0:T(8,128)} %pad_maximum_fusion.b0, ...), custom_call_target="tpu_custom_call" | custom-call | flops 5000000000 | bytes 10000000 | tf_op jit(solution)/shard_map/solve/pallas_call | solution.py:400
  209.0 10.4 %combine.1 = f32[1024,512]{1,0:T(8,128)} custom-call(f32[4096,256]{1,0:T(8,128)} %all-gather.5.cloned.1.call-done.rhs, f32[1024,512]{1,0:T(8,128)} %solve.1.work, f32[8,128]{1,0:T(8,128)} %slice.42.misfit), custom_call_target="tpu_custom_call" | custom-call | flops 6000000000 | bytes 10000000 | tf_op jit(solution)/shard_map/combine/pallas_call | solution.py:420
  219.4 31.3 %all_to_all.24 = f32[16,64,512]{2,1,0:T(8,128)S(1)} all-to-all(f32[16,64,512]{2,1,0:T(8,128)} %bitcast.29), channel_id=1, replica_groups=mesh['z'=4,'y'=4,'x'=4,'core'=2] {'z','y'}, dimensions={0} | all-to-all | bytes 4194304 | tf_op jit(solution)/shard_map/all_to_all | solution.py:494
  (65 shorter events, 29.6 us)
Async XLA Ops:
  6.5 61.0 %all-gather.3.cloned.1.call-start = ((), (), s32[]{:S(2)}) async-start(), calls=%async_computation.2 | async-start | bytes 2621440 | tf_op jit(solution)/shard_map/all_gather | solution.py:456
  16.5 5.7 %collective-permute-start = (f32[1,2176]{1,0:T(1,128)}, f32[1,2176]{1,0:T(1,128)S(1)}, u32[]{:S(2)}, u32[]{:S(2)}) collective-permute-start(f32[1,2176]{1,0:T(1,128)} %get-tuple-element.22), channel_id=1, source_target_pairs={{0,32},{32,0},{64,96},{96,64},{1,33},{33,1},{65,97},{97,65},{2,34}... | collective-permute-start | bytes 26120 | tf_op jit(solution)/shard_map/ppermute | solution.py:434
  18.5 5.5 %collective-permute-start.1 = (f32[1,2176]{1,0:T(1,128)}, f32[1,2176]{1,0:T(1,128)S(1)}, u32[]{:S(2)}, u32[]{:S(2)}) collective-permute-start(f32[1,2176]{1,0:T(1,128)} %get-tuple-element.22), channel_id=1, source_target_pairs={{0,64},{32,96},{64,0},{96,32},{1,65},{33,97},{65,1},{97,33},{2,66}... | collective-permute-start | bytes 26120 | tf_op jit(solution)/shard_map/ppermute | solution.py:434
  22.1 5.1 %collective-permute-start.2 = (f32[1,2176]{1,0:T(1,128)}, f32[1,2176]{1,0:T(1,128)S(1)}, u32[]{:S(2)}, u32[]{:S(2)}) collective-permute-start(f32[1,2176]{1,0:T(1,128)} %get-tuple-element.22), channel_id=1, source_target_pairs={{0,96},{32,64},{64,32},{96,0},{1,97},{33,65},{65,33},{97,1},{2,98}... | collective-permute-start | bytes 26120 | tf_op jit(solution)/shard_map/ppermute | solution.py:434
  28.5 15.1 %collective-permute-start.3 = (f32[64,2048]{1,0:T(8,128)}, f32[64,2048]{1,0:T(8,128)S(1)}, u32[]{:S(2)}, u32[]{:S(2)}) collective-permute-start(f32[64,2048]{1,0:T(8,128)} %get-tuple-element.24), channel_id=1, source_target_pairs={{0,32},{32,0},{64,96},{96,64},{1,33},{33,1},{65,97},{97,65},{2,34}... | collective-permute-start | bytes 1572872 | tf_op jit(solution)/shard_map/ppermute | solution.py:434
  30.4 32.1 %collective-permute-start.6 = (f32[72,2048]{1,0:T(8,128)S(1)}, f32[72,2048]{1,0:T(8,128)S(1)}, u32[]{:S(2)}, u32[]{:S(2)}) collective-permute-start(f32[72,2048]{1,0:T(8,128)S(1)} %maximum_maximum_fusion.e0), channel_id=1, source_target_pairs={{0,8},{8,0},{16,24},{24,16},{1,9},{9,1},{17,25},{25,17},{2,10},{10... | collective-permute-start | bytes 1769480 | tf_op jit(solution)/shard_map/ppermute | solution.py:434
  32.0 35.5 %collective-permute-start.7 = (f32[72,2048]{1,0:T(8,128)S(1)}, f32[72,2048]{1,0:T(8,128)S(1)}, u32[]{:S(2)}, u32[]{:S(2)}) collective-permute-start(f32[72,2048]{1,0:T(8,128)S(1)} %maximum_maximum_fusion.e0), channel_id=1, source_target_pairs={{0,16},{8,24},{16,0},{24,8},{1,17},{9,25},{17,1},{25,9},{2,18},{10... | collective-permute-start | bytes 1769480 | tf_op jit(solution)/shard_map/ppermute | solution.py:434
  34.9 32.6 %collective-permute-start.8 = (f32[72,2048]{1,0:T(8,128)S(1)}, f32[72,2048]{1,0:T(8,128)S(1)}, u32[]{:S(2)}, u32[]{:S(2)}) collective-permute-start(f32[72,2048]{1,0:T(8,128)S(1)} %maximum_maximum_fusion.e0), channel_id=1, source_target_pairs={{0,24},{8,16},{16,8},{24,0},{1,25},{9,17},{17,9},{25,1},{2,26},{10... | collective-permute-start | bytes 1769480 | tf_op jit(solution)/shard_map/ppermute | solution.py:434
  35.1 16.7 %collective-permute-start.4 = (f32[64,2048]{1,0:T(8,128)}, f32[64,2048]{1,0:T(8,128)}, u32[]{:S(2)}, u32[]{:S(2)}) collective-permute-start(f32[64,2048]{1,0:T(8,128)} %get-tuple-element.24), channel_id=1, source_target_pairs={{0,64},{32,96},{64,0},{96,32},{1,65},{33,97},{65,1},{97,33},{2,66}... | collective-permute-start | bytes 1572872 | tf_op jit(solution)/shard_map/ppermute | solution.py:434
  43.5 18.9 %collective-permute-start.5 = (f32[64,2048]{1,0:T(8,128)}, f32[64,2048]{1,0:T(8,128)}, u32[]{:S(2)}, u32[]{:S(2)}) collective-permute-start(f32[64,2048]{1,0:T(8,128)} %get-tuple-element.24), channel_id=1, source_target_pairs={{0,96},{32,64},{64,32},{96,0},{1,97},{33,65},{65,33},{97,1},{2,98}... | collective-permute-start | bytes 1572872 | tf_op jit(solution)/shard_map/ppermute | solution.py:434
  76.3 1.9 collective-permute-start.9
  79.3 4.8 %collective-permute-start.10 = (f32[40,512]{1,0:T(8,128)S(1)}, f32[40,512]{1,0:T(8,128)S(1)}, u32[]{:S(2)}, u32[]{:S(2)}) collective-permute-start(f32[40,512]{1,0:T(8,128)S(1)} %get-tuple-element.61), channel_id=1, source_target_pairs={{0,2},{2,0},{4,6},{6,4},{1,3},{3,1},{5,7},{7,5},{8,10},{10,8},{12,... | collective-permute-start | bytes 245768 | tf_op jit(solution)/shard_map/ppermute | solution.py:434
  80.8 7.0 %collective-permute-start.11 = (f32[40,512]{1,0:T(8,128)S(1)}, f32[40,512]{1,0:T(8,128)S(1)}, u32[]{:S(2)}, u32[]{:S(2)}) collective-permute-start(f32[40,512]{1,0:T(8,128)S(1)} %get-tuple-element.59), channel_id=1, source_target_pairs={{0,4},{2,6},{4,0},{6,2},{1,5},{3,7},{5,1},{7,3},{8,12},{10,14},{12... | collective-permute-start | bytes 245768 | tf_op jit(solution)/shard_map/ppermute | solution.py:434
  83.5 6.0 %collective-permute-start.12 = (f32[40,512]{1,0:T(8,128)S(1)}, f32[40,512]{1,0:T(8,128)S(1)}, u32[]{:S(2)}, u32[]{:S(2)}) collective-permute-start(f32[40,512]{1,0:T(8,128)S(1)} %get-tuple-element.60), channel_id=1, source_target_pairs={{0,6},{2,4},{4,2},{6,0},{1,7},{3,5},{5,3},{7,1},{8,14},{10,12},{12... | collective-permute-start | bytes 245768 | tf_op jit(solution)/shard_map/ppermute | solution.py:434
  91.7 37.6 %copy-start = (f32[64,8192]{1,0:T(8,128)S(1)}, f32[64,8192]{1,0:T(8,128)}, u32[]{:S(2)}) copy-start(f32[64,8192]{1,0:T(8,128)} %effect.1) | copy-start | bytes 6291460
  91.7 37.0 %all-to-all-start = ((f32[64,32,256]{2,1,0:T(8,128)}), f32[64,32,256]{2,1,0:T(8,128)}, u32[]{:S(2)}, u32[]{:S(2)}) async-start(f32[64,32,256]{2,1,0:T(8,128)} %broadcast_in_dim.35), calls=%async_computation | async-start | bytes 4194304 | tf_op jit(solution)/shard_map/all_to_all | solution.py:473
  98.7 110.3 %all-gather.5.cloned.1.call-start = ((), (), s32[]{:S(2)}) async-start(), calls=%async_computation.3 | async-start | bytes 4227072 | tf_op jit(solution)/shard_map/all_gather | solution.py:472
  128.7 6.5 %collective-permute-start.16 = (f32[2048,256]{1,0:T(8,128)}, f32[2048,256]{1,0:T(8,128)}, u32[]{:S(2)}, u32[]{:S(2)}) collective-permute-start(f32[2048,256]{1,0:T(8,128)} %bitcast.16.mine), channel_id=1, source_target_pairs={{0,1},{1,0},{2,3},{3,2},{4,5},{5,4},{6,7},{7,6},{8,9},{9,8},{10,11... | collective-permute-start | bytes 6291464 | tf_op jit(solution)/shard_map/ppermute | solution.py:434
  130.5 30.0 %collective-permute-start.13 = (f32[64,2048]{1,0:T(8,128)}, f32[64,2048]{1,0:T(8,128)}, u32[]{:S(2)}, u32[]{:S(2)}) collective-permute-start(f32[64,2048]{1,0:T(8,128)} %get-tuple-element.41), channel_id=1, source_target_pairs={{0,32},{32,0},{64,96},{96,64},{1,33},{33,1},{65,97},{97,65},{2,34}... | collective-permute-start | bytes 1572872 | tf_op jit(solution)/shard_map/ppermute | solution.py:434
  130.8 29.7 %collective-permute-start.14 = (f32[64,2048]{1,0:T(8,128)}, f32[64,2048]{1,0:T(8,128)S(1)}, u32[]{:S(2)}, u32[]{:S(2)}) collective-permute-start(f32[64,2048]{1,0:T(8,128)} %get-tuple-element.40), channel_id=1, source_target_pairs={{0,64},{32,96},{64,0},{96,32},{1,65},{33,97},{65,1},{97,33},{2,66}... | collective-permute-start | bytes 1572872 | tf_op jit(solution)/shard_map/ppermute | solution.py:434
  132.7 27.8 %collective-permute-start.15 = (f32[64,2048]{1,0:T(8,128)}, f32[64,2048]{1,0:T(8,128)}, u32[]{:S(2)}, u32[]{:S(2)}) collective-permute-start(f32[64,2048]{1,0:T(8,128)} %get-tuple-element.39), channel_id=1, source_target_pairs={{0,96},{32,64},{64,32},{96,0},{1,97},{33,65},{65,33},{97,1},{2,98}... | collective-permute-start | bytes 1572872 | tf_op jit(solution)/shard_map/ppermute | solution.py:434
  163.6 31.4 %collective-permute-start.19 = (f32[256,512]{1,0:T(8,128)S(1)}, f32[256,512]{1,0:T(8,128)}, u32[]{:S(2)}, u32[]{:S(2)}) collective-permute-start(f32[256,512]{1,0:T(8,128)S(1)} %pad_maximum_fusion.3), channel_id=1, source_target_pairs={{0,24},{8,16},{16,8},{24,0},{1,25},{9,17},{17,9},{25,1},{2,26},{10... | collective-permute-start | bytes 1572872 | tf_op jit(solution)/shard_map/ppermute | solution.py:434
  164.6 30.4 %collective-permute-start.18 = (f32[256,512]{1,0:T(8,128)S(1)}, f32[256,512]{1,0:T(8,128)}, u32[]{:S(2)}, u32[]{:S(2)}) collective-permute-start(f32[256,512]{1,0:T(8,128)S(1)} %pad_maximum_fusion.2), channel_id=1, source_target_pairs={{0,16},{8,24},{16,0},{24,8},{1,17},{9,25},{17,1},{25,9},{2,18},{10... | collective-permute-start | bytes 1572872 | tf_op jit(solution)/shard_map/ppermute | solution.py:434
  167.3 28.4 %collective-permute-start.17 = (f32[256,512]{1,0:T(8,128)}, f32[256,512]{1,0:T(8,128)}, u32[]{:S(2)}, u32[]{:S(2)}) collective-permute-start(f32[256,512]{1,0:T(8,128)} %pad_maximum_fusion.1), channel_id=1, source_target_pairs={{0,8},{8,0},{16,24},{24,16},{1,9},{9,1},{17,25},{25,17},{2,10},{10... | collective-permute-start | bytes 1572872 | tf_op jit(solution)/shard_map/ppermute | solution.py:434
  (5 other events, 68.3 us)
Sparse Core Ops, SparseCore 0:
  9.0 41.5 all-gather.2
  102.7 89.8 all-gather.4

commit v5 on v4

--- a/solution.py
+++ b/solution.py
@@ -120,31 +120,38 @@
             jax.ShapeDtypeStruct((1, obs + LANES), f32),
         ],
         scratch_shapes=[pltpu.VMEM((members, CHUNK), f32), pltpu.VMEM((8, CHUNK), f32)],
+        cost_estimate=cost(2e10),
         name="forward",
     )(effect, base, fast, slow, init, fall, taps, weights, observed, var)
 
 
 def gram_kernel(
-    where, p1, p2, p3, e0, e1, e2, e3, noise, observed, var, keep, send, left, right, total
+    where, e0, e1, e2, e3, e4, p1, p2, p3, p4, n0, n1, n2, n3, n4, observed, var,
+    keep, send, left, right, total,
 ):
     step = pl.program_id(0)
     zid, yid = where[0], where[1]
     members = p1.shape[0]
+    half = members // 2
     member_count = members * Z * Y
     inv_root = 1.0 / math.sqrt(member_count - 1)
-    tails = e0[members:, :] + e1[members:, :] + e2[members:, :] + e3[members:, :]
+    tails = e0[members:, :] + e1[members:, :] + e2[members:, :] + e4[half:, :]
     mean = tails[0:1, :] / member_count
     inv_var = 1.0 / var[...]
     root_var = jnp.sqrt(var[...])
-    for a, e in enumerate((e0, e1, e2, e3)):
-        at = pl.multiple_of((yid ^ a) * members, members)
-        left[pl.ds(at, members), :] = (e[0:members, :] - mean) * inv_root
-        left[pl.ds(at + Y * members, members), :] = (
-            observed[...] + root_var * noise[pl.ds(at, members), :] - e[0:members, :]
-        )
-    for b, p in enumerate((e0, p1, p2, p3)):
-        at = pl.multiple_of((zid ^ b) * members, members)
-        right[pl.ds(at, members), :] = (p[0:members, :] - mean) * inv_root * inv_var
+
+    def pieces(own, back, forth, low, high):
+        return ((0, 0, own), (3, 0, back), (1, 0, forth), (2, 0, low), (2, half, high))
+
+    for (turn, skip, e), (_, _, n) in zip(pieces(e0, e1, e2, e3, e4), pieces(n0, n1, n2, n3, n4)):
+        count = n.shape[0]
+        at = pl.multiple_of(((yid + turn) & 3) * members + skip, half)
+        left[pl.ds(at, count), :] = (e[0:count, :] - mean) * inv_root
+        left[pl.ds(at + Y * members, count), :] = observed[...] + root_var * n[...] - e[0:count, :]
+    for turn, skip, p in pieces(e0, p1, p2, p3, p4):
+        count = half if turn == 2 else members
+        at = pl.multiple_of(((zid + turn) & 3) * members + skip, half)
+        right[pl.ds(at, count), :] = (p[0:count, :] - mean) * inv_root * inv_var
 
     product = mm_last(left[...], right[...])
 
@@ -169,6 +176,7 @@
 
 def gram_block(where, rows, columns, noise, observed, var):
     members, obs = columns[0].shape
+    half = members // 2
     width = 512
 
     def chunk(n):
@@ -177,8 +185,9 @@
     return pl.pallas_call(
         gram_kernel,
         grid=(obs // width,),
-        in_specs=[ANY_SMEM] + [chunk(members)] * 3 + [chunk(members + 8)] * 4
-        + [chunk(members * Y)] + [chunk(1)] * 2,
+        in_specs=[ANY_SMEM] + [chunk(members + 8)] * 3 + [chunk(half), chunk(half + 8)]
+        + [chunk(members)] * 2 + [chunk(half)] * 2 + [chunk(members)] * 3 + [chunk(half)] * 2
+        + [chunk(1)] * 2,
         out_specs=[pl.BlockSpec((X, 40, 2 * TILE), lambda i: (0, 0, 0))] * 2,
         out_shape=[jax.ShapeDtypeStruct((X, 40, 2 * TILE), f32)] * 2,
         scratch_shapes=[
@@ -188,7 +197,7 @@
         ],
         cost_estimate=cost(8e9),
         name="gram",
-    )(where, *columns, *rows, noise, observed, var)
+    )(where, *rows, *columns, *noise, observed, var)
 
 
 def cost(flops):
@@ -387,9 +396,13 @@
         at = slice(k * TILE, (k + 1) * TILE)
         source = earlier if k < 2 else later
         work[at, :] = mm(source[(k % 2) * TILE : (k % 2 + 1) * TILE, :], work[at, :])
-        for i in range(k + 1, tiles):
-            down = slice(i * TILE, (i + 1) * TILE)
-            work[down, :] = work[down, :] - mm(system[down, at], work[at, :])
+
+        def down(i, _, at=at):
+            low = pl.ds(pl.multiple_of(i * TILE, TILE), TILE)
+            work[low, :] = work[low, :] - mm(system[low, at], work[at, :])
+            return 0
+
+        lax.fori_loop(k + 1, tiles, down, 0)
     for k in range(tiles - 2, -1, -1):
         at = slice(k * TILE, (k + 1) * TILE)
         rest = slice((k + 1) * TILE, n)
@@ -428,6 +441,19 @@
         cost_estimate=cost(6e9),
         name="combine",
     )(rhs, work, misfit)
+
+
+def neighbours(value, axis):
+    back = lax.ppermute(value, axis, [(i, (i + 1) % 4) for i in range(4)])
+    forth = lax.ppermute(value, axis, [(i, (i + 3) % 4) for i in range(4)])
+    return back, forth
+
+
+def opposite(back, forth, axis):
+    half = 32
+    low = lax.ppermute(back[:half], axis, [(i, (i + 1) % 4) for i in range(4)])
+    high = lax.ppermute(forth[half:], axis, [(i, (i + 3) % 4) for i in range(4)])
+    return low, high
 
 
 def swap(value, axis, size, bit):
@@ -453,18 +479,22 @@
     where = jnp.stack([zid, yid, core, lax.axis_index("x")]).astype(jnp.int32)
     observed = observed[None, :]
     obs_var = obs_var[None, :]
-    noise = lax.all_gather(obs_noise, "y", axis=0, tiled=True)
+    noise = neighbours(obs_noise, "y")
     predicted, small = forward(
         turnover_effect, base_rate[None, :], fast_rate[None, :], slow_rate[None, :],
         init_pools, litterfall, obs_taps.T, obs_weights.T, observed, obs_var,
     )
+    small, noise = lax.optimization_barrier((small, noise))
+    noise = (obs_noise,) + noise + opposite(*noise, "y")
     small = small + sum(swap(small, "z", Z, b) for b in range(1, Z))
-    small, predicted = lax.optimization_barrier((small, predicted))
-    columns = [swap(predicted, "z", Z, b) for b in range(1, Z)]
+    small, predicted, noise = lax.optimization_barrier((small, predicted, noise))
     extended = jnp.concatenate(
         [predicted, small[:, :obs], jnp.broadcast_to(small[:, obs : obs + 1], (7, obs))], axis=0
     )
-    rows = [extended] + [swap(extended, "y", Y, a) for a in range(1, Y)]
+    rows = neighbours(extended, "y")
+    columns = neighbours(predicted, "z")
+    rows = (extended,) + rows + opposite(*rows, "y")
+    columns = columns + opposite(*columns, "z")
     keep, send = gram_block(where, rows, columns, noise, observed, obs_var)
     part = keep + swap(send, "core", 2, 1)
     shared = part[0] + sum(swap(part[a], "x", X, a) for a in range(1, X))

time: 260 us -> 259 us (level)
  waiting for transfers between devices: 74 us -> 58.4 us
  starting transfers between devices: 32.8 us -> 44.5 us
    ppermute x20 -> x14, waiting for transfers between devices: 43.4 us -> 9.92 us  [swap(): return lax.ppermute(value, axis, [(i, i ^ bit) for i in range(size)])]
    ppermute x0 -> x12, starting transfers between devices: none -> 19.4 us  [the longest x3 8.08 us: opposite(): lax.ppermute(forth[half:], axis, [(i, (i + 3) % 4) for i in range(4)])]
    ppermute x0 -> x12, waiting for transfers between devices: none -> 18.6 us  [the longest x3 8.45 us: opposite(): low = lax.ppermute(back[:half], axis, [(i, (i + 1) % 4) for i in range(4)])]
    ppermute x20 -> x14, starting transfers between devices: 25.8 us -> 19.4 us  [swap(): return lax.ppermute(value, axis, [(i, i ^ bit) for i in range(size)])]
  transfers between devices with their start and end apart: 23 -> 28, of which waited for: 12 -> 14; matrix products, arithmetic and copies ran while one was open for 4% -> 3% of each run, Pallas kernels for 28% -> 28%
where the time goes in v5:
time: 259 us; the launch traced here: 258 us
  Pallas kernels  92.2 us (36%)
  waiting for transfers between devices  58.4 us (23%)
  starting transfers between devices  44.5 us (17%)
  blocking collectives  31.4 us (12%)
  between operations  13.6 us (5%)
  local copies, waits for them, and re-layouts  10 us (4%)
  other arithmetic  7.73 us (3%)
    all_to_all x1, blocking collectives, body(): lax.all_to_all(change, ('z', 'y'), 0, 1, tiled=True)  31.4 us
    all_to_all x1, waiting for transfers between devices, body(): lax.all_to_all(jnp.broadcast_to(piece[None], (Z * Y * X, 32, TILE)), ('z'...  29.2 us
    pallas_call x1, Pallas kernels, factor_begin(): pl.pallas_call(begin_kernel, in_specs=[ANY_SMEM, ANY_VMEM, ANY_VMEM, ANY_...  25.2 us
    pallas_call x1, Pallas kernels, factor_finish(): pl.pallas_call(finish_kernel, in_specs=[pl.BlockSpec(memory_space=pl.ANY)...  24.3 us
    ppermute x14, starting transfers between devices, swap(): return lax.ppermute(value, axis, [(i, i ^ bit) for i in range(size)])  19.4 us
    pallas_call x1, Pallas kernels, solve(): pl.pallas_call(solve_kernel, in_specs=[ANY_SMEM] + [ANY_VMEM] * 7, out_sp...  14.3 us
    pallas_call x1, Pallas kernels, combine(): pl.pallas_call(combine_kernel, grid=(Z,), in_specs=[pl.BlockSpec((Y * TIL...  10.4 us
    ppermute x14, waiting for transfers between devices, swap(): return lax.ppermute(value, axis, [(i, i ^ bit) for i in range(size)])  9.92 us
  transfers between devices with their start and end apart: 28, of which 14 were waited for; matrix products, arithmetic and copies ran while one was open for 3% of the time, Pallas kernels for 28%

profile of v5, /device:TPU:0, one launch (start us, length us, event | category | flops | bytes accessed | tf_op | source)
XLA Modules:
  0.0 257.8 jit_solution(10422798343978197459)
XLA Ops:
  9.8 9.2 %forward.1 = (f32[64,2048]{1,0:T(8,128)}, f32[1,2176]{1,0:T(1,128)}) custom-call(f32[64,8192]{1,0:T(8,128)} %effect.1, f32[1,8192]{1,0:T(1,128)} %bitcast.30, f32[1,8192]{1,0:T(1,128)} %bitcast.31, f32[1,8192]{1,0:T(1,128)} %bitcast.32, f32[3,8192]{1,0:T(4,128)} %init.1, f32[6,8192]{1,0:T(8,128)} %fall.1, s32[4,2048]{1,0:T(4,128)} %bitcast.33, ...), custom_call_target="tpu_custom_call" | custom-call | flops 20000000000 | bytes 10000000 | tf_op jit(solution)/shard_map/forward/pallas_call | solution.py:109
  19.0 2.8 %collective-permute-done.n1 = f32[64,2048]{1,0:T(8,128)S(1)} collective-permute-done((f32[64,2048]{1,0:T(8,128)}, f32[64,2048]{1,0:T(8,128)S(1)}, u32[]{:S(2)}, u32[]{:S(2)}) %collective-permute-start) | collective-permute-done | bytes 524320 | tf_op jit(solution)/shard_map/ppermute | solution.py:447
  21.8 2.0 collective-permute-start.2
  23.8 3.6 %collective-permute-start.3 = (f32[1,2176]{1,0:T(1,128)}, f32[1,2176]{1,0:T(1,128)S(1)}, u32[]{:S(2)}, u32[]{:S(2)}) collective-permute-start(f32[1,2176]{1,0:T(1,128)} %get-tuple-element.31), channel_id=1, source_target_pairs={{0,64},{32,96},{64,0},{96,32},{1,65},{33,97},{65,1},{97,33},{2,66}... | collective-permute-start | bytes 26120 | tf_op jit(solution)/shard_map/ppermute | solution.py:460
  33.1 2.2 collective-permute-done.5.n3
  37.9 3.0 %collective-permute-start.8 = (f32[72,2048]{1,0:T(8,128)S(1)}, f32[72,2048]{1,0:T(8,128)S(1)}, u32[]{:S(2)}, u32[]{:S(2)}) collective-permute-start(f32[72,2048]{1,0:T(8,128)S(1)} %maximum_maximum_fusion.e0), channel_id=1, source_target_pairs={{0,24},{8,0},{16,8},{24,16},{1,25},{9,1},{17,9},{25,17},{2,26},{10... | collective-permute-start | bytes 1769480 | tf_op jit(solution)/shard_map/ppermute | solution.py:448
  40.9 3.3 %collective-permute-start.12 = (f32[64,2048]{1,0:T(8,128)S(1)}, f32[64,2048]{1,0:T(8,128)S(1)}, u32[]{:S(2)}, u32[]{:S(2)}) collective-permute-start(f32[64,2048]{1,0:T(8,128)S(1)} %copy-done.2), channel_id=1, source_target_pairs={{0,96},{32,0},{64,32},{96,64},{1,97},{33,1},{65,33},{97,65},{2,98}... | collective-permute-start | bytes 1572872 | tf_op jit(solution)/shard_map/ppermute | solution.py:448
  44.2 7.2 %collective-permute-done.8.e2 = f32[72,2048]{1,0:T(8,128)S(1)} collective-permute-done((f32[72,2048]{1,0:T(8,128)S(1)}, f32[72,2048]{1,0:T(8,128)S(1)}, u32[]{:S(2)}, u32[]{:S(2)}) %collective-permute-start.8) | collective-permute-done | bytes 589856 | tf_op jit(solution)/shard_map/ppermute | solution.py:448
  51.4 3.1 %collective-permute-start.10 = (f32[40,2048]{1,0:T(8,128)S(1)}, f32[40,2048]{1,0:T(8,128)}, u32[]{:S(2)}, u32[]{:S(2)}) collective-permute-start(f32[40,2048]{1,0:T(8,128)S(1)} %slice.61), channel_id=1, source_target_pairs={{0,24},{8,0},{16,8},{24,16},{1,25},{9,1},{17,9},{25,17},{2,26},{10... | collective-permute-start | bytes 983048 | tf_op jit(solution)/shard_map/ppermute | solution.py:455
  55.3 3.2 %collective-permute-start.14 = (f32[32,2048]{1,0:T(8,128)S(1)}, f32[32,2048]{1,0:T(8,128)}, u32[]{:S(2)}, u32[]{:S(2)}) collective-permute-start(f32[32,2048]{1,0:T(8,128)S(1)} %slice.63), channel_id=1, source_target_pairs={{0,96},{32,0},{64,32},{96,64},{1,97},{33,1},{65,33},{97,65},{2,98}... | collective-permute-start | bytes 786440 | tf_op jit(solution)/shard_map/ppermute | solution.py:455
  59.9 2.3 collective-permute-done.13.p3
  62.4 3.9 %collective-permute-done.9.e3 = f32[32,2048]{1,0:T(8,128)} collective-permute-done((f32[32,2048]{1,0:T(8,128)S(1)}, f32[32,2048]{1,0:T(8,128)}, u32[]{:S(2)}, u32[]{:S(2)}) %collective-permute-start.9) | collective-permute-done | bytes 262176 | tf_op jit(solution)/shard_map/ppermute | solution.py:454
  66.3 8.7 %gram.1 = (f32[4,40,512]{2,1,0:T(8,128)}, f32[4,40,512]{2,1,0:T(8,128)}) custom-call(s32[4]{0:T(128)} %pad_add_fusion.where, f32[72,2048]{1,0:T(8,128)} %copy-done.1, f32[72,2048]{1,0:T(8,128)} %copy-done.8, f32[72,2048]{1,0:T(8,128)} %copy-done.3, f32[32,2048]{1,0:T(8,128)} %collective-permute-done.9.e3, f32[40,2048]{1,0:T(8,128)} %collective-permute-done.10.e4, ...), custom_call_target="tpu_custom_call" | custom-call | flops 8000000000 | bytes 10000000 | tf_op jit(solution)/shard_map/gram/pallas_call | solution.py:185
  79.5 2.7 %collective-permute-start.17 = (f32[40,512]{1,0:T(8,128)S(1)}, f32[40,512]{1,0:T(8,128)S(1)}, u32[]{:S(2)}, u32[]{:S(2)}) collective-permute-start(f32[40,512]{1,0:T(8,128)S(1)} %get-tuple-element.75), channel_id=1, source_target_pairs={{0,4},{2,6},{4,0},{6,2},{1,5},{3,7},{5,1},{7,3},{8,12},{10,14},{12... | collective-permute-start | bytes 245768 | tf_op jit(solution)/shard_map/ppermute | solution.py:460
  82.8 3.8 %collective-permute-done.17 = f32[40,512]{1,0:T(8,128)S(1)} collective-permute-done((f32[40,512]{1,0:T(8,128)S(1)}, f32[40,512]{1,0:T(8,128)S(1)}, u32[]{:S(2)}, u32[]{:S(2)}) %collective-permute-start.17) | collective-permute-done | bytes 81952 | tf_op jit(solution)/shard_map/ppermute | solution.py:460
  90.5 5.7 %all-to-all-start = ((f32[64,32,256]{2,1,0:T(8,128)}), f32[64,32,256]{2,1,0:T(8,128)}, u32[]{:S(2)}, u32[]{:S(2)}) async-start(f32[64,32,256]{2,1,0:T(8,128)} %broadcast_in_dim.35), calls=%async_computation | async-start | bytes 4194304 | tf_op jit(solution)/shard_map/all_to_all | solution.py:503
  96.9 29.2 %all-to-all-done = f32[64,32,256]{2,1,0:T(8,128)} async-done(((f32[64,32,256]{2,1,0:T(8,128)}), f32[64,32,256]{2,1,0:T(8,128)}, u32[]{:S(2)}, u32[]{:S(2)}) %all-to-all-start) | async-done | bytes 2097184 | tf_op jit(solution)/shard_map/all_to_all | solution.py:503
  128.1 1.9 collective-permute-start.20
  130.1 2.5 collective-permute-start.21
  132.6 25.2 %factor_begin.1 = (f32[1024,1024]{1,0:T(8,128)}, f32[512,256]{1,0:T(8,128)}) custom-call(s32[4]{0:T(128)} %pad_add_fusion.where, f32[2048,256]{1,0:T(8,128)} %bitcast.16.mine, f32[2048,256]{1,0:T(8,128)} %collective-permute-done.22.other, f32[8,128]{1,0:T(8,128)} %slice.70.misfit), custom_call_target="tpu_custom_call" | custom-call | flops 20000000000 | bytes 10000000 | tf_op jit(solution)/shard_map/factor_begin/pallas_call | solution.py:360
  166.0 24.3 %factor_finish.1 = (f32[1024,1024]{1,0:T(8,128)}, f32[512,256]{1,0:T(8,128)}) custom-call(f32[1024,1024]{1,0:T(8,128)} %get-tuple-element.47.before, f32[512,256]{1,0:T(8,128)} %get-tuple-element.48.earlier), custom_call_target="tpu_custom_call" | custom-call | flops 20000000000 | bytes 10000000 | tf_op jit(solution)/shard_map/factor_finish/pallas_call | solution.py:373
  193.0 14.3 %solve.1.work = f32[1024,512]{1,0:T(8,128)} custom-call(s32[4]{0:T(128)} %pad_add_fusion.where, f32[1024,1024]{1,0:T(8,128)} %get-tuple-element.49.system, f32[512,256]{1,0:T(8,128)} %get-tuple-element.48.earlier, f32[512,256]{1,0:T(8,128)} %get-tuple-element.50.later, f32[256,512]{1,0:T(8,128)} %pad_maximum_fusion.b0, ...), custom_call_target="tpu_custom_call" | custom-call | flops 5000000000 | bytes 10000000 | tf_op jit(solution)/shard_map/solve/pallas_call | solution.py:413
  207.4 10.4 %combine.1 = f32[1024,512]{1,0:T(8,128)} custom-call(f32[4096,256]{1,0:T(8,128)} %all-gather.2.cloned.1.call-done.rhs, f32[1024,512]{1,0:T(8,128)} %solve.1.work, f32[8,128]{1,0:T(8,128)} %slice.70.misfit), custom_call_target="tpu_custom_call" | custom-call | flops 6000000000 | bytes 10000000 | tf_op jit(solution)/shard_map/combine/pallas_call | solution.py:433
  217.8 31.4 %all_to_all.24 = f32[16,64,512]{2,1,0:T(8,128)S(1)} all-to-all(f32[16,64,512]{2,1,0:T(8,128)} %bitcast.29), channel_id=1, replica_groups=mesh['z'=4,'y'=4,'x'=4,'core'=2] {'z','y'}, dimensions={0} | all-to-all | bytes 4194304 | tf_op jit(solution)/shard_map/all_to_all | solution.py:524
  (90 shorter events, 38.2 us)
Async XLA Ops:
  6.5 15.2 %collective-permute-start = (f32[64,2048]{1,0:T(8,128)}, f32[64,2048]{1,0:T(8,128)S(1)}, u32[]{:S(2)}, u32[]{:S(2)}) collective-permute-start(f32[64,2048]{1,0:T(8,128)} %n0), channel_id=1, source_target_pairs={{0,8},{8,16},{16,24},{24,0},{1,9},{9,17},{17,25},{25,1},{2,10},{10... | collective-permute-start | bytes 1572872 | tf_op jit(solution)/shard_map/ppermute | solution.py:447
  8.2 13.6 %collective-permute-start.1 = (f32[64,2048]{1,0:T(8,128)}, f32[64,2048]{1,0:T(8,128)S(1)}, u32[]{:S(2)}, u32[]{:S(2)}) collective-permute-start(f32[64,2048]{1,0:T(8,128)} %n0), channel_id=1, source_target_pairs={{0,24},{8,0},{16,8},{24,16},{1,25},{9,1},{17,9},{25,17},{2,26},{10... | collective-permute-start | bytes 1572872 | tf_op jit(solution)/shard_map/ppermute | solution.py:448
  21.8 9.0 %collective-permute-start.2 = (f32[1,2176]{1,0:T(1,128)}, f32[1,2176]{1,0:T(1,128)S(1)}, u32[]{:S(2)}, u32[]{:S(2)}) collective-permute-start(f32[1,2176]{1,0:T(1,128)} %get-tuple-element.31), channel_id=1, source_target_pairs={{0,32},{32,0},{64,96},{96,64},{1,33},{33,1},{65,97},{97,65},{2,34}... | collective-permute-start | bytes 26120 | tf_op jit(solution)/shard_map/ppermute | solution.py:460
  23.8 7.0 %collective-permute-start.3 = (f32[1,2176]{1,0:T(1,128)}, f32[1,2176]{1,0:T(1,128)S(1)}, u32[]{:S(2)}, u32[]{:S(2)}) collective-permute-start(f32[1,2176]{1,0:T(1,128)} %get-tuple-element.31), channel_id=1, source_target_pairs={{0,64},{32,96},{64,0},{96,32},{1,65},{33,97},{65,1},{97,33},{2,66}... | collective-permute-start | bytes 26120 | tf_op jit(solution)/shard_map/ppermute | solution.py:460
  27.4 8.0 %collective-permute-start.5 = (f32[32,2048]{1,0:T(8,128)S(1)}, f32[32,2048]{1,0:T(8,128)S(1)}, u32[]{:S(2)}, u32[]{:S(2)}) collective-permute-start(f32[32,2048]{1,0:T(8,128)S(1)} %slice.45), channel_id=1, source_target_pairs={{0,8},{8,16},{16,24},{24,0},{1,9},{9,17},{17,25},{25,1},{2,10},{10... | collective-permute-start | bytes 786440 | tf_op jit(solution)/shard_map/ppermute | solution.py:454
  29.0 6.4 %collective-permute-start.6 = (f32[32,2048]{1,0:T(8,128)S(1)}, f32[32,2048]{1,0:T(8,128)S(1)}, u32[]{:S(2)}, u32[]{:S(2)}) collective-permute-start(f32[32,2048]{1,0:T(8,128)S(1)} %slice.46), channel_id=1, source_target_pairs={{0,24},{8,0},{16,8},{24,16},{1,25},{9,1},{17,9},{25,17},{2,26},{10... | collective-permute-start | bytes 786440 | tf_op jit(solution)/shard_map/ppermute | solution.py:455
  37.9 13.5 %collective-permute-start.8 = (f32[72,2048]{1,0:T(8,128)S(1)}, f32[72,2048]{1,0:T(8,128)S(1)}, u32[]{:S(2)}, u32[]{:S(2)}) collective-permute-start(f32[72,2048]{1,0:T(8,128)S(1)} %maximum_maximum_fusion.e0), channel_id=1, source_target_pairs={{0,24},{8,0},{16,8},{24,16},{1,25},{9,1},{17,9},{25,17},{2,26},{10... | collective-permute-start | bytes 1769480 | tf_op jit(solution)/shard_map/ppermute | solution.py:448
  40.9 17.6 %collective-permute-start.7 = (f32[72,2048]{1,0:T(8,128)S(1)}, f32[72,2048]{1,0:T(8,128)S(1)}, u32[]{:S(2)}, u32[]{:S(2)}) collective-permute-start(f32[72,2048]{1,0:T(8,128)S(1)} %maximum_maximum_fusion.e0), channel_id=1, source_target_pairs={{0,8},{8,16},{16,24},{24,0},{1,9},{9,17},{17,25},{25,1},{2,10},{10... | collective-permute-start | bytes 1769480 | tf_op jit(solution)/shard_map/ppermute | solution.py:447
  40.9 13.6 %collective-permute-start.11 = (f32[64,2048]{1,0:T(8,128)S(1)}, f32[64,2048]{1,0:T(8,128)S(1)}, u32[]{:S(2)}, u32[]{:S(2)}) collective-permute-start(f32[64,2048]{1,0:T(8,128)S(1)} %copy-done.2), channel_id=1, source_target_pairs={{0,32},{32,64},{64,96},{96,0},{1,33},{33,65},{65,97},{97,1},{2,34}... | collective-permute-start | bytes 1572872 | tf_op jit(solution)/shard_map/ppermute | solution.py:447
  40.9 14.4 %collective-permute-start.12 = (f32[64,2048]{1,0:T(8,128)S(1)}, f32[64,2048]{1,0:T(8,128)S(1)}, u32[]{:S(2)}, u32[]{:S(2)}) collective-permute-start(f32[64,2048]{1,0:T(8,128)S(1)} %copy-done.2), channel_id=1, source_target_pairs={{0,96},{32,0},{64,32},{96,64},{1,97},{33,1},{65,33},{97,65},{2,98}... | collective-permute-start | bytes 1572872 | tf_op jit(solution)/shard_map/ppermute | solution.py:448
  51.4 14.9 %collective-permute-start.10 = (f32[40,2048]{1,0:T(8,128)S(1)}, f32[40,2048]{1,0:T(8,128)}, u32[]{:S(2)}, u32[]{:S(2)}) collective-permute-start(f32[40,2048]{1,0:T(8,128)S(1)} %slice.61), channel_id=1, source_target_pairs={{0,24},{8,0},{16,8},{24,16},{1,25},{9,1},{17,9},{25,17},{2,26},{10... | collective-permute-start | bytes 983048 | tf_op jit(solution)/shard_map/ppermute | solution.py:455
  54.5 7.8 %collective-permute-start.13 = (f32[32,2048]{1,0:T(8,128)S(1)}, f32[32,2048]{1,0:T(8,128)}, u32[]{:S(2)}, u32[]{:S(2)}) collective-permute-start(f32[32,2048]{1,0:T(8,128)S(1)} %slice.62), channel_id=1, source_target_pairs={{0,32},{32,64},{64,96},{96,0},{1,33},{33,65},{65,97},{97,1},{2,34}... | collective-permute-start | bytes 786440 | tf_op jit(solution)/shard_map/ppermute | solution.py:454
  55.3 7.1 %collective-permute-start.14 = (f32[32,2048]{1,0:T(8,128)S(1)}, f32[32,2048]{1,0:T(8,128)}, u32[]{:S(2)}, u32[]{:S(2)}) collective-permute-start(f32[32,2048]{1,0:T(8,128)S(1)} %slice.63), channel_id=1, source_target_pairs={{0,96},{32,0},{64,32},{96,64},{1,97},{33,1},{65,33},{97,65},{2,98}... | collective-permute-start | bytes 786440 | tf_op jit(solution)/shard_map/ppermute | solution.py:455
  58.6 7.8 %collective-permute-start.9 = (f32[32,2048]{1,0:T(8,128)S(1)}, f32[32,2048]{1,0:T(8,128)}, u32[]{:S(2)}, u32[]{:S(2)}) collective-permute-start(f32[32,2048]{1,0:T(8,128)S(1)} %slice.60), channel_id=1, source_target_pairs={{0,8},{8,16},{16,24},{24,0},{1,9},{9,17},{17,25},{25,1},{2,10},{10... | collective-permute-start | bytes 786440 | tf_op jit(solution)/shard_map/ppermute | solution.py:454
  79.5 7.0 %collective-permute-start.17 = (f32[40,512]{1,0:T(8,128)S(1)}, f32[40,512]{1,0:T(8,128)S(1)}, u32[]{:S(2)}, u32[]{:S(2)}) collective-permute-start(f32[40,512]{1,0:T(8,128)S(1)} %get-tuple-element.75), channel_id=1, source_target_pairs={{0,4},{2,6},{4,0},{6,2},{1,5},{3,7},{5,1},{7,3},{8,12},{10,14},{12... | collective-permute-start | bytes 245768 | tf_op jit(solution)/shard_map/ppermute | solution.py:460
  90.5 35.6 %all-to-all-start = ((f32[64,32,256]{2,1,0:T(8,128)}), f32[64,32,256]{2,1,0:T(8,128)}, u32[]{:S(2)}, u32[]{:S(2)}) async-start(f32[64,32,256]{2,1,0:T(8,128)} %broadcast_in_dim.35), calls=%async_computation | async-start | bytes 4194304 | tf_op jit(solution)/shard_map/all_to_all | solution.py:503
  96.2 111.2 %all-gather.2.cloned.1.call-start = ((), (), s32[]{:S(2)}) async-start(), calls=%async_computation.2 | async-start | bytes 4227072 | tf_op jit(solution)/shard_map/all_gather | solution.py:502
  126.1 6.5 %collective-permute-start.22 = (f32[2048,256]{1,0:T(8,128)}, f32[2048,256]{1,0:T(8,128)}, u32[]{:S(2)}, u32[]{:S(2)}) collective-permute-start(f32[2048,256]{1,0:T(8,128)} %bitcast.16.mine), channel_id=1, source_target_pairs={{0,1},{1,0},{2,3},{3,2},{4,5},{5,4},{6,7},{7,6},{8,9},{9,8},{10,11... | collective-permute-start | bytes 6291464 | tf_op jit(solution)/shard_map/ppermute | solution.py:460
  127.9 29.9 %collective-permute-start.19 = (f32[64,2048]{1,0:T(8,128)}, f32[64,2048]{1,0:T(8,128)}, u32[]{:S(2)}, u32[]{:S(2)}) collective-permute-start(f32[64,2048]{1,0:T(8,128)} %get-tuple-element.57), channel_id=1, source_target_pairs={{0,32},{32,0},{64,96},{96,64},{1,33},{33,1},{65,97},{97,65},{2,34}... | collective-permute-start | bytes 1572872 | tf_op jit(solution)/shard_map/ppermute | solution.py:460
  128.1 29.7 %collective-permute-start.20 = (f32[64,2048]{1,0:T(8,128)}, f32[64,2048]{1,0:T(8,128)S(1)}, u32[]{:S(2)}, u32[]{:S(2)}) collective-permute-start(f32[64,2048]{1,0:T(8,128)} %get-tuple-element.56), channel_id=1, source_target_pairs={{0,64},{32,96},{64,0},{96,32},{1,65},{33,97},{65,1},{97,33},{2,66}... | collective-permute-start | bytes 1572872 | tf_op jit(solution)/shard_map/ppermute | solution.py:460
  130.1 27.8 %collective-permute-start.21 = (f32[64,2048]{1,0:T(8,128)}, f32[64,2048]{1,0:T(8,128)}, u32[]{:S(2)}, u32[]{:S(2)}) collective-permute-start(f32[64,2048]{1,0:T(8,128)} %get-tuple-element.55), channel_id=1, source_target_pairs={{0,96},{32,64},{64,32},{96,0},{1,97},{33,65},{65,33},{97,1},{2,98}... | collective-permute-start | bytes 1572872 | tf_op jit(solution)/shard_map/ppermute | solution.py:460
  160.9 31.4 %collective-permute-start.25 = (f32[256,512]{1,0:T(8,128)S(1)}, f32[256,512]{1,0:T(8,128)}, u32[]{:S(2)}, u32[]{:S(2)}) collective-permute-start(f32[256,512]{1,0:T(8,128)S(1)} %pad_maximum_fusion.3), channel_id=1, source_target_pairs={{0,24},{8,16},{16,8},{24,0},{1,25},{9,17},{17,9},{25,1},{2,26},{10... | collective-permute-start | bytes 1572872 | tf_op jit(solution)/shard_map/ppermute | solution.py:460
  162.0 30.3 %collective-permute-start.24 = (f32[256,512]{1,0:T(8,128)S(1)}, f32[256,512]{1,0:T(8,128)}, u32[]{:S(2)}, u32[]{:S(2)}) collective-permute-start(f32[256,512]{1,0:T(8,128)S(1)} %pad_maximum_fusion.2), channel_id=1, source_target_pairs={{0,16},{8,24},{16,0},{24,8},{1,17},{9,25},{17,1},{25,9},{2,18},{10... | collective-permute-start | bytes 1572872 | tf_op jit(solution)/shard_map/ppermute | solution.py:460
  164.6 28.4 %collective-permute-start.23 = (f32[256,512]{1,0:T(8,128)}, f32[256,512]{1,0:T(8,128)}, u32[]{:S(2)}, u32[]{:S(2)}) collective-permute-start(f32[256,512]{1,0:T(8,128)} %pad_maximum_fusion.1), channel_id=1, source_target_pairs={{0,8},{8,0},{16,24},{24,16},{1,9},{9,1},{17,25},{25,17},{2,10},{10... | collective-permute-start | bytes 1572872 | tf_op jit(solution)/shard_map/ppermute | solution.py:460
  (15 other events, 200.3 us)
Sparse Core Ops, SparseCore 0:
  100.1 89.7 all-gather.1

commit v6 on v5

--- a/solution.py
+++ b/solution.py
@@ -35,9 +35,8 @@
 
 
 def forward_kernel(
-    effect, base, fast, slow, init, fall, taps, weights, observed, var, pred, small, resp, coef
+    effect, base, fast, slow, init, fall, taps, weights, observed, var, pred, resp, coef
 ):
-    step = pl.program_id(0)
     members, cells = effect.shape
     w = slow[...]
     f = fast[...]
@@ -67,7 +66,6 @@
     lax.fori_loop(0, members // 8, rows, 0)
     position = lax.broadcasted_iota(jnp.int32, (BLOCK, LANES), 0)
     owner = lax.broadcasted_iota(jnp.int32, (members, LANES), 1) // 32
-    spread = jnp.zeros((1, LANES), f32)
     for group in range(cells // (4 * BLOCK)):
         lanes = slice(group * LANES, (group + 1) * LANES)
         table = jnp.zeros((BLOCK, LANES), f32)
@@ -80,22 +78,11 @@
         out = product[:members]
         for b in range(1, 4):
             out = jnp.where(owner == b, product[b * members : (b + 1) * members], out)
-        pred[:, lanes] = out
-        small[0:1, pl.ds(pl.multiple_of(step * (cells // 4) + group * LANES, LANES), LANES)] = jnp.sum(
-            out, axis=0, keepdims=True
-        )
+        pred[0:members, lanes] = out
         residual = observed[:, lanes] - out
-        spread = spread + jnp.sum(residual * residual, axis=0, keepdims=True) / var[:, lanes]
-    spread = jnp.broadcast_to(jnp.sum(spread, axis=1, keepdims=True), (1, LANES))
-    tail = pl.ds(small.shape[1] - LANES, LANES)
-
-    @pl.when(step == 0)
-    def _():
-        small[0:1, tail] = spread
-
-    @pl.when(step > 0)
-    def _():
-        small[0:1, tail] = small[0:1, tail] + spread
+        spread = jnp.sum(residual * residual, axis=0, keepdims=True) / var[:, lanes]
+        pred[members : members + 1, lanes] = jnp.sum(out, axis=0, keepdims=True)
+        pred[members + 1 :, lanes] = jnp.broadcast_to(spread, (7, LANES))
 
 
 def forward(effect, base, fast, slow, init, fall, taps, weights, observed, var):
@@ -114,11 +101,8 @@
             wide(3, CHUNK), wide(STEPS, CHUNK), wide(TAPS, obs_chunk), wide(TAPS, obs_chunk),
             wide(1, obs_chunk), wide(1, obs_chunk),
         ],
-        out_specs=[wide(members, obs_chunk), pl.BlockSpec((1, obs + LANES), lambda i: (0, 0))],
-        out_shape=[
-            jax.ShapeDtypeStruct((members, obs), f32),
-            jax.ShapeDtypeStruct((1, obs + LANES), f32),
-        ],
+        out_specs=wide(members + 8, obs_chunk),
+        out_shape=jax.ShapeDtypeStruct((members + 8, obs), f32),
         scratch_shapes=[pltpu.VMEM((members, CHUNK), f32), pltpu.VMEM((8, CHUNK), f32)],
         cost_estimate=cost(2e10),
         name="forward",
@@ -126,42 +110,46 @@
 
 
 def gram_kernel(
-    where, e0, e1, e2, e3, e4, p1, p2, p3, p4, n0, n1, n2, n3, n4, observed, var,
-    keep, send, left, right, total,
+    where, e0, e1, e2, e3, e4, t0, t2, p1, p2, p3, n0, n1, n2, observed, var,
+    keep, send, left, right, total, misfit,
 ):
     step = pl.program_id(0)
     zid, yid = where[0], where[1]
-    members = p1.shape[0]
+    members = n0.shape[0]
     half = members // 2
     member_count = members * Z * Y
     inv_root = 1.0 / math.sqrt(member_count - 1)
-    tails = e0[members:, :] + e1[members:, :] + e2[members:, :] + e4[half:, :]
+    tails = t0[...] + t2[...] + e3[half:, :] + e4[half:, :]
+    shares = jnp.sum(tails[1:2, :], axis=1, keepdims=True)
     mean = tails[0:1, :] / member_count
     inv_var = 1.0 / var[...]
     root_var = jnp.sqrt(var[...])
 
-    def pieces(own, back, forth, low, high):
-        return ((0, 0, own), (3, 0, back), (1, 0, forth), (2, 0, low), (2, half, high))
-
-    for (turn, skip, e), (_, _, n) in zip(pieces(e0, e1, e2, e3, e4), pieces(n0, n1, n2, n3, n4)):
-        count = n.shape[0]
+    kept = members + 8
+    for turn, skip, count, e, n, below in (
+        (0, 0, members, e0, n0, 0), (3, 0, members, e1, n1, 0), (1, 0, members, e2, n2, 0),
+        (2, 0, half, e3, e1, kept), (2, half, half, e4, e2, kept),
+    ):
         at = pl.multiple_of(((yid + turn) & 3) * members + skip, half)
         left[pl.ds(at, count), :] = (e[0:count, :] - mean) * inv_root
-        left[pl.ds(at + Y * members, count), :] = observed[...] + root_var * n[...] - e[0:count, :]
-    for turn, skip, p in pieces(e0, p1, p2, p3, p4):
-        count = half if turn == 2 else members
-        at = pl.multiple_of(((zid + turn) & 3) * members + skip, half)
-        right[pl.ds(at, count), :] = (p[0:count, :] - mean) * inv_root * inv_var
+        left[pl.ds(at + Y * members, count), :] = (
+            observed[...] + root_var * n[below : below + count, :] - e[0:count, :]
+        )
+    for turn, p in ((0, e0), (3, p1), (1, p2), (2, p3)):
+        at = pl.multiple_of(((zid + turn) & 3) * members, members)
+        right[pl.ds(at, members), :] = (p[0:members, :] - mean) * inv_root * inv_var
 
     product = mm_last(left[...], right[...])
 
     @pl.when(step == 0)
     def _():
         total[...] = product
+        misfit[...] = jnp.broadcast_to(shares, misfit.shape)
 
     @pl.when(step > 0)
     def _():
         total[...] = total[...] + product
+        misfit[...] = misfit[...] + shares
 
     @pl.when(step == pl.num_programs(0) - 1)
     def _():
@@ -171,11 +159,11 @@
                 at = pl.multiple_of((xid ^ a) * 64 + offset, 32)
                 part[a, 0:32, 0:TILE] = total[pl.ds(at, 32), :]
                 part[a, 0:32, TILE : 2 * TILE] = total[pl.ds(at + TILE, 32), :]
-                part[a, 32:40, :] = jnp.broadcast_to(tails[1:2, 0:1], (8, 2 * TILE))
+                part[a, 32:40, :] = jnp.broadcast_to(misfit[0:1, 0:1], (8, 2 * TILE))
 
 
 def gram_block(where, rows, columns, noise, observed, var):
-    members, obs = columns[0].shape
+    members, obs = noise[0].shape
     half = members // 2
     width = 512
 
@@ -185,8 +173,8 @@
     return pl.pallas_call(
         gram_kernel,
         grid=(obs // width,),
-        in_specs=[ANY_SMEM] + [chunk(members + 8)] * 3 + [chunk(half), chunk(half + 8)]
-        + [chunk(members)] * 2 + [chunk(half)] * 2 + [chunk(members)] * 3 + [chunk(half)] * 2
+        in_specs=[ANY_SMEM, chunk(members + 8)] + [chunk(members + half + 8)] * 2
+        + [chunk(half + 8)] * 2 + [chunk(8)] * 2 + [chunk(members + 8)] * 3 + [chunk(members)] * 3
         + [chunk(1)] * 2,
         out_specs=[pl.BlockSpec((X, 40, 2 * TILE), lambda i: (0, 0, 0))] * 2,
         out_shape=[jax.ShapeDtypeStruct((X, 40, 2 * TILE), f32)] * 2,
@@ -194,6 +182,7 @@
             pltpu.VMEM((2 * TILE, width), f32),
             pltpu.VMEM((TILE, width), f32),
             pltpu.VMEM((2 * TILE, TILE), f32),
+            pltpu.VMEM((8, LANES), f32),
         ],
         cost_estimate=cost(8e9),
         name="gram",
@@ -443,16 +432,9 @@
     )(rhs, work, misfit)
 
 
-def neighbours(value, axis):
-    back = lax.ppermute(value, axis, [(i, (i + 1) % 4) for i in range(4)])
-    forth = lax.ppermute(value, axis, [(i, (i + 3) % 4) for i in range(4)])
-    return back, forth
-
-
-def opposite(back, forth, axis):
-    half = 32
-    low = lax.ppermute(back[:half], axis, [(i, (i + 1) % 4) for i in range(4)])
-    high = lax.ppermute(forth[half:], axis, [(i, (i + 3) % 4) for i in range(4)])
+def onward(low, high, axis):
+    low = lax.ppermute(low, axis, [(i, (i + 1) % 4) for i in range(4)])
+    high = lax.ppermute(high, axis, [(i, (i + 3) % 4) for i in range(4)])
     return low, high
 
 
@@ -479,22 +461,27 @@
     where = jnp.stack([zid, yid, core, lax.axis_index("x")]).astype(jnp.int32)
     observed = observed[None, :]
     obs_var = obs_var[None, :]
-    noise = neighbours(obs_noise, "y")
-    predicted, small = forward(
+    noise = onward(obs_noise, obs_noise, "y")
+    predicted = forward(
         turnover_effect, base_rate[None, :], fast_rate[None, :], slow_rate[None, :],
         init_pools, litterfall, obs_taps.T, obs_weights.T, observed, obs_var,
     )
-    small, noise = lax.optimization_barrier((small, noise))
-    noise = (obs_noise,) + noise + opposite(*noise, "y")
-    small = small + sum(swap(small, "z", Z, b) for b in range(1, Z))
-    small, predicted, noise = lax.optimization_barrier((small, predicted, noise))
-    extended = jnp.concatenate(
-        [predicted, small[:, :obs], jnp.broadcast_to(small[:, obs : obs + 1], (7, obs))], axis=0
+    predicted, noise = lax.optimization_barrier((predicted, noise))
+    half = members // 2
+    columns = onward(predicted, predicted, "z") + (swap(predicted, "z", Z, 2),)
+    back, forth = onward(
+        jnp.concatenate([predicted, noise[0][:half]], axis=0),
+        jnp.concatenate([predicted, noise[1][half:]], axis=0),
+        "y",
     )
-    rows = neighbours(extended, "y")
-    columns = neighbours(predicted, "z")
-    rows = (extended,) + rows + opposite(*rows, "y")
-    columns = columns + opposite(*columns, "z")
+    sums = sum((block[members:] for block in columns), predicted[members:])
+    sums, back, forth = lax.optimization_barrier((sums, back, forth))
+    rows = (predicted, back, forth) + onward(
+        jnp.concatenate([back[:half], sums], axis=0),
+        jnp.concatenate([forth[half:members], sums], axis=0),
+        "y",
+    ) + (sums, swap(sums, "y", Y, 2))
+    noise = (obs_noise,) + noise
     keep, send = gram_block(where, rows, columns, noise, observed, obs_var)
     part = keep + swap(send, "core", 2, 1)
     shared = part[0] + sum(swap(part[a], "x", X, a) for a in range(1, X))

time: 259 us -> 259 us (level)
  waiting for transfers between devices: 58.4 us -> 66.9 us
  starting transfers between devices: 44.5 us -> 36.7 us
    ppermute x14 -> x13, waiting for transfers between devices: 9.92 us -> 15.6 us  [swap(): return lax.ppermute(value, axis, [(i, i ^ bit) for i in range(size)])]
    ppermute x12 -> x8, starting transfers between devices: 19.4 us -> 14 us  [the longest x4 7.57 us: onward(): high = lax.ppermute(high, axis, [(i, (i + 3) % 4) for i in range(4)])]
    ppermute x12 -> x8, waiting for transfers between devices: 18.6 us -> 21.5 us  [the longest x4 11.3 us: onward(): high = lax.ppermute(high, axis, [(i, (i + 3) % 4) for i in range(4)])]
    ppermute x14 -> x13, starting transfers between devices: 19.4 us -> 16.9 us  [swap(): return lax.ppermute(value, axis, [(i, i ^ bit) for i in range(size)])]
  transfers between devices with their start and end apart: 28 -> 23, of which waited for: 14 -> 11; matrix products, arithmetic and copies ran while one was open for 3% -> 4% of each run, Pallas kernels for 28% -> 28%
where the time goes in v6:
time: 259 us
  Pallas kernels  92 us (36%)
  waiting for transfers between devices  66.9 us (26%)
  starting transfers between devices  36.7 us (14%)
  blocking collectives  31.3 us (12%)
  between operations  13.6 us (5%)
  local copies, waits for them, and re-layouts  9.98 us (4%)
  other arithmetic  8.08 us (3%)
    all_to_all x1, blocking collectives, body(): lax.all_to_all(change, ('z', 'y'), 0, 1, tiled=True)  31.3 us
    all_to_all x1, waiting for transfers between devices, body(): lax.all_to_all(jnp.broadcast_to(piece[None], (Z * Y * X, 32, TILE)), ('z'...  29.2 us
    pallas_call x1, Pallas kernels, factor_begin(): pl.pallas_call(begin_kernel, in_specs=[ANY_SMEM, ANY_VMEM, ANY_VMEM, ANY_...  25.3 us
    pallas_call x1, Pallas kernels, factor_finish(): pl.pallas_call(finish_kernel, in_specs=[pl.BlockSpec(memory_space=pl.ANY)...  24.3 us
    ppermute x13, starting transfers between devices, swap(): return lax.ppermute(value, axis, [(i, i ^ bit) for i in range(size)])  16.9 us
    ppermute x13, waiting for transfers between devices, swap(): return lax.ppermute(value, axis, [(i, i ^ bit) for i in range(size)])  15.6 us
    pallas_call x1, Pallas kernels, solve(): pl.pallas_call(solve_kernel, in_specs=[ANY_SMEM] + [ANY_VMEM] * 7, out_sp...  14.3 us
    ppermute x4, waiting for transfers between devices, onward(): high = lax.ppermute(high, axis, [(i, (i + 3) % 4) for i in range(4)])  11.3 us
  transfers between devices with their start and end apart: 23, of which 11 were waited for; matrix products, arithmetic and copies ran while one was open for 4% of the time, Pallas kernels for 28%

profile of v6, /device:TPU:0, one launch (start us, length us, event | category | flops | bytes accessed | tf_op | source)
XLA Modules:
  0.0 258.6 jit_solution(10030632372686606518)
XLA Ops:
  9.8 8.9 %forward.1.e0 = f32[72,2048]{1,0:T(8,128)} custom-call(f32[64,8192]{1,0:T(8,128)} %effect.1, f32[1,8192]{1,0:T(1,128)} %bitcast.29, f32[1,8192]{1,0:T(1,128)} %bitcast.30, f32[1,8192]{1,0:T(1,128)} %bitcast.31, f32[3,8192]{1,0:T(4,128)} %init.1, f32[6,8192]{1,0:T(8,128)} %fall.1, s32[4,2048]{1,0:T(4,128)} %bitcast.32, f32[4,2048]{1,0:T(4,128)} %bitcast.33, ...), custom_call_target="tpu_custom_call" | custom-call | flops 20000000000 | bytes 10000000 | tf_op jit(solution)/shard_map/forward/pallas_call | solution.py:96
  18.7 3.1 %collective-permute-done.n1 = f32[64,2048]{1,0:T(8,128)S(1)} collective-permute-done((f32[64,2048]{1,0:T(8,128)}, f32[64,2048]{1,0:T(8,128)S(1)}, u32[]{:S(2)}, u32[]{:S(2)}) %collective-permute-start) | collective-permute-done | bytes 524320 | tf_op jit(solution)/shard_map/ppermute | solution.py:436
  21.8 2.0 collective-permute-start.2
  23.8 2.2 collective-permute-start.3
  26.0 1.8 collective-permute-start.4
  32.4 7.1 %collective-permute-done.2.p1 = f32[72,2048]{1,0:T(8,128)S(1)} collective-permute-done((f32[72,2048]{1,0:T(8,128)}, f32[72,2048]{1,0:T(8,128)S(1)}, u32[]{:S(2)}, u32[]{:S(2)}) %collective-permute-start.2) | collective-permute-done | bytes 589856 | tf_op jit(solution)/shard_map/ppermute | solution.py:436
  39.4 11.3 %collective-permute-done.3.p2 = f32[72,2048]{1,0:T(8,128)S(1)} collective-permute-done((f32[72,2048]{1,0:T(8,128)}, f32[72,2048]{1,0:T(8,128)S(1)}, u32[]{:S(2)}, u32[]{:S(2)}) %collective-permute-start.3) | collective-permute-done | bytes 589856 | tf_op jit(solution)/shard_map/ppermute | solution.py:437
  55.9 2.1 collective-permute-start.8
  59.9 5.6 %collective-permute-done.9.t2 = f32[8,2048]{1,0:T(8,128)S(1)} collective-permute-done((f32[8,2048]{1,0:T(8,128)S(1)}, f32[8,2048]{1,0:T(8,128)S(1)}, u32[]{:S(2)}, u32[]{:S(2)}) %collective-permute-start.9) | collective-permute-done | bytes 65568 | tf_op jit(solution)/shard_map/ppermute | solution.py:442
  67.1 8.7 %gram.1 = (f32[4,40,512]{2,1,0:T(8,128)}, f32[4,40,512]{2,1,0:T(8,128)}) custom-call(s32[4]{0:T(128)} %pad_add_fusion.where, f32[72,2048]{1,0:T(8,128)} %forward.1.e0, f32[104,2048]{1,0:T(8,128)} %copy-done.4, f32[104,2048]{1,0:T(8,128)} %copy-done.5, f32[40,2048]{1,0:T(8,128)} %copy-done.9, f32[40,2048]{1,0:T(8,128)} %copy-done.10, f32[8,2048]{1,0:T(8,128)} %copy-done.1, ...), custom_call_target="tpu_custom_call" | custom-call | flops 8000000000 | bytes 10000000 | tf_op jit(solution)/shard_map/gram/pallas_call | solution.py:173
  75.9 1.8 collective-permute-done.10
  80.3 2.7 %collective-permute-start.12 = (f32[40,512]{1,0:T(8,128)S(1)}, f32[40,512]{1,0:T(8,128)S(1)}, u32[]{:S(2)}, u32[]{:S(2)}) collective-permute-start(f32[40,512]{1,0:T(8,128)S(1)} %get-tuple-element.65), channel_id=1, source_target_pairs={{0,4},{2,6},{4,0},{6,2},{1,5},{3,7},{5,1},{7,3},{8,12},{10,14},{12... | collective-permute-start | bytes 245768 | tf_op jit(solution)/shard_map/ppermute | solution.py:442
  83.6 3.8 %collective-permute-done.12 = f32[40,512]{1,0:T(8,128)S(1)} collective-permute-done((f32[40,512]{1,0:T(8,128)S(1)}, f32[40,512]{1,0:T(8,128)S(1)}, u32[]{:S(2)}, u32[]{:S(2)}) %collective-permute-start.12) | collective-permute-done | bytes 81952 | tf_op jit(solution)/shard_map/ppermute | solution.py:442
  91.3 5.7 %all-to-all-start = ((f32[64,32,256]{2,1,0:T(8,128)}), f32[64,32,256]{2,1,0:T(8,128)}, u32[]{:S(2)}, u32[]{:S(2)}) async-start(f32[64,32,256]{2,1,0:T(8,128)} %broadcast_in_dim.26), calls=%async_computation | async-start | bytes 4194304 | tf_op jit(solution)/shard_map/all_to_all | solution.py:490
  97.7 29.2 %all-to-all-done = f32[64,32,256]{2,1,0:T(8,128)} async-done(((f32[64,32,256]{2,1,0:T(8,128)}), f32[64,32,256]{2,1,0:T(8,128)}, u32[]{:S(2)}, u32[]{:S(2)}) %all-to-all-start) | async-done | bytes 2097184 | tf_op jit(solution)/shard_map/all_to_all | solution.py:490
  128.9 1.9 collective-permute-start.15
  130.8 2.5 collective-permute-start.16
  133.3 25.3 %factor_begin.1 = (f32[1024,1024]{1,0:T(8,128)}, f32[512,256]{1,0:T(8,128)}) custom-call(s32[4]{0:T(128)} %pad_add_fusion.where, f32[2048,256]{1,0:T(8,128)} %bitcast.15.mine, f32[2048,256]{1,0:T(8,128)} %collective-permute-done.17.other, f32[8,128]{1,0:T(8,128)} %slice.69.misfit), custom_call_target="tpu_custom_call" | custom-call | flops 20000000000 | bytes 10000000 | tf_op jit(solution)/shard_map/factor_begin/pallas_call | solution.py:349
  159.8 1.9 constant_dynamic-slice_fusion
  162.8 1.8 collective-permute-start.19
  166.8 24.3 %factor_finish.1 = (f32[1024,1024]{1,0:T(8,128)}, f32[512,256]{1,0:T(8,128)}) custom-call(f32[1024,1024]{1,0:T(8,128)} %get-tuple-element.35.before, f32[512,256]{1,0:T(8,128)} %get-tuple-element.36.earlier), custom_call_target="tpu_custom_call" | custom-call | flops 20000000000 | bytes 10000000 | tf_op jit(solution)/shard_map/factor_finish/pallas_call | solution.py:362
  193.9 14.3 %solve.1.work = f32[1024,512]{1,0:T(8,128)} custom-call(s32[4]{0:T(128)} %pad_add_fusion.where, f32[1024,1024]{1,0:T(8,128)} %get-tuple-element.37.system, f32[512,256]{1,0:T(8,128)} %get-tuple-element.36.earlier, f32[512,256]{1,0:T(8,128)} %get-tuple-element.38.later, f32[256,512]{1,0:T(8,128)} %pad_maximum_fusion.2.b0, ...), custom_call_target="tpu_custom_call" | custom-call | flops 5000000000 | bytes 10000000 | tf_op jit(solution)/shard_map/solve/pallas_call | solution.py:402
  208.2 10.4 %combine.1 = f32[1024,512]{1,0:T(8,128)} custom-call(f32[4096,256]{1,0:T(8,128)} %all-gather.2.cloned.1.call-done.rhs, f32[1024,512]{1,0:T(8,128)} %solve.1.work, f32[8,128]{1,0:T(8,128)} %slice.69.misfit), custom_call_target="tpu_custom_call" | custom-call | flops 6000000000 | bytes 10000000 | tf_op jit(solution)/shard_map/combine/pallas_call | solution.py:422
  218.6 31.3 %all_to_all.24 = f32[16,64,512]{2,1,0:T(8,128)S(1)} all-to-all(f32[16,64,512]{2,1,0:T(8,128)} %bitcast.28), channel_id=1, replica_groups=mesh['z'=4,'y'=4,'x'=4,'core'=2] {'z','y'}, dimensions={0} | all-to-all | bytes 4194304 | tf_op jit(solution)/shard_map/all_to_all | solution.py:511
  (77 shorter events, 35.2 us)
Async XLA Ops:
  6.5 15.2 %collective-permute-start = (f32[64,2048]{1,0:T(8,128)}, f32[64,2048]{1,0:T(8,128)S(1)}, u32[]{:S(2)}, u32[]{:S(2)}) collective-permute-start(f32[64,2048]{1,0:T(8,128)} %n0.1), channel_id=1, source_target_pairs={{0,8},{8,16},{16,24},{24,0},{1,9},{9,17},{17,25},{25,1},{2,10},{10... | collective-permute-start | bytes 1572872 | tf_op jit(solution)/shard_map/ppermute | solution.py:436
  8.2 13.6 %collective-permute-start.1 = (f32[64,2048]{1,0:T(8,128)}, f32[64,2048]{1,0:T(8,128)S(1)}, u32[]{:S(2)}, u32[]{:S(2)}) collective-permute-start(f32[64,2048]{1,0:T(8,128)} %n0.1), channel_id=1, source_target_pairs={{0,24},{8,0},{16,8},{24,16},{1,25},{9,1},{17,9},{25,17},{2,26},{10... | collective-permute-start | bytes 1572872 | tf_op jit(solution)/shard_map/ppermute | solution.py:437
  21.8 17.6 %collective-permute-start.2 = (f32[72,2048]{1,0:T(8,128)}, f32[72,2048]{1,0:T(8,128)S(1)}, u32[]{:S(2)}, u32[]{:S(2)}) collective-permute-start(f32[72,2048]{1,0:T(8,128)} %forward.1.e0), channel_id=1, source_target_pairs={{0,32},{32,64},{64,96},{96,0},{1,33},{33,65},{65,97},{97,1},{2,34}... | collective-permute-start | bytes 1769480 | tf_op jit(solution)/shard_map/ppermute | solution.py:436
  23.8 27.0 %collective-permute-start.3 = (f32[72,2048]{1,0:T(8,128)}, f32[72,2048]{1,0:T(8,128)S(1)}, u32[]{:S(2)}, u32[]{:S(2)}) collective-permute-start(f32[72,2048]{1,0:T(8,128)} %forward.1.e0), channel_id=1, source_target_pairs={{0,96},{32,0},{64,32},{96,64},{1,97},{33,1},{65,33},{97,65},{2,98}... | collective-permute-start | bytes 1769480 | tf_op jit(solution)/shard_map/ppermute | solution.py:437
  26.0 26.5 %collective-permute-start.4 = (f32[72,2048]{1,0:T(8,128)}, f32[72,2048]{1,0:T(8,128)S(1)}, u32[]{:S(2)}, u32[]{:S(2)}) collective-permute-start(f32[72,2048]{1,0:T(8,128)} %forward.1.e0), channel_id=1, source_target_pairs={{0,64},{32,96},{64,0},{96,32},{1,65},{33,97},{65,1},{97,33},{2,66}... | collective-permute-start | bytes 1769480 | tf_op jit(solution)/shard_map/ppermute | solution.py:442
  29.1 24.3 %collective-permute-start.5 = (f32[104,2048]{1,0:T(8,128)S(1)}, f32[104,2048]{1,0:T(8,128)S(1)}, u32[]{:S(2)}, u32[]{:S(2)}) collective-permute-start(f32[104,2048]{1,0:T(8,128)S(1)} %get-tuple-element.48), channel_id=1, source_target_pairs={{0,8},{8,16},{16,24},{24,0},{1,9},{9,17},{17,25},{25,1},{2,10},{10... | collective-permute-start | bytes 2555912 | tf_op jit(solution)/shard_map/ppermute | solution.py:436
  30.7 22.7 %collective-permute-start.6 = (f32[104,2048]{1,0:T(8,128)S(1)}, f32[104,2048]{1,0:T(8,128)S(1)}, u32[]{:S(2)}, u32[]{:S(2)}) collective-permute-start(f32[104,2048]{1,0:T(8,128)S(1)} %get-tuple-element.47), channel_id=1, source_target_pairs={{0,24},{8,0},{16,8},{24,16},{1,25},{9,1},{17,9},{25,17},{2,26},{10... | collective-permute-start | bytes 2555912 | tf_op jit(solution)/shard_map/ppermute | solution.py:437
  54.7 10.9 %collective-permute-start.7 = (f32[40,2048]{1,0:T(8,128)S(1)}, f32[40,2048]{1,0:T(8,128)S(1)}, u32[]{:S(2)}, u32[]{:S(2)}) collective-permute-start(f32[40,2048]{1,0:T(8,128)S(1)} %get-tuple-element.71), channel_id=1, source_target_pairs={{0,8},{8,16},{16,24},{24,0},{1,9},{9,17},{17,25},{25,1},{2,10},{10... | collective-permute-start | bytes 983048 | tf_op jit(solution)/shard_map/ppermute | solution.py:436
  55.9 9.7 %collective-permute-start.8 = (f32[40,2048]{1,0:T(8,128)S(1)}, f32[40,2048]{1,0:T(8,128)S(1)}, u32[]{:S(2)}, u32[]{:S(2)}) collective-permute-start(f32[40,2048]{1,0:T(8,128)S(1)} %get-tuple-element.70), channel_id=1, source_target_pairs={{0,24},{8,0},{16,8},{24,16},{1,25},{9,1},{17,9},{25,17},{2,26},{10... | collective-permute-start | bytes 983048 | tf_op jit(solution)/shard_map/ppermute | solution.py:437
  58.0 7.6 %collective-permute-start.9 = (f32[8,2048]{1,0:T(8,128)S(1)}, f32[8,2048]{1,0:T(8,128)S(1)}, u32[]{:S(2)}, u32[]{:S(2)}) collective-permute-start(f32[8,2048]{1,0:T(8,128)S(1)} %slice_add_fusion.t0), channel_id=1, source_target_pairs={{0,16},{8,24},{16,0},{24,8},{1,17},{9,25},{17,1},{25,9},{2,18},{10... | collective-permute-start | bytes 196616 | tf_op jit(solution)/shard_map/ppermute | solution.py:442
  75.8 1.9 collective-permute-start.10
  78.8 4.8 %collective-permute-start.11 = (f32[40,512]{1,0:T(8,128)S(1)}, f32[40,512]{1,0:T(8,128)S(1)}, u32[]{:S(2)}, u32[]{:S(2)}) collective-permute-start(f32[40,512]{1,0:T(8,128)S(1)} %get-tuple-element.67), channel_id=1, source_target_pairs={{0,2},{2,0},{4,6},{6,4},{1,3},{3,1},{5,7},{7,5},{8,10},{10,8},{12,... | collective-permute-start | bytes 245768 | tf_op jit(solution)/shard_map/ppermute | solution.py:442
  80.3 7.0 %collective-permute-start.12 = (f32[40,512]{1,0:T(8,128)S(1)}, f32[40,512]{1,0:T(8,128)S(1)}, u32[]{:S(2)}, u32[]{:S(2)}) collective-permute-start(f32[40,512]{1,0:T(8,128)S(1)} %get-tuple-element.65), channel_id=1, source_target_pairs={{0,4},{2,6},{4,0},{6,2},{1,5},{3,7},{5,1},{7,3},{8,12},{10,14},{12... | collective-permute-start | bytes 245768 | tf_op jit(solution)/shard_map/ppermute | solution.py:442
  83.1 6.0 %collective-permute-start.13 = (f32[40,512]{1,0:T(8,128)S(1)}, f32[40,512]{1,0:T(8,128)S(1)}, u32[]{:S(2)}, u32[]{:S(2)}) collective-permute-start(f32[40,512]{1,0:T(8,128)S(1)} %get-tuple-element.66), channel_id=1, source_target_pairs={{0,6},{2,4},{4,2},{6,0},{1,7},{3,5},{5,3},{7,1},{8,14},{10,12},{12... | collective-permute-start | bytes 245768 | tf_op jit(solution)/shard_map/ppermute | solution.py:442
  91.2 36.2 %copy-start = (f32[64,8192]{1,0:T(8,128)S(1)}, f32[64,8192]{1,0:T(8,128)}, u32[]{:S(2)}) copy-start(f32[64,8192]{1,0:T(8,128)} %effect.1) | copy-start | bytes 6291460
  91.3 35.6 %all-to-all-start = ((f32[64,32,256]{2,1,0:T(8,128)}), f32[64,32,256]{2,1,0:T(8,128)}, u32[]{:S(2)}, u32[]{:S(2)}) async-start(f32[64,32,256]{2,1,0:T(8,128)} %broadcast_in_dim.26), calls=%async_computation | async-start | bytes 4194304 | tf_op jit(solution)/shard_map/all_to_all | solution.py:490
  97.0 111.2 %all-gather.2.cloned.1.call-start = ((), (), s32[]{:S(2)}) async-start(), calls=%async_computation.2 | async-start | bytes 4227072 | tf_op jit(solution)/shard_map/all_gather | solution.py:489
  126.9 6.5 %collective-permute-start.17 = (f32[2048,256]{1,0:T(8,128)}, f32[2048,256]{1,0:T(8,128)}, u32[]{:S(2)}, u32[]{:S(2)}) collective-permute-start(f32[2048,256]{1,0:T(8,128)} %bitcast.15.mine), channel_id=1, source_target_pairs={{0,1},{1,0},{2,3},{3,2},{4,5},{5,4},{6,7},{7,6},{8,9},{9,8},{10,11... | collective-permute-start | bytes 6291464 | tf_op jit(solution)/shard_map/ppermute | solution.py:442
  128.6 30.0 %collective-permute-start.14 = (f32[64,2048]{1,0:T(8,128)}, f32[64,2048]{1,0:T(8,128)}, u32[]{:S(2)}, u32[]{:S(2)}) collective-permute-start(f32[64,2048]{1,0:T(8,128)} %get-tuple-element.45), channel_id=1, source_target_pairs={{0,32},{32,0},{64,96},{96,64},{1,33},{33,1},{65,97},{97,65},{2,34}... | collective-permute-start | bytes 1572872 | tf_op jit(solution)/shard_map/ppermute | solution.py:442
  128.9 29.7 %collective-permute-start.15 = (f32[64,2048]{1,0:T(8,128)}, f32[64,2048]{1,0:T(8,128)S(1)}, u32[]{:S(2)}, u32[]{:S(2)}) collective-permute-start(f32[64,2048]{1,0:T(8,128)} %get-tuple-element.44), channel_id=1, source_target_pairs={{0,64},{32,96},{64,0},{96,32},{1,65},{33,97},{65,1},{97,33},{2,66}... | collective-permute-start | bytes 1572872 | tf_op jit(solution)/shard_map/ppermute | solution.py:442
  130.8 27.8 %collective-permute-start.16 = (f32[64,2048]{1,0:T(8,128)}, f32[64,2048]{1,0:T(8,128)}, u32[]{:S(2)}, u32[]{:S(2)}) collective-permute-start(f32[64,2048]{1,0:T(8,128)} %get-tuple-element.43), channel_id=1, source_target_pairs={{0,96},{32,64},{64,32},{96,0},{1,97},{33,65},{65,33},{97,1},{2,98}... | collective-permute-start | bytes 1572872 | tf_op jit(solution)/shard_map/ppermute | solution.py:442
  161.7 31.4 %collective-permute-start.20 = (f32[256,512]{1,0:T(8,128)S(1)}, f32[256,512]{1,0:T(8,128)}, u32[]{:S(2)}, u32[]{:S(2)}) collective-permute-start(f32[256,512]{1,0:T(8,128)S(1)} %pad_maximum_fusion.5), channel_id=1, source_target_pairs={{0,24},{8,16},{16,8},{24,0},{1,25},{9,17},{17,9},{25,1},{2,26},{10... | collective-permute-start | bytes 1572872 | tf_op jit(solution)/shard_map/ppermute | solution.py:442
  162.8 30.3 %collective-permute-start.19 = (f32[256,512]{1,0:T(8,128)S(1)}, f32[256,512]{1,0:T(8,128)}, u32[]{:S(2)}, u32[]{:S(2)}) collective-permute-start(f32[256,512]{1,0:T(8,128)S(1)} %pad_maximum_fusion.4), channel_id=1, source_target_pairs={{0,16},{8,24},{16,0},{24,8},{1,17},{9,25},{17,1},{25,9},{2,18},{10... | collective-permute-start | bytes 1572872 | tf_op jit(solution)/shard_map/ppermute | solution.py:442
  165.4 28.4 %collective-permute-start.18 = (f32[256,512]{1,0:T(8,128)}, f32[256,512]{1,0:T(8,128)}, u32[]{:S(2)}, u32[]{:S(2)}) collective-permute-start(f32[256,512]{1,0:T(8,128)} %pad_maximum_fusion.3), channel_id=1, source_target_pairs={{0,8},{8,0},{16,24},{24,16},{1,9},{9,1},{17,25},{25,17},{2,10},{10... | collective-permute-start | bytes 1572872 | tf_op jit(solution)/shard_map/ppermute | solution.py:442
  (11 other events, 111.0 us)
Sparse Core Ops, SparseCore 0:
  100.9 89.7 all-gather.1

commit v7 on v6

--- a/solution.py
+++ b/solution.py
@@ -409,27 +409,41 @@
     )(where, system, earlier, later, *blocks)
 
 
-def combine_kernel(rhs, work, misfit, out):
+def combine_kernel(where, mine, other, work, misfit, out):
+    core = where[2]
     scale = f32(1024 * 16384) / misfit[0:1, 0:1]
-    total = mm(rhs[0:TILE, :], work[0:TILE, :])
-    for y in range(1, Y):
-        total = total + mm(rhs[y * TILE : (y + 1) * TILE, :], work[y * TILE : (y + 1) * TILE, :])
-    out[...] = scale * total
-
-
-def combine(rhs, work, misfit):
+    rows = TILE // 2
+    total = jnp.zeros((TILE, work.shape[1]), f32)
+    for y in range(Y):
+        at = slice(y * rows, (y + 1) * rows)
+        block = jnp.concatenate([mine[at, :], other[at, :]], axis=0)
+        total = total + mm(block, work[y * TILE : (y + 1) * TILE, :])
+    total = scale * total
+    for c, offset in enumerate((core * 32, 32 - core * 32)):
+        for x in range(X):
+            low = c * rows + x * 32
+            out[pl.ds(pl.multiple_of(x * 64 + offset, 32), 32), :] = total[low : low + 32, :]
+
+
+def combine(where, mine, other, work, misfit):
     n, width = work.shape
+    rows = pl.BlockSpec((Y * TILE // 2, TILE), lambda z: (z, 0))
     return pl.pallas_call(
         combine_kernel,
         grid=(Z,),
-        in_specs=[
-            pl.BlockSpec((Y * TILE, TILE), lambda z: (z, 0)), ANY_VMEM, ANY_VMEM,
-        ],
+        in_specs=[ANY_SMEM, rows, rows, ANY_VMEM, ANY_VMEM],
         out_specs=pl.BlockSpec((TILE, width), lambda z: (z, 0)),
         out_shape=jax.ShapeDtypeStruct((n, width), f32),
         cost_estimate=cost(6e9),
         name="combine",
-    )(rhs, work, misfit)
+    )(where, mine, other, work, misfit)
+
+
+def collect(piece):
+    pieces = lax.all_to_all(
+        jnp.broadcast_to(piece[None], (Z * Y * X,) + piece.shape), ("z", "y", "x"), 0, 0, tiled=True
+    )
+    return pieces.reshape(Z * Y * X * piece.shape[0], piece.shape[1])
 
 
 def onward(low, high, axis):
@@ -486,11 +500,9 @@
     part = keep + swap(send, "core", 2, 1)
     shared = part[0] + sum(swap(part[a], "x", X, a) for a in range(1, X))
     piece, right, misfit = shared[:32, :TILE], shared[:32, TILE:], shared[32:, :LANES]
-    rhs = lax.all_gather(right, ("z", "y", "x", "core"), axis=0, tiled=True)
-    mine = lax.all_to_all(
-        jnp.broadcast_to(piece[None], (Z * Y * X, 32, TILE)), ("z", "y", "x"), 0, 0, tiled=True
-    ).reshape(Z * Y * X * 32, TILE)
-    effect, mine = lax.optimization_barrier((turnover_effect, mine))
+    mine = collect(piece)
+    effect, right, mine = lax.optimization_barrier((turnover_effect, right, mine))
+    right = collect(right)
     other = swap(mine, "core", 2, 1)
     wide = cells // Z
     strip = [lax.dynamic_slice_in_dim(effect, (zid ^ b) * wide, wide, 1) for b in range(Z)]
@@ -506,8 +518,9 @@
     ]
     cut = [cut[0]] + [swap(cut[a], "y", Y, a) for a in range(1, Y)]
     system, later = factor_finish(system, inverse)
+    right, cut, system = lax.optimization_barrier((right, cut, system))
     work = solve(where, system, inverse, later, cut)
-    change = combine(rhs, work, misfit)
+    change = combine(where, right, swap(right, "core", 2, 1), work, misfit)
     return turnover_effect + lax.all_to_all(change, ("z", "y"), 0, 1, tiled=True)
 
 

time: 259 us -> 265 us (1.023)
  blocking collectives: 31.3 us -> 67.9 us
  waiting for transfers between devices: 66.9 us -> 49.7 us
  between operations: 13.6 us -> 0.26 us
    all_to_all x0 -> x1, blocking collectives: none -> 34.8 us  [collect(): lax.all_to_all(jnp.broadcast_to(piece[None], (Z * Y * X,) + piece.shape),...]
    all_to_all x1, waiting for transfers between devices: 29.2 us -> 0.01 us  [collect(): lax.all_to_all(jnp.broadcast_to(piece[None], (Z * Y * X,) + piece.shape),...]
    ppermute x13 -> x14, waiting for transfers between devices: 15.6 us -> 28.2 us  [swap(): return lax.ppermute(value, axis, [(i, i ^ bit) for i in range(size)])]
    ppermute x13 -> x14, starting transfers between devices: 16.9 us -> 17.2 us  [swap(): return lax.ppermute(value, axis, [(i, i ^ bit) for i in range(size)])]
  transfers between devices with their start and end apart: 23 -> 23, of which waited for: 11 -> 10; matrix products, arithmetic and copies ran while one was open for 4% -> 5% of each run, Pallas kernels for 28% -> 27%
where the time goes in v7:
time: 265 us
  Pallas kernels  91.9 us (35%)
  blocking collectives  67.9 us (26%)
  waiting for transfers between devices  49.7 us (19%)
  starting transfers between devices  37 us (14%)
  local copies, waits for them, and re-layouts  9.68 us (4%)
  other arithmetic  8.17 us (3%)
    all_to_all x1, blocking collectives, collect(): lax.all_to_all(jnp.broadcast_to(piece[None], (Z * Y * X,) + piece.shape),...  34.8 us
    all_to_all x1, blocking collectives, body(): lax.all_to_all(change, ('z', 'y'), 0, 1, tiled=True)  33.1 us
    ppermute x14, waiting for transfers between devices, swap(): return lax.ppermute(value, axis, [(i, i ^ bit) for i in range(size)])  28.2 us
    pallas_call x1, Pallas kernels, factor_begin(): pl.pallas_call(begin_kernel, in_specs=[ANY_SMEM, ANY_VMEM, ANY_VMEM, ANY_...  25.2 us
    pallas_call x1, Pallas kernels, factor_finish(): pl.pallas_call(finish_kernel, in_specs=[pl.BlockSpec(memory_space=pl.ANY)...  24.2 us
    ppermute x14, starting transfers between devices, swap(): return lax.ppermute(value, axis, [(i, i ^ bit) for i in range(size)])  17.2 us
    pallas_call x1, Pallas kernels, solve(): pl.pallas_call(solve_kernel, in_specs=[ANY_SMEM] + [ANY_VMEM] * 7, out_sp...  14.3 us
    ppermute x4, waiting for transfers between devices, onward(): high = lax.ppermute(high, axis, [(i, (i + 3) % 4) for i in range(4)])  11.3 us
  transfers between devices with their start and end apart: 23, of which 10 were waited for; matrix products, arithmetic and copies ran while one was open for 5% of the time, Pallas kernels for 27%

profile of v7, /device:TPU:0, one launch (start us, length us, event | category | flops | bytes accessed | tf_op | source)
XLA Modules:
  0.0 264.6 jit_solution(17558402126648270552)
XLA Ops:
  3.2 9.0 %forward.1.e0 = f32[72,2048]{1,0:T(8,128)} custom-call(f32[64,8192]{1,0:T(8,128)} %effect.1, f32[1,8192]{1,0:T(1,128)} %bitcast.30, f32[1,8192]{1,0:T(1,128)} %bitcast.31, f32[1,8192]{1,0:T(1,128)} %bitcast.32, f32[3,8192]{1,0:T(4,128)} %init.1, f32[6,8192]{1,0:T(8,128)} %fall.1, s32[4,2048]{1,0:T(4,128)} %bitcast.33, f32[4,2048]{1,0:T(4,128)} %bitcast.34, ...), custom_call_target="tpu_custom_call" | custom-call | flops 20000000000 | bytes 10000000 | tf_op jit(solution)/shard_map/forward/pallas_call | solution.py:96
  12.2 3.0 %collective-permute-done.n1 = f32[64,2048]{1,0:T(8,128)S(1)} collective-permute-done((f32[64,2048]{1,0:T(8,128)}, f32[64,2048]{1,0:T(8,128)S(1)}, u32[]{:S(2)}, u32[]{:S(2)}) %collective-permute-start) | collective-permute-done | bytes 524320 | tf_op jit(solution)/shard_map/ppermute | solution.py:450
  15.3 2.0 collective-permute-start.2
  17.2 2.2 collective-permute-start.3
  25.8 7.1 %collective-permute-done.2.p1 = f32[72,2048]{1,0:T(8,128)S(1)} collective-permute-done((f32[72,2048]{1,0:T(8,128)}, f32[72,2048]{1,0:T(8,128)S(1)}, u32[]{:S(2)}, u32[]{:S(2)}) %collective-permute-start.2) | collective-permute-done | bytes 589856 | tf_op jit(solution)/shard_map/ppermute | solution.py:450
  32.9 11.3 %collective-permute-done.3.p2 = f32[72,2048]{1,0:T(8,128)S(1)} collective-permute-done((f32[72,2048]{1,0:T(8,128)}, f32[72,2048]{1,0:T(8,128)S(1)}, u32[]{:S(2)}, u32[]{:S(2)}) %collective-permute-start.3) | collective-permute-done | bytes 589856 | tf_op jit(solution)/shard_map/ppermute | solution.py:451
  49.3 2.1 collective-permute-start.8
  53.4 5.6 %collective-permute-done.9.t2 = f32[8,2048]{1,0:T(8,128)S(1)} collective-permute-done((f32[8,2048]{1,0:T(8,128)S(1)}, f32[8,2048]{1,0:T(8,128)S(1)}, u32[]{:S(2)}, u32[]{:S(2)}) %collective-permute-start.9) | collective-permute-done | bytes 65568 | tf_op jit(solution)/shard_map/ppermute | solution.py:456
  60.5 8.7 %gram.1 = (f32[4,40,512]{2,1,0:T(8,128)}, f32[4,40,512]{2,1,0:T(8,128)}) custom-call(s32[4]{0:T(128)} %pad_add_fusion.where, f32[72,2048]{1,0:T(8,128)} %forward.1.e0, f32[104,2048]{1,0:T(8,128)} %copy-done.4, f32[104,2048]{1,0:T(8,128)} %copy-done.5, f32[40,2048]{1,0:T(8,128)} %copy-done.9, f32[40,2048]{1,0:T(8,128)} %copy-done.10, f32[8,2048]{1,0:T(8,128)} %copy-done.1, ...), custom_call_target="tpu_custom_call" | custom-call | flops 8000000000 | bytes 10000000 | tf_op jit(solution)/shard_map/gram/pallas_call | solution.py:173
  69.3 1.8 collective-permute-done.10
  73.8 2.7 %collective-permute-start.12 = (f32[40,512]{1,0:T(8,128)S(1)}, f32[40,512]{1,0:T(8,128)S(1)}, u32[]{:S(2)}, u32[]{:S(2)}) collective-permute-start(f32[40,512]{1,0:T(8,128)S(1)} %get-tuple-element.79), channel_id=1, source_target_pairs={{0,4},{2,6},{4,0},{6,2},{1,5},{3,7},{5,1},{7,3},{8,12},{10,14},{12... | collective-permute-start | bytes 245768 | tf_op jit(solution)/shard_map/ppermute | solution.py:456
  77.0 3.8 %collective-permute-done.12 = f32[40,512]{1,0:T(8,128)S(1)} collective-permute-done((f32[40,512]{1,0:T(8,128)S(1)}, f32[40,512]{1,0:T(8,128)S(1)}, u32[]{:S(2)}, u32[]{:S(2)}) %collective-permute-start.12) | collective-permute-done | bytes 81952 | tf_op jit(solution)/shard_map/ppermute | solution.py:456
  82.8 34.8 %all_to_all.29 = f32[64,32,256]{2,1,0:T(8,128)} all-to-all(f32[64,32,256]{2,1,0:T(8,128)S(1)} %broadcast_in_dim.32), channel_id=1, replica_groups=mesh['z'=4,'y'=4,'x'=4,'core'=2] {'z','y','x'}, dimensions={0} | all-to-all | bytes 4194304 | tf_op jit(solution)/shard_map/all_to_all | solution.py:443
  119.7 1.9 collective-permute-start.15
  121.7 2.5 collective-permute-start.16
  125.7 5.7 %all-to-all-start.1 = ((f32[64,32,256]{2,1,0:T(8,128)}), f32[64,32,256]{2,1,0:T(8,128)}, u32[]{:S(2)}, u32[]{:S(2)}) async-start(f32[64,32,256]{2,1,0:T(8,128)} %broadcast_in_dim.33), calls=%async_computation.1 | async-start | bytes 4194304 | tf_op jit(solution)/shard_map/all_to_all | solution.py:443
  131.5 25.2 %factor_begin.1 = (f32[1024,1024]{1,0:T(8,128)}, f32[512,256]{1,0:T(8,128)}) custom-call(s32[4]{0:T(128)} %pad_add_fusion.where, f32[2048,256]{1,0:T(8,128)} %bitcast.15.mine, f32[2048,256]{1,0:T(8,128)} %collective-permute-done.17.other, f32[8,128]{1,0:T(8,128)} %slice.69.misfit), custom_call_target="tpu_custom_call" | custom-call | flops 20000000000 | bytes 10000000 | tf_op jit(solution)/shard_map/factor_begin/pallas_call | solution.py:349
  156.7 10.3 %collective-permute-done.15 = f32[64,2048]{1,0:T(8,128)S(1)} collective-permute-done((f32[64,2048]{1,0:T(8,128)}, f32[64,2048]{1,0:T(8,128)S(1)}, u32[]{:S(2)}, u32[]{:S(2)}) %collective-permute-start.15) | collective-permute-done | bytes 524320 | tf_op jit(solution)/shard_map/ppermute | solution.py:456
  167.0 3.3 %collective-permute-done.16 = f32[64,2048]{1,0:T(8,128)} collective-permute-done((f32[64,2048]{1,0:T(8,128)}, f32[64,2048]{1,0:T(8,128)}, u32[]{:S(2)}, u32[]{:S(2)}) %collective-permute-start.16) | collective-permute-done | bytes 524320 | tf_op jit(solution)/shard_map/ppermute | solution.py:456
  171.5 1.9 constant_dynamic-slice_fusion
  178.5 24.2 %factor_finish.1 = (f32[1024,1024]{1,0:T(8,128)}, f32[512,256]{1,0:T(8,128)}) custom-call(f32[1024,1024]{1,0:T(8,128)} %get-tuple-element.47.before, f32[512,256]{1,0:T(8,128)} %get-tuple-element.48.earlier), custom_call_target="tpu_custom_call" | custom-call | flops 20000000000 | bytes 10000000 | tf_op jit(solution)/shard_map/factor_finish/pallas_call | solution.py:362
  204.9 14.3 %solve.1.work = f32[1024,512]{1,0:T(8,128)} custom-call(s32[4]{0:T(128)} %pad_add_fusion.where, f32[1024,1024]{1,0:T(8,128)} %get-tuple-element.51.system, f32[512,256]{1,0:T(8,128)} %get-tuple-element.48.earlier, f32[512,256]{1,0:T(8,128)} %get-tuple-element.52.later, f32[256,512]{1,0:T(8,128)} %pad_maximum_fusion.2.b0, ...), custom_call_target="tpu_custom_call" | custom-call | flops 5000000000 | bytes 10000000 | tf_op jit(solution)/shard_map/solve/pallas_call | solution.py:402
  219.2 10.5 %combine.1 = f32[1024,512]{1,0:T(8,128)} custom-call(s32[4]{0:T(128)} %pad_add_fusion.where, f32[2048,256]{1,0:T(8,128)} %bitcast.16.mine, f32[2048,256]{1,0:T(8,128)} %collective-permute-done.21.other, f32[1024,512]{1,0:T(8,128)} %solve.1.work, f32[8,128]{1,0:T(8,128)} %slice.69.misfit), custom_call_target="tpu_custom_call" | custom-call | flops 6000000000 | bytes 10000000 | tf_op jit(solution)/shard_map/combine/pallas_call | solution.py:431
  229.7 33.1 %all_to_all.30 = f32[16,64,512]{2,1,0:T(8,128)S(1)} all-to-all(f32[16,64,512]{2,1,0:T(8,128)} %bitcast.29), channel_id=1, replica_groups=mesh['z'=4,'y'=4,'x'=4,'core'=2] {'z','y'}, dimensions={0} | all-to-all | bytes 4194304 | tf_op jit(solution)/shard_map/all_to_all | solution.py:524
  (78 shorter events, 37.3 us)
Async XLA Ops:
  0.0 15.2 %collective-permute-start = (f32[64,2048]{1,0:T(8,128)}, f32[64,2048]{1,0:T(8,128)S(1)}, u32[]{:S(2)}, u32[]{:S(2)}) collective-permute-start(f32[64,2048]{1,0:T(8,128)} %n0.1), channel_id=1, source_target_pairs={{0,8},{8,16},{16,24},{24,0},{1,9},{9,17},{17,25},{25,1},{2,10},{10... | collective-permute-start | bytes 1572872 | tf_op jit(solution)/shard_map/ppermute | solution.py:450
  1.7 13.6 %collective-permute-start.1 = (f32[64,2048]{1,0:T(8,128)}, f32[64,2048]{1,0:T(8,128)S(1)}, u32[]{:S(2)}, u32[]{:S(2)}) collective-permute-start(f32[64,2048]{1,0:T(8,128)} %n0.1), channel_id=1, source_target_pairs={{0,24},{8,0},{16,8},{24,16},{1,25},{9,1},{17,9},{25,17},{2,26},{10... | collective-permute-start | bytes 1572872 | tf_op jit(solution)/shard_map/ppermute | solution.py:451
  15.3 17.6 %collective-permute-start.2 = (f32[72,2048]{1,0:T(8,128)}, f32[72,2048]{1,0:T(8,128)S(1)}, u32[]{:S(2)}, u32[]{:S(2)}) collective-permute-start(f32[72,2048]{1,0:T(8,128)} %forward.1.e0), channel_id=1, source_target_pairs={{0,32},{32,64},{64,96},{96,0},{1,33},{33,65},{65,97},{97,1},{2,34}... | collective-permute-start | bytes 1769480 | tf_op jit(solution)/shard_map/ppermute | solution.py:450
  17.2 27.0 %collective-permute-start.3 = (f32[72,2048]{1,0:T(8,128)}, f32[72,2048]{1,0:T(8,128)S(1)}, u32[]{:S(2)}, u32[]{:S(2)}) collective-permute-start(f32[72,2048]{1,0:T(8,128)} %forward.1.e0), channel_id=1, source_target_pairs={{0,96},{32,0},{64,32},{96,64},{1,97},{33,1},{65,33},{97,65},{2,98}... | collective-permute-start | bytes 1769480 | tf_op jit(solution)/shard_map/ppermute | solution.py:451
  19.4 26.5 %collective-permute-start.4 = (f32[72,2048]{1,0:T(8,128)}, f32[72,2048]{1,0:T(8,128)S(1)}, u32[]{:S(2)}, u32[]{:S(2)}) collective-permute-start(f32[72,2048]{1,0:T(8,128)} %forward.1.e0), channel_id=1, source_target_pairs={{0,64},{32,96},{64,0},{96,32},{1,65},{33,97},{65,1},{97,33},{2,66}... | collective-permute-start | bytes 1769480 | tf_op jit(solution)/shard_map/ppermute | solution.py:456
  22.5 24.3 %collective-permute-start.5 = (f32[104,2048]{1,0:T(8,128)S(1)}, f32[104,2048]{1,0:T(8,128)S(1)}, u32[]{:S(2)}, u32[]{:S(2)}) collective-permute-start(f32[104,2048]{1,0:T(8,128)S(1)} %get-tuple-element.62), channel_id=1, source_target_pairs={{0,8},{8,16},{16,24},{24,0},{1,9},{9,17},{17,25},{25,1},{2,10},{10... | collective-permute-start | bytes 2555912 | tf_op jit(solution)/shard_map/ppermute | solution.py:450
  24.1 22.7 %collective-permute-start.6 = (f32[104,2048]{1,0:T(8,128)S(1)}, f32[104,2048]{1,0:T(8,128)S(1)}, u32[]{:S(2)}, u32[]{:S(2)}) collective-permute-start(f32[104,2048]{1,0:T(8,128)S(1)} %get-tuple-element.61), channel_id=1, source_target_pairs={{0,24},{8,0},{16,8},{24,16},{1,25},{9,1},{17,9},{25,17},{2,26},{10... | collective-permute-start | bytes 2555912 | tf_op jit(solution)/shard_map/ppermute | solution.py:451
  48.1 10.9 %collective-permute-start.7 = (f32[40,2048]{1,0:T(8,128)S(1)}, f32[40,2048]{1,0:T(8,128)S(1)}, u32[]{:S(2)}, u32[]{:S(2)}) collective-permute-start(f32[40,2048]{1,0:T(8,128)S(1)} %get-tuple-element.85), channel_id=1, source_target_pairs={{0,8},{8,16},{16,24},{24,0},{1,9},{9,17},{17,25},{25,1},{2,10},{10... | collective-permute-start | bytes 983048 | tf_op jit(solution)/shard_map/ppermute | solution.py:450
  49.3 9.7 %collective-permute-start.8 = (f32[40,2048]{1,0:T(8,128)S(1)}, f32[40,2048]{1,0:T(8,128)S(1)}, u32[]{:S(2)}, u32[]{:S(2)}) collective-permute-start(f32[40,2048]{1,0:T(8,128)S(1)} %get-tuple-element.84), channel_id=1, source_target_pairs={{0,24},{8,0},{16,8},{24,16},{1,25},{9,1},{17,9},{25,17},{2,26},{10... | collective-permute-start | bytes 983048 | tf_op jit(solution)/shard_map/ppermute | solution.py:451
  51.4 7.6 %collective-permute-start.9 = (f32[8,2048]{1,0:T(8,128)S(1)}, f32[8,2048]{1,0:T(8,128)S(1)}, u32[]{:S(2)}, u32[]{:S(2)}) collective-permute-start(f32[8,2048]{1,0:T(8,128)S(1)} %slice_add_fusion.t0), channel_id=1, source_target_pairs={{0,16},{8,24},{16,0},{24,8},{1,17},{9,25},{17,1},{25,9},{2,18},{10... | collective-permute-start | bytes 196616 | tf_op jit(solution)/shard_map/ppermute | solution.py:456
  69.2 1.9 collective-permute-start.10
  72.2 4.8 %collective-permute-start.11 = (f32[40,512]{1,0:T(8,128)S(1)}, f32[40,512]{1,0:T(8,128)S(1)}, u32[]{:S(2)}, u32[]{:S(2)}) collective-permute-start(f32[40,512]{1,0:T(8,128)S(1)} %get-tuple-element.81), channel_id=1, source_target_pairs={{0,2},{2,0},{4,6},{6,4},{1,3},{3,1},{5,7},{7,5},{8,10},{10,8},{12,... | collective-permute-start | bytes 245768 | tf_op jit(solution)/shard_map/ppermute | solution.py:456
  73.8 7.0 %collective-permute-start.12 = (f32[40,512]{1,0:T(8,128)S(1)}, f32[40,512]{1,0:T(8,128)S(1)}, u32[]{:S(2)}, u32[]{:S(2)}) collective-permute-start(f32[40,512]{1,0:T(8,128)S(1)} %get-tuple-element.79), channel_id=1, source_target_pairs={{0,4},{2,6},{4,0},{6,2},{1,5},{3,7},{5,1},{7,3},{8,12},{10,14},{12... | collective-permute-start | bytes 245768 | tf_op jit(solution)/shard_map/ppermute | solution.py:456
  76.5 6.0 %collective-permute-start.13 = (f32[40,512]{1,0:T(8,128)S(1)}, f32[40,512]{1,0:T(8,128)S(1)}, u32[]{:S(2)}, u32[]{:S(2)}) collective-permute-start(f32[40,512]{1,0:T(8,128)S(1)} %get-tuple-element.80), channel_id=1, source_target_pairs={{0,6},{2,4},{4,2},{6,0},{1,7},{3,5},{5,3},{7,1},{8,14},{10,12},{12... | collective-permute-start | bytes 245768 | tf_op jit(solution)/shard_map/ppermute | solution.py:456
  82.8 35.4 %copy-start = (f32[64,8192]{1,0:T(8,128)S(1)}, f32[64,8192]{1,0:T(8,128)}, u32[]{:S(2)}) copy-start(f32[64,8192]{1,0:T(8,128)} %effect.1) | copy-start | bytes 6291460
  117.6 13.9 %collective-permute-start.17 = (f32[2048,256]{1,0:T(8,128)}, f32[2048,256]{1,0:T(8,128)}, u32[]{:S(2)}, u32[]{:S(2)}) collective-permute-start(f32[2048,256]{1,0:T(8,128)} %bitcast.15.mine), channel_id=1, source_target_pairs={{0,1},{1,0},{2,3},{3,2},{4,5},{5,4},{6,7},{7,6},{8,9},{9,8},{10,11... | collective-permute-start | bytes 6291464 | tf_op jit(solution)/shard_map/ppermute | solution.py:456
  119.4 37.2 %collective-permute-start.14 = (f32[64,2048]{1,0:T(8,128)}, f32[64,2048]{1,0:T(8,128)}, u32[]{:S(2)}, u32[]{:S(2)}) collective-permute-start(f32[64,2048]{1,0:T(8,128)} %get-tuple-element.59), channel_id=1, source_target_pairs={{0,32},{32,0},{64,96},{96,64},{1,33},{33,1},{65,97},{97,65},{2,34}... | collective-permute-start | bytes 1572872 | tf_op jit(solution)/shard_map/ppermute | solution.py:456
  119.7 47.3 %collective-permute-start.15 = (f32[64,2048]{1,0:T(8,128)}, f32[64,2048]{1,0:T(8,128)S(1)}, u32[]{:S(2)}, u32[]{:S(2)}) collective-permute-start(f32[64,2048]{1,0:T(8,128)} %get-tuple-element.58), channel_id=1, source_target_pairs={{0,64},{32,96},{64,0},{96,32},{1,65},{33,97},{65,1},{97,33},{2,66}... | collective-permute-start | bytes 1572872 | tf_op jit(solution)/shard_map/ppermute | solution.py:456
  121.7 48.7 %collective-permute-start.16 = (f32[64,2048]{1,0:T(8,128)}, f32[64,2048]{1,0:T(8,128)}, u32[]{:S(2)}, u32[]{:S(2)}) collective-permute-start(f32[64,2048]{1,0:T(8,128)} %get-tuple-element.57), channel_id=1, source_target_pairs={{0,96},{32,64},{64,32},{96,0},{1,97},{33,65},{65,33},{97,1},{2,98}... | collective-permute-start | bytes 1572872 | tf_op jit(solution)/shard_map/ppermute | solution.py:456
  125.7 78.8 %all-to-all-start.1 = ((f32[64,32,256]{2,1,0:T(8,128)}), f32[64,32,256]{2,1,0:T(8,128)}, u32[]{:S(2)}, u32[]{:S(2)}) async-start(f32[64,32,256]{2,1,0:T(8,128)} %broadcast_in_dim.33), calls=%async_computation.1 | async-start | bytes 4194304 | tf_op jit(solution)/shard_map/all_to_all | solution.py:443
  173.4 31.2 %collective-permute-start.20 = (f32[256,512]{1,0:T(8,128)S(1)}, f32[256,512]{1,0:T(8,128)}, u32[]{:S(2)}, u32[]{:S(2)}) collective-permute-start(f32[256,512]{1,0:T(8,128)S(1)} %pad_maximum_fusion.5), channel_id=1, source_target_pairs={{0,24},{8,16},{16,8},{24,0},{1,25},{9,17},{17,9},{25,1},{2,26},{10... | collective-permute-start | bytes 1572872 | tf_op jit(solution)/shard_map/ppermute | solution.py:456
  174.5 30.1 %collective-permute-start.19 = (f32[256,512]{1,0:T(8,128)S(1)}, f32[256,512]{1,0:T(8,128)}, u32[]{:S(2)}, u32[]{:S(2)}) collective-permute-start(f32[256,512]{1,0:T(8,128)S(1)} %pad_maximum_fusion.4), channel_id=1, source_target_pairs={{0,16},{8,24},{16,0},{24,8},{1,17},{9,25},{17,1},{25,9},{2,18},{10... | collective-permute-start | bytes 1572872 | tf_op jit(solution)/shard_map/ppermute | solution.py:456
  177.1 27.5 %collective-permute-start.18 = (f32[256,512]{1,0:T(8,128)}, f32[256,512]{1,0:T(8,128)}, u32[]{:S(2)}, u32[]{:S(2)}) collective-permute-start(f32[256,512]{1,0:T(8,128)} %pad_maximum_fusion.3), channel_id=1, source_target_pairs={{0,8},{8,0},{16,24},{24,16},{1,9},{9,1},{17,25},{25,17},{2,10},{10... | collective-permute-start | bytes 1572872 | tf_op jit(solution)/shard_map/ppermute | solution.py:456
  204.6 14.6 %collective-permute-start.21 = (f32[2048,256]{1,0:T(8,128)}, f32[2048,256]{1,0:T(8,128)}, u32[]{:S(2)}, u32[]{:S(2)}) collective-permute-start(f32[2048,256]{1,0:T(8,128)} %bitcast.16.mine), channel_id=1, source_target_pairs={{0,1},{1,0},{2,3},{3,2},{4,5},{5,4},{6,7},{7,6},{8,9},{9,8},{10,11... | collective-permute-start | bytes 6291464 | tf_op jit(solution)/shard_map/ppermute | solution.py:456
  (11 other events, 110.8 us)

commit v8 on v7

--- a/solution.py
+++ b/solution.py
@@ -501,14 +501,14 @@
     shared = part[0] + sum(swap(part[a], "x", X, a) for a in range(1, X))
     piece, right, misfit = shared[:32, :TILE], shared[:32, TILE:], shared[32:, :LANES]
     mine = collect(piece)
-    effect, right, mine = lax.optimization_barrier((turnover_effect, right, mine))
-    right = collect(right)
+    effect, mine = lax.optimization_barrier((turnover_effect, mine))
     other = swap(mine, "core", 2, 1)
     wide = cells // Z
     strip = [lax.dynamic_slice_in_dim(effect, (zid ^ b) * wide, wide, 1) for b in range(Z)]
     strip = [strip[0]] + [swap(strip[b], "z", Z, b) for b in range(1, Z)]
     system, inverse = factor_begin(where, mine, other, misfit)
-    strip, system = lax.optimization_barrier((strip, system))
+    strip, right, system = lax.optimization_barrier((strip, right, system))
+    right = collect(right)
     narrow = wide // Y
     cut = [
         jnp.concatenate(
@@ -518,8 +518,9 @@
     ]
     cut = [cut[0]] + [swap(cut[a], "y", Y, a) for a in range(1, Y)]
     system, later = factor_finish(system, inverse)
-    right, cut, system = lax.optimization_barrier((right, cut, system))
+    cut, system = lax.optimization_barrier((cut, system))
     work = solve(where, system, inverse, later, cut)
+    right, work = lax.optimization_barrier((right, work))
     change = combine(where, right, swap(right, "core", 2, 1), work, misfit)
     return turnover_effect + lax.all_to_all(change, ("z", "y"), 0, 1, tiled=True)
 

time: 265 us -> 263 us (level)
  transfers between devices with their start and end apart: 23 -> 23, of which waited for: 10 -> 11; matrix products, arithmetic and copies ran while one was open for 5% -> 3% of each run, Pallas kernels for 27% -> 28%
where the time goes in v8:
time: 263 us; the launch traced here: 262 us
  Pallas kernels  92 us (35%)
  blocking collectives  67.5 us (26%)
  waiting for transfers between devices  47.3 us (18%)
  starting transfers between devices  36.7 us (14%)
  local copies, waits for them, and re-layouts  10.2 us (4%)
  other arithmetic  8.11 us (3%)
    all_to_all x1, blocking collectives, collect(): lax.all_to_all(jnp.broadcast_to(piece[None], (Z * Y * X,) + piece.shape),...  34.8 us
    all_to_all x1, blocking collectives, body(): lax.all_to_all(change, ('z', 'y'), 0, 1, tiled=True)  32.8 us
    ppermute x14, waiting for transfers between devices, swap(): return lax.ppermute(value, axis, [(i, i ^ bit) for i in range(size)])  25.8 us
    pallas_call x1, Pallas kernels, factor_begin(): pl.pallas_call(begin_kernel, in_specs=[ANY_SMEM, ANY_VMEM, ANY_VMEM, ANY_...  25.2 us
    pallas_call x1, Pallas kernels, factor_finish(): pl.pallas_call(finish_kernel, in_specs=[pl.BlockSpec(memory_space=pl.ANY)...  24.4 us
    ppermute x14, starting transfers between devices, swap(): return lax.ppermute(value, axis, [(i, i ^ bit) for i in range(size)])  16.9 us
    pallas_call x1, Pallas kernels, solve(): pl.pallas_call(solve_kernel, in_specs=[ANY_SMEM] + [ANY_VMEM] * 7, out_sp...  14.3 us
    ppermute x4, waiting for transfers between devices, onward(): high = lax.ppermute(high, axis, [(i, (i + 3) % 4) for i in range(4)])  11.3 us
  transfers between devices with their start and end apart: 23, of which 11 were waited for; matrix products, arithmetic and copies ran while one was open for 3% of the time, Pallas kernels for 28%

profile of v8, /device:TPU:0, one launch (start us, length us, event | category | flops | bytes accessed | tf_op | source)
XLA Modules:
  0.0 262.1 jit_solution(15772067163530032419)
XLA Ops:
  3.2 8.9 %forward.1.e0 = f32[72,2048]{1,0:T(8,128)} custom-call(f32[64,8192]{1,0:T(8,128)} %effect.1, f32[1,8192]{1,0:T(1,128)} %bitcast.30, f32[1,8192]{1,0:T(1,128)} %bitcast.31, f32[1,8192]{1,0:T(1,128)} %bitcast.32, f32[3,8192]{1,0:T(4,128)} %init.1, f32[6,8192]{1,0:T(8,128)} %fall.1, s32[4,2048]{1,0:T(4,128)} %bitcast.33, f32[4,2048]{1,0:T(4,128)} %bitcast.34, ...), custom_call_target="tpu_custom_call" | custom-call | flops 20000000000 | bytes 10000000 | tf_op jit(solution)/shard_map/forward/pallas_call | solution.py:96
  12.2 3.1 %collective-permute-done.n1 = f32[64,2048]{1,0:T(8,128)S(1)} collective-permute-done((f32[64,2048]{1,0:T(8,128)}, f32[64,2048]{1,0:T(8,128)S(1)}, u32[]{:S(2)}, u32[]{:S(2)}) %collective-permute-start) | collective-permute-done | bytes 524320 | tf_op jit(solution)/shard_map/ppermute | solution.py:450
  15.3 2.0 collective-permute-start.2
  17.2 2.2 collective-permute-start.3
  25.8 7.1 %collective-permute-done.2.p1 = f32[72,2048]{1,0:T(8,128)S(1)} collective-permute-done((f32[72,2048]{1,0:T(8,128)}, f32[72,2048]{1,0:T(8,128)S(1)}, u32[]{:S(2)}, u32[]{:S(2)}) %collective-permute-start.2) | collective-permute-done | bytes 589856 | tf_op jit(solution)/shard_map/ppermute | solution.py:450
  32.9 11.3 %collective-permute-done.3.p2 = f32[72,2048]{1,0:T(8,128)S(1)} collective-permute-done((f32[72,2048]{1,0:T(8,128)}, f32[72,2048]{1,0:T(8,128)S(1)}, u32[]{:S(2)}, u32[]{:S(2)}) %collective-permute-start.3) | collective-permute-done | bytes 589856 | tf_op jit(solution)/shard_map/ppermute | solution.py:451
  49.3 2.1 collective-permute-start.8
  53.4 5.6 %collective-permute-done.9.t2 = f32[8,2048]{1,0:T(8,128)S(1)} collective-permute-done((f32[8,2048]{1,0:T(8,128)S(1)}, f32[8,2048]{1,0:T(8,128)S(1)}, u32[]{:S(2)}, u32[]{:S(2)}) %collective-permute-start.9) | collective-permute-done | bytes 65568 | tf_op jit(solution)/shard_map/ppermute | solution.py:456
  60.5 8.7 %gram.1 = (f32[4,40,512]{2,1,0:T(8,128)}, f32[4,40,512]{2,1,0:T(8,128)}) custom-call(s32[4]{0:T(128)} %pad_add_fusion.where, f32[72,2048]{1,0:T(8,128)} %forward.1.e0, f32[104,2048]{1,0:T(8,128)} %copy-done.5, f32[104,2048]{1,0:T(8,128)} %copy-done.6, f32[40,2048]{1,0:T(8,128)} %copy-done.10, f32[40,2048]{1,0:T(8,128)} %copy-done.11, f32[8,2048]{1,0:T(8,128)} %copy-done.1, ...), custom_call_target="tpu_custom_call" | custom-call | flops 8000000000 | bytes 10000000 | tf_op jit(solution)/shard_map/gram/pallas_call | solution.py:173
  73.8 2.7 %collective-permute-start.12 = (f32[40,512]{1,0:T(8,128)S(1)}, f32[40,512]{1,0:T(8,128)S(1)}, u32[]{:S(2)}, u32[]{:S(2)}) collective-permute-start(f32[40,512]{1,0:T(8,128)S(1)} %get-tuple-element.81), channel_id=1, source_target_pairs={{0,4},{2,6},{4,0},{6,2},{1,5},{3,7},{5,1},{7,3},{8,12},{10,14},{12... | collective-permute-start | bytes 245768 | tf_op jit(solution)/shard_map/ppermute | solution.py:456
  77.0 3.8 %collective-permute-done.12 = f32[40,512]{1,0:T(8,128)S(1)} collective-permute-done((f32[40,512]{1,0:T(8,128)S(1)}, f32[40,512]{1,0:T(8,128)S(1)}, u32[]{:S(2)}, u32[]{:S(2)}) %collective-permute-start.12) | collective-permute-done | bytes 81952 | tf_op jit(solution)/shard_map/ppermute | solution.py:456
  83.4 34.8 %all_to_all.29 = f32[64,32,256]{2,1,0:T(8,128)} all-to-all(f32[64,32,256]{2,1,0:T(8,128)S(1)} %broadcast_in_dim.32), channel_id=1, replica_groups=mesh['z'=4,'y'=4,'x'=4,'core'=2] {'z','y','x'}, dimensions={0} | all-to-all | bytes 4194304 | tf_op jit(solution)/shard_map/all_to_all | solution.py:443
  120.2 1.9 collective-permute-start.15
  122.2 2.5 collective-permute-start.16
  124.6 25.2 %factor_begin.1 = (f32[1024,1024]{1,0:T(8,128)}, f32[512,256]{1,0:T(8,128)}) custom-call(s32[4]{0:T(128)} %pad_add_fusion.where, f32[2048,256]{1,0:T(8,128)} %bitcast.15.mine, f32[2048,256]{1,0:T(8,128)} %collective-permute-done.17.other, f32[8,128]{1,0:T(8,128)} %slice.69.misfit), custom_call_target="tpu_custom_call" | custom-call | flops 20000000000 | bytes 10000000 | tf_op jit(solution)/shard_map/factor_begin/pallas_call | solution.py:349
  151.1 1.9 constant_dynamic-slice_fusion
  153.6 2.3 collective-permute-start.19
  159.7 5.8 %all-to-all-start.1 = ((f32[64,32,256]{2,1,0:T(8,128)}), f32[64,32,256]{2,1,0:T(8,128)}, u32[]{:S(2)}, u32[]{:S(2)}) async-start(f32[64,32,256]{2,1,0:T(8,128)} %broadcast_in_dim.33), calls=%async_computation.1 | async-start | bytes 4194304 | tf_op jit(solution)/shard_map/all_to_all | solution.py:443
  165.5 24.4 %factor_finish.1 = (f32[1024,1024]{1,0:T(8,128)}, f32[512,256]{1,0:T(8,128)}) custom-call(f32[1024,1024]{1,0:T(8,128)} %get-tuple-element.48.before, f32[512,256]{1,0:T(8,128)} %get-tuple-element.49.earlier), custom_call_target="tpu_custom_call" | custom-call | flops 20000000000 | bytes 10000000 | tf_op jit(solution)/shard_map/factor_finish/pallas_call | solution.py:362
  191.6 5.4 %collective-permute-done.20.b3 = f32[256,512]{1,0:T(8,128)} collective-permute-done((f32[256,512]{1,0:T(8,128)S(1)}, f32[256,512]{1,0:T(8,128)}, u32[]{:S(2)}, u32[]{:S(2)}) %collective-permute-start.20) | collective-permute-done | bytes 524320 | tf_op jit(solution)/shard_map/ppermute | solution.py:456
  198.3 14.3 %solve.1.work = f32[1024,512]{1,0:T(8,128)} custom-call(s32[4]{0:T(128)} %pad_add_fusion.where, f32[1024,1024]{1,0:T(8,128)} %get-tuple-element.51.system, f32[512,256]{1,0:T(8,128)} %get-tuple-element.49.earlier, f32[512,256]{1,0:T(8,128)} %get-tuple-element.52.later, f32[256,512]{1,0:T(8,128)} %pad_maximum_fusion.2.b0, ...), custom_call_target="tpu_custom_call" | custom-call | flops 5000000000 | bytes 10000000 | tf_op jit(solution)/shard_map/solve/pallas_call | solution.py:402
  212.6 4.5 %collective-permute-done.21.other = f32[2048,256]{1,0:T(8,128)} collective-permute-done((f32[2048,256]{1,0:T(8,128)}, f32[2048,256]{1,0:T(8,128)}, u32[]{:S(2)}, u32[]{:S(2)}) %collective-permute-start.21) | collective-permute-done | bytes 2097184 | tf_op jit(solution)/shard_map/ppermute | solution.py:456
  217.1 10.4 %combine.1 = f32[1024,512]{1,0:T(8,128)} custom-call(s32[4]{0:T(128)} %pad_add_fusion.where, f32[2048,256]{1,0:T(8,128)} %bitcast.16.mine, f32[2048,256]{1,0:T(8,128)} %collective-permute-done.21.other, f32[1024,512]{1,0:T(8,128)} %solve.1.work, f32[8,128]{1,0:T(8,128)} %slice.69.misfit), custom_call_target="tpu_custom_call" | custom-call | flops 6000000000 | bytes 10000000 | tf_op jit(solution)/shard_map/combine/pallas_call | solution.py:431
  227.6 32.8 %all_to_all.30 = f32[16,64,512]{2,1,0:T(8,128)S(1)} all-to-all(f32[16,64,512]{2,1,0:T(8,128)} %bitcast.29), channel_id=1, replica_groups=mesh['z'=4,'y'=4,'x'=4,'core'=2] {'z','y'}, dimensions={0} | all-to-all | bytes 4194304 | tf_op jit(solution)/shard_map/all_to_all | solution.py:525
  (80 shorter events, 38.2 us)
Async XLA Ops:
  0.0 15.2 %collective-permute-start = (f32[64,2048]{1,0:T(8,128)}, f32[64,2048]{1,0:T(8,128)S(1)}, u32[]{:S(2)}, u32[]{:S(2)}) collective-permute-start(f32[64,2048]{1,0:T(8,128)} %n0.1), channel_id=1, source_target_pairs={{0,8},{8,16},{16,24},{24,0},{1,9},{9,17},{17,25},{25,1},{2,10},{10... | collective-permute-start | bytes 1572872 | tf_op jit(solution)/shard_map/ppermute | solution.py:450
  1.7 13.6 %collective-permute-start.1 = (f32[64,2048]{1,0:T(8,128)}, f32[64,2048]{1,0:T(8,128)S(1)}, u32[]{:S(2)}, u32[]{:S(2)}) collective-permute-start(f32[64,2048]{1,0:T(8,128)} %n0.1), channel_id=1, source_target_pairs={{0,24},{8,0},{16,8},{24,16},{1,25},{9,1},{17,9},{25,17},{2,26},{10... | collective-permute-start | bytes 1572872 | tf_op jit(solution)/shard_map/ppermute | solution.py:451
  15.3 17.6 %collective-permute-start.2 = (f32[72,2048]{1,0:T(8,128)}, f32[72,2048]{1,0:T(8,128)S(1)}, u32[]{:S(2)}, u32[]{:S(2)}) collective-permute-start(f32[72,2048]{1,0:T(8,128)} %forward.1.e0), channel_id=1, source_target_pairs={{0,32},{32,64},{64,96},{96,0},{1,33},{33,65},{65,97},{97,1},{2,34}... | collective-permute-start | bytes 1769480 | tf_op jit(solution)/shard_map/ppermute | solution.py:450
  17.2 27.0 %collective-permute-start.3 = (f32[72,2048]{1,0:T(8,128)}, f32[72,2048]{1,0:T(8,128)S(1)}, u32[]{:S(2)}, u32[]{:S(2)}) collective-permute-start(f32[72,2048]{1,0:T(8,128)} %forward.1.e0), channel_id=1, source_target_pairs={{0,96},{32,0},{64,32},{96,64},{1,97},{33,1},{65,33},{97,65},{2,98}... | collective-permute-start | bytes 1769480 | tf_op jit(solution)/shard_map/ppermute | solution.py:451
  19.4 26.5 %collective-permute-start.4 = (f32[72,2048]{1,0:T(8,128)}, f32[72,2048]{1,0:T(8,128)S(1)}, u32[]{:S(2)}, u32[]{:S(2)}) collective-permute-start(f32[72,2048]{1,0:T(8,128)} %forward.1.e0), channel_id=1, source_target_pairs={{0,64},{32,96},{64,0},{96,32},{1,65},{33,97},{65,1},{97,33},{2,66}... | collective-permute-start | bytes 1769480 | tf_op jit(solution)/shard_map/ppermute | solution.py:456
  22.5 24.3 %collective-permute-start.5 = (f32[104,2048]{1,0:T(8,128)S(1)}, f32[104,2048]{1,0:T(8,128)S(1)}, u32[]{:S(2)}, u32[]{:S(2)}) collective-permute-start(f32[104,2048]{1,0:T(8,128)S(1)} %get-tuple-element.64), channel_id=1, source_target_pairs={{0,8},{8,16},{16,24},{24,0},{1,9},{9,17},{17,25},{25,1},{2,10},{10... | collective-permute-start | bytes 2555912 | tf_op jit(solution)/shard_map/ppermute | solution.py:450
  24.1 22.7 %collective-permute-start.6 = (f32[104,2048]{1,0:T(8,128)S(1)}, f32[104,2048]{1,0:T(8,128)S(1)}, u32[]{:S(2)}, u32[]{:S(2)}) collective-permute-start(f32[104,2048]{1,0:T(8,128)S(1)} %get-tuple-element.63), channel_id=1, source_target_pairs={{0,24},{8,0},{16,8},{24,16},{1,25},{9,1},{17,9},{25,17},{2,26},{10... | collective-permute-start | bytes 2555912 | tf_op jit(solution)/shard_map/ppermute | solution.py:451
  48.1 10.9 %collective-permute-start.7 = (f32[40,2048]{1,0:T(8,128)S(1)}, f32[40,2048]{1,0:T(8,128)S(1)}, u32[]{:S(2)}, u32[]{:S(2)}) collective-permute-start(f32[40,2048]{1,0:T(8,128)S(1)} %get-tuple-element.87), channel_id=1, source_target_pairs={{0,8},{8,16},{16,24},{24,0},{1,9},{9,17},{17,25},{25,1},{2,10},{10... | collective-permute-start | bytes 983048 | tf_op jit(solution)/shard_map/ppermute | solution.py:450
  49.3 9.7 %collective-permute-start.8 = (f32[40,2048]{1,0:T(8,128)S(1)}, f32[40,2048]{1,0:T(8,128)S(1)}, u32[]{:S(2)}, u32[]{:S(2)}) collective-permute-start(f32[40,2048]{1,0:T(8,128)S(1)} %get-tuple-element.86), channel_id=1, source_target_pairs={{0,24},{8,0},{16,8},{24,16},{1,25},{9,1},{17,9},{25,17},{2,26},{10... | collective-permute-start | bytes 983048 | tf_op jit(solution)/shard_map/ppermute | solution.py:451
  51.5 7.6 %collective-permute-start.9 = (f32[8,2048]{1,0:T(8,128)S(1)}, f32[8,2048]{1,0:T(8,128)S(1)}, u32[]{:S(2)}, u32[]{:S(2)}) collective-permute-start(f32[8,2048]{1,0:T(8,128)S(1)} %slice_add_fusion.t0), channel_id=1, source_target_pairs={{0,16},{8,24},{16,0},{24,8},{1,17},{9,25},{17,1},{25,9},{2,18},{10... | collective-permute-start | bytes 196616 | tf_op jit(solution)/shard_map/ppermute | solution.py:456
  69.3 1.9 collective-permute-start.10
  72.2 4.8 %collective-permute-start.11 = (f32[40,512]{1,0:T(8,128)S(1)}, f32[40,512]{1,0:T(8,128)S(1)}, u32[]{:S(2)}, u32[]{:S(2)}) collective-permute-start(f32[40,512]{1,0:T(8,128)S(1)} %get-tuple-element.83), channel_id=1, source_target_pairs={{0,2},{2,0},{4,6},{6,4},{1,3},{3,1},{5,7},{7,5},{8,10},{10,8},{12,... | collective-permute-start | bytes 245768 | tf_op jit(solution)/shard_map/ppermute | solution.py:456
  73.8 7.0 %collective-permute-start.12 = (f32[40,512]{1,0:T(8,128)S(1)}, f32[40,512]{1,0:T(8,128)S(1)}, u32[]{:S(2)}, u32[]{:S(2)}) collective-permute-start(f32[40,512]{1,0:T(8,128)S(1)} %get-tuple-element.81), channel_id=1, source_target_pairs={{0,4},{2,6},{4,0},{6,2},{1,5},{3,7},{5,1},{7,3},{8,12},{10,14},{12... | collective-permute-start | bytes 245768 | tf_op jit(solution)/shard_map/ppermute | solution.py:456
  76.5 6.0 %collective-permute-start.13 = (f32[40,512]{1,0:T(8,128)S(1)}, f32[40,512]{1,0:T(8,128)S(1)}, u32[]{:S(2)}, u32[]{:S(2)}) collective-permute-start(f32[40,512]{1,0:T(8,128)S(1)} %get-tuple-element.82), channel_id=1, source_target_pairs={{0,6},{2,4},{4,2},{6,0},{1,7},{3,5},{5,3},{7,1},{8,14},{10,12},{12... | collective-permute-start | bytes 245768 | tf_op jit(solution)/shard_map/ppermute | solution.py:456
  83.4 35.4 %copy-start = (f32[64,8192]{1,0:T(8,128)S(1)}, f32[64,8192]{1,0:T(8,128)}, u32[]{:S(2)}) copy-start(f32[64,8192]{1,0:T(8,128)} %effect.1) | copy-start | bytes 6291460
  118.2 6.5 %collective-permute-start.17 = (f32[2048,256]{1,0:T(8,128)}, f32[2048,256]{1,0:T(8,128)}, u32[]{:S(2)}, u32[]{:S(2)}) collective-permute-start(f32[2048,256]{1,0:T(8,128)} %bitcast.15.mine), channel_id=1, source_target_pairs={{0,1},{1,0},{2,3},{3,2},{4,5},{5,4},{6,7},{7,6},{8,9},{9,8},{10,11... | collective-permute-start | bytes 6291464 | tf_op jit(solution)/shard_map/ppermute | solution.py:456
  119.9 29.9 %collective-permute-start.14 = (f32[64,2048]{1,0:T(8,128)}, f32[64,2048]{1,0:T(8,128)}, u32[]{:S(2)}, u32[]{:S(2)}) collective-permute-start(f32[64,2048]{1,0:T(8,128)} %get-tuple-element.61), channel_id=1, source_target_pairs={{0,32},{32,0},{64,96},{96,64},{1,33},{33,1},{65,97},{97,65},{2,34}... | collective-permute-start | bytes 1572872 | tf_op jit(solution)/shard_map/ppermute | solution.py:456
  120.2 29.6 %collective-permute-start.15 = (f32[64,2048]{1,0:T(8,128)}, f32[64,2048]{1,0:T(8,128)S(1)}, u32[]{:S(2)}, u32[]{:S(2)}) collective-permute-start(f32[64,2048]{1,0:T(8,128)} %get-tuple-element.60), channel_id=1, source_target_pairs={{0,64},{32,96},{64,0},{96,32},{1,65},{33,97},{65,1},{97,33},{2,66}... | collective-permute-start | bytes 1572872 | tf_op jit(solution)/shard_map/ppermute | solution.py:456
  122.2 27.7 %collective-permute-start.16 = (f32[64,2048]{1,0:T(8,128)}, f32[64,2048]{1,0:T(8,128)}, u32[]{:S(2)}, u32[]{:S(2)}) collective-permute-start(f32[64,2048]{1,0:T(8,128)} %get-tuple-element.59), channel_id=1, source_target_pairs={{0,96},{32,64},{64,32},{96,0},{1,97},{33,65},{65,33},{97,1},{2,98}... | collective-permute-start | bytes 1572872 | tf_op jit(solution)/shard_map/ppermute | solution.py:456
  153.0 44.1 %collective-permute-start.20 = (f32[256,512]{1,0:T(8,128)S(1)}, f32[256,512]{1,0:T(8,128)}, u32[]{:S(2)}, u32[]{:S(2)}) collective-permute-start(f32[256,512]{1,0:T(8,128)S(1)} %pad_maximum_fusion.5), channel_id=1, source_target_pairs={{0,24},{8,16},{16,8},{24,0},{1,25},{9,17},{17,9},{25,1},{2,26},{10... | collective-permute-start | bytes 1572872 | tf_op jit(solution)/shard_map/ppermute | solution.py:456
  153.6 43.5 %collective-permute-start.19 = (f32[256,512]{1,0:T(8,128)S(1)}, f32[256,512]{1,0:T(8,128)}, u32[]{:S(2)}, u32[]{:S(2)}) collective-permute-start(f32[256,512]{1,0:T(8,128)S(1)} %pad_maximum_fusion.4), channel_id=1, source_target_pairs={{0,16},{8,24},{16,0},{24,8},{1,17},{9,25},{17,1},{25,9},{2,18},{10... | collective-permute-start | bytes 1572872 | tf_op jit(solution)/shard_map/ppermute | solution.py:456
  156.7 41.6 %collective-permute-start.18 = (f32[256,512]{1,0:T(8,128)}, f32[256,512]{1,0:T(8,128)}, u32[]{:S(2)}, u32[]{:S(2)}) collective-permute-start(f32[256,512]{1,0:T(8,128)} %pad_maximum_fusion.3), channel_id=1, source_target_pairs={{0,8},{8,0},{16,24},{24,16},{1,9},{9,1},{17,25},{25,17},{2,10},{10... | collective-permute-start | bytes 1572872 | tf_op jit(solution)/shard_map/ppermute | solution.py:456
  159.7 53.0 %all-to-all-start.1 = ((f32[64,32,256]{2,1,0:T(8,128)}), f32[64,32,256]{2,1,0:T(8,128)}, u32[]{:S(2)}, u32[]{:S(2)}) async-start(f32[64,32,256]{2,1,0:T(8,128)} %broadcast_in_dim.33), calls=%async_computation.1 | async-start | bytes 4194304 | tf_op jit(solution)/shard_map/all_to_all | solution.py:443
  212.6 4.5 %collective-permute-start.21 = (f32[2048,256]{1,0:T(8,128)}, f32[2048,256]{1,0:T(8,128)}, u32[]{:S(2)}, u32[]{:S(2)}) collective-permute-start(f32[2048,256]{1,0:T(8,128)} %bitcast.16.mine), channel_id=1, source_target_pairs={{0,1},{1,0},{2,3},{3,2},{4,5},{5,4},{6,7},{7,6},{8,9},{9,8},{10,11... | collective-permute-start | bytes 6291464 | tf_op jit(solution)/shard_map/ppermute | solution.py:456
  (12 other events, 116.1 us)

commit v9 on v6

--- a/solution.py
+++ b/solution.py
@@ -353,6 +353,7 @@
         out_shape=[jax.ShapeDtypeStruct((n, n), f32), jax.ShapeDtypeStruct((2 * TILE, TILE), f32)],
         scratch_shapes=FACTOR_SCRATCH,
         cost_estimate=cost(2e10),
+        compiler_params=pltpu.CompilerParams(vmem_limit_bytes=24 << 20),
         name="factor_begin",
     )(where, mine, other, misfit)
 
@@ -366,6 +367,7 @@
         out_shape=[jax.ShapeDtypeStruct((n, n), f32), jax.ShapeDtypeStruct((2 * TILE, TILE), f32)],
         scratch_shapes=FACTOR_SCRATCH + [pltpu.SemaphoreType.DMA],
         cost_estimate=cost(2e10),
+        compiler_params=pltpu.CompilerParams(vmem_limit_bytes=24 << 20),
         name="factor_finish",
     )(system, earlier)
 
@@ -385,13 +387,9 @@
         at = slice(k * TILE, (k + 1) * TILE)
         source = earlier if k < 2 else later
         work[at, :] = mm(source[(k % 2) * TILE : (k % 2 + 1) * TILE, :], work[at, :])
-
-        def down(i, _, at=at):
-            low = pl.ds(pl.multiple_of(i * TILE, TILE), TILE)
-            work[low, :] = work[low, :] - mm(system[low, at], work[at, :])
-            return 0
-
-        lax.fori_loop(k + 1, tiles, down, 0)
+        for i in range(k + 1, tiles):
+            down = slice(i * TILE, (i + 1) * TILE)
+            work[down, :] = work[down, :] - mm(system[down, at], work[at, :])
     for k in range(tiles - 2, -1, -1):
         at = slice(k * TILE, (k + 1) * TILE)
         rest = slice((k + 1) * TILE, n)
@@ -405,6 +403,7 @@
         out_specs=ANY_VMEM,
         out_shape=jax.ShapeDtypeStruct((system.shape[0], blocks[0].shape[1]), f32),
         cost_estimate=cost(5e9),
+        compiler_params=pltpu.CompilerParams(vmem_limit_bytes=24 << 20),
         name="solve",
     )(where, system, earlier, later, *blocks)
 

time: 259 us -> 249 us (0.961)
  Pallas kernels: 92 us -> 80.1 us
  waiting for transfers between devices: 66.9 us -> 75.1 us
    ppermute x13, waiting for transfers between devices: 15.6 us -> 23.6 us  [swap(): return lax.ppermute(value, axis, [(i, i ^ bit) for i in range(size)])]
    pallas_call x1, Pallas kernels: 24.3 us -> 19.6 us  [factor_finish(): pl.pallas_call(finish_kernel, in_specs=[pl.BlockSpec(memory_space=pl.ANY)...]
    pallas_call x1, Pallas kernels: 14.3 us -> 9.63 us  [solve(): pl.pallas_call(solve_kernel, in_specs=[ANY_SMEM] + [ANY_VMEM] * 7, out_sp...]
    dynamic_slice x2, local copies, waits for them, and re-layouts: 3.06 us -> 0.18 us  [body(): lax.dynamic_slice_in_dim(part, (yid ^ a) * narrow, narrow, 1)]
  transfers between devices with their start and end apart: 23 -> 23, of which waited for: 11 -> 12; matrix products, arithmetic and copies ran while one was open for 4% -> 2% of each run, Pallas kernels for 28% -> 25%
where the time goes in v9:
time: 249 us; the launch traced here: 248 us
  Pallas kernels  80.1 us (32%)
  waiting for transfers between devices  75.1 us (30%)
  starting transfers between devices  36 us (14%)
  blocking collectives  29.1 us (12%)
  between operations  13.7 us (6%)
  local copies, waits for them, and re-layouts  8.52 us (3%)
  other arithmetic  5.6 us (2%)
    all_to_all x1, waiting for transfers between devices, body(): lax.all_to_all(jnp.broadcast_to(piece[None], (Z * Y * X, 32, TILE)), ('z'...  29.4 us
    all_to_all x1, blocking collectives, body(): lax.all_to_all(change, ('z', 'y'), 0, 1, tiled=True)  29.1 us
    ppermute x13, waiting for transfers between devices, swap(): return lax.ppermute(value, axis, [(i, i ^ bit) for i in range(size)])  23.6 us
    pallas_call x1, Pallas kernels, factor_begin(): pl.pallas_call(begin_kernel, in_specs=[ANY_SMEM, ANY_VMEM, ANY_VMEM, ANY_...  22.8 us
    pallas_call x1, Pallas kernels, factor_finish(): pl.pallas_call(finish_kernel, in_specs=[pl.BlockSpec(memory_space=pl.ANY)...  19.6 us
    ppermute x13, starting transfers between devices, swap(): return lax.ppermute(value, axis, [(i, i ^ bit) for i in range(size)])  17.1 us
    ppermute x4, waiting for transfers between devices, onward(): high = lax.ppermute(high, axis, [(i, (i + 3) % 4) for i in range(4)])  11.3 us
    pallas_call x1, Pallas kernels, combine(): pl.pallas_call(combine_kernel, grid=(Z,), in_specs=[pl.BlockSpec((Y * TIL...  10.4 us
  transfers between devices with their start and end apart: 23, of which 12 were waited for; matrix products, arithmetic and copies ran while one was open for 2% of the time, Pallas kernels for 25%

profile of v9, /device:TPU:0, one launch (start us, length us, event | category | flops | bytes accessed | tf_op | source)
XLA Modules:
  0.0 248.2 jit_solution(17424839294598076161)
XLA Ops:
  9.8 8.9 %forward.1.e0 = f32[72,2048]{1,0:T(8,128)} custom-call(f32[64,8192]{1,0:T(8,128)} %effect.1, f32[1,8192]{1,0:T(1,128)} %bitcast.31, f32[1,8192]{1,0:T(1,128)} %bitcast.32, f32[1,8192]{1,0:T(1,128)} %bitcast.33, f32[3,8192]{1,0:T(4,128)} %init.1, f32[6,8192]{1,0:T(8,128)} %fall.1, s32[4,2048]{1,0:T(4,128)} %bitcast.34, f32[4,2048]{1,0:T(4,128)} %bitcast.35, ...), custom_call_target="tpu_custom_call" | custom-call | flops 20000000000 | bytes 10000000 | tf_op jit(solution)/shard_map/forward/pallas_call | solution.py:96
  18.7 3.1 %collective-permute-done.n1 = f32[64,2048]{1,0:T(8,128)S(1)} collective-permute-done((f32[64,2048]{1,0:T(8,128)}, f32[64,2048]{1,0:T(8,128)S(1)}, u32[]{:S(2)}, u32[]{:S(2)}) %collective-permute-start) | collective-permute-done | bytes 524320 | tf_op jit(solution)/shard_map/ppermute | solution.py:435
  21.8 2.0 collective-permute-start.2
  23.8 2.2 collective-permute-start.3
  32.4 7.0 %collective-permute-done.2.p1 = f32[72,2048]{1,0:T(8,128)S(1)} collective-permute-done((f32[72,2048]{1,0:T(8,128)}, f32[72,2048]{1,0:T(8,128)S(1)}, u32[]{:S(2)}, u32[]{:S(2)}) %collective-permute-start.2) | collective-permute-done | bytes 589856 | tf_op jit(solution)/shard_map/ppermute | solution.py:435
  39.4 11.3 %collective-permute-done.3.p2 = f32[72,2048]{1,0:T(8,128)S(1)} collective-permute-done((f32[72,2048]{1,0:T(8,128)}, f32[72,2048]{1,0:T(8,128)S(1)}, u32[]{:S(2)}, u32[]{:S(2)}) %collective-permute-start.3) | collective-permute-done | bytes 589856 | tf_op jit(solution)/shard_map/ppermute | solution.py:436
  54.7 2.1 collective-permute-start.8
  58.8 5.6 %collective-permute-done.9.t2 = f32[8,2048]{1,0:T(8,128)S(1)} collective-permute-done((f32[8,2048]{1,0:T(8,128)S(1)}, f32[8,2048]{1,0:T(8,128)S(1)}, u32[]{:S(2)}, u32[]{:S(2)}) %collective-permute-start.9) | collective-permute-done | bytes 65568 | tf_op jit(solution)/shard_map/ppermute | solution.py:441
  65.9 8.7 %gram.1 = (f32[4,40,512]{2,1,0:T(8,128)}, f32[4,40,512]{2,1,0:T(8,128)}) custom-call(s32[4]{0:T(128)} %pad_add_fusion.where, f32[72,2048]{1,0:T(8,128)} %forward.1.e0, f32[104,2048]{1,0:T(8,128)} %copy-done.7, f32[104,2048]{1,0:T(8,128)} %copy-done.8, f32[40,2048]{1,0:T(8,128)} %copy-done.12, f32[40,2048]{1,0:T(8,128)} %copy-done.13, f32[8,2048]{1,0:T(8,128)} %copy-done.4, ...), custom_call_target="tpu_custom_call" | custom-call | flops 8000000000 | bytes 10000000 | tf_op jit(solution)/shard_map/gram/pallas_call | solution.py:173
  79.2 2.7 %collective-permute-start.12 = (f32[40,512]{1,0:T(8,128)S(1)}, f32[40,512]{1,0:T(8,128)S(1)}, u32[]{:S(2)}, u32[]{:S(2)}) collective-permute-start(f32[40,512]{1,0:T(8,128)S(1)} %get-tuple-element.65), channel_id=1, source_target_pairs={{0,4},{2,6},{4,0},{6,2},{1,5},{3,7},{5,1},{7,3},{8,12},{10,14},{12... | collective-permute-start | bytes 245768 | tf_op jit(solution)/shard_map/ppermute | solution.py:441
  82.4 3.8 %collective-permute-done.12 = f32[40,512]{1,0:T(8,128)S(1)} collective-permute-done((f32[40,512]{1,0:T(8,128)S(1)}, f32[40,512]{1,0:T(8,128)S(1)}, u32[]{:S(2)}, u32[]{:S(2)}) %collective-permute-start.12) | collective-permute-done | bytes 81952 | tf_op jit(solution)/shard_map/ppermute | solution.py:441
  90.1 4.8 %all-to-all-start = ((f32[64,32,256]{2,1,0:T(8,128)}), f32[64,32,256]{2,1,0:T(8,128)S(1)}, u32[]{:S(2)}, u32[]{:S(2)}) async-start(f32[64,32,256]{2,1,0:T(8,128)} %broadcast_in_dim.26), calls=%async_computation | async-start | bytes 4194304 | tf_op jit(solution)/shard_map/all_to_all | solution.py:489
  95.7 29.4 %all-to-all-done = f32[64,32,256]{2,1,0:T(8,128)S(1)} async-done(((f32[64,32,256]{2,1,0:T(8,128)}), f32[64,32,256]{2,1,0:T(8,128)S(1)}, u32[]{:S(2)}, u32[]{:S(2)}) %all-to-all-start) | async-done | bytes 2097184 | tf_op jit(solution)/shard_map/all_to_all | solution.py:489
  127.1 1.9 collective-permute-start.15
  129.0 2.5 %collective-permute-start.16 = (f32[64,2048]{1,0:T(8,128)S(1)}, f32[64,2048]{1,0:T(8,128)S(1)}, u32[]{:S(2)}, u32[]{:S(2)}) collective-permute-start(f32[64,2048]{1,0:T(8,128)S(1)} %get-tuple-element.43), channel_id=1, source_target_pairs={{0,96},{32,64},{64,32},{96,0},{1,97},{33,65},{65,33},{97,1},{2,98}... | collective-permute-start | bytes 1572872 | tf_op jit(solution)/shard_map/ppermute | solution.py:441
  131.5 22.8 %factor_begin.1 = (f32[1024,1024]{1,0:T(8,128)S(1)}, f32[512,256]{1,0:T(8,128)S(1)}) custom-call(s32[4]{0:T(128)S(1)} %copy-done.1, f32[2048,256]{1,0:T(8,128)S(1)} %bitcast.27, f32[2048,256]{1,0:T(8,128)} %collective-permute-done.17.other, f32[8,128]{1,0:T(8,128)S(1)} %slice.69.misfit), custom_call_target="tpu_custom_call" | custom-call | flops 20000000000 | bytes 10000000 | tf_op jit(solution)/shard_map/factor_begin/pallas_call | solution.py:349
  154.3 2.1 collective-permute-done.16
  157.6 1.9 collective-permute-start.19
  161.1 19.6 %factor_finish.1 = (f32[1024,1024]{1,0:T(8,128)S(1)}, f32[512,256]{1,0:T(8,128)S(1)}) custom-call(f32[1024,1024]{1,0:T(8,128)S(1)} %get-tuple-element.35.before, f32[512,256]{1,0:T(8,128)S(1)} %get-tuple-element.36.earlier), custom_call_target="tpu_custom_call" | custom-call | flops 20000000000 | bytes 10000000 | tf_op jit(solution)/shard_map/factor_finish/pallas_call | solution.py:363
  180.8 4.9 %collective-permute-done.20.b3 = f32[256,512]{1,0:T(8,128)S(1)} collective-permute-done((f32[256,512]{1,0:T(8,128)S(1)}, f32[256,512]{1,0:T(8,128)S(1)}, u32[]{:S(2)}, u32[]{:S(2)}) %collective-permute-start.20) | collective-permute-done | bytes 524320 | tf_op jit(solution)/shard_map/ppermute | solution.py:441
  185.6 2.1 collective-permute-done.18.b1
  187.7 9.6 %solve.1.work = f32[1024,512]{1,0:T(8,128)S(1)} custom-call(s32[4]{0:T(128)S(1)} %copy-done.1, f32[1024,1024]{1,0:T(8,128)S(1)} %get-tuple-element.37.system, f32[512,256]{1,0:T(8,128)S(1)} %get-tuple-element.36.earlier, f32[512,256]{1,0:T(8,128)S(1)} %get-tuple-element.38.later, f32[256,512]{1,0:T(8,128)S(1)} %pad_maximum_fusion.2.b0, ...), custom_call_target="tpu_custom_call" | custom-call | flops 5000000000 | bytes 10000000 | tf_op jit(solution)/shard_map/solve/pallas_call | solution.py:400
  198.7 10.4 %combine.1 = f32[1024,512]{1,0:T(8,128)} custom-call(f32[4096,256]{1,0:T(8,128)} %all-gather.2.cloned.1.call-done.rhs, f32[1024,512]{1,0:T(8,128)} %copy-done.2, f32[8,128]{1,0:T(8,128)} %copy-done), custom_call_target="tpu_custom_call" | custom-call | flops 6000000000 | bytes 10000000 | tf_op jit(solution)/shard_map/combine/pallas_call | solution.py:421
  209.1 29.1 %all_to_all.24 = f32[16,64,512]{2,1,0:T(8,128)S(1)} all-to-all(f32[16,64,512]{2,1,0:T(8,128)} %bitcast.30), channel_id=1, replica_groups=mesh['z'=4,'y'=4,'x'=4,'core'=2] {'z','y'}, dimensions={0} | all-to-all | bytes 4194304 | tf_op jit(solution)/shard_map/all_to_all | solution.py:510
  (83 shorter events, 35.9 us)
Async XLA Ops:
  6.5 15.2 %collective-permute-start = (f32[64,2048]{1,0:T(8,128)}, f32[64,2048]{1,0:T(8,128)S(1)}, u32[]{:S(2)}, u32[]{:S(2)}) collective-permute-start(f32[64,2048]{1,0:T(8,128)} %n0.1), channel_id=1, source_target_pairs={{0,8},{8,16},{16,24},{24,0},{1,9},{9,17},{17,25},{25,1},{2,10},{10... | collective-permute-start | bytes 1572872 | tf_op jit(solution)/shard_map/ppermute | solution.py:435
  8.2 13.6 %collective-permute-start.1 = (f32[64,2048]{1,0:T(8,128)}, f32[64,2048]{1,0:T(8,128)S(1)}, u32[]{:S(2)}, u32[]{:S(2)}) collective-permute-start(f32[64,2048]{1,0:T(8,128)} %n0.1), channel_id=1, source_target_pairs={{0,24},{8,0},{16,8},{24,16},{1,25},{9,1},{17,9},{25,17},{2,26},{10... | collective-permute-start | bytes 1572872 | tf_op jit(solution)/shard_map/ppermute | solution.py:436
  21.8 31.6 %copy-start.5 = (f32[64,2048]{1,0:T(8,128)}, f32[64,2048]{1,0:T(8,128)S(1)}, u32[]{:S(2)}) copy-start(f32[64,2048]{1,0:T(8,128)S(1)} %collective-permute-done.n1) | copy-start | bytes 1572868
  21.8 17.6 %collective-permute-start.2 = (f32[72,2048]{1,0:T(8,128)}, f32[72,2048]{1,0:T(8,128)S(1)}, u32[]{:S(2)}, u32[]{:S(2)}) collective-permute-start(f32[72,2048]{1,0:T(8,128)} %forward.1.e0), channel_id=1, source_target_pairs={{0,32},{32,64},{64,96},{96,0},{1,33},{33,65},{65,97},{97,1},{2,34}... | collective-permute-start | bytes 1769480 | tf_op jit(solution)/shard_map/ppermute | solution.py:435
  23.8 27.0 %collective-permute-start.3 = (f32[72,2048]{1,0:T(8,128)}, f32[72,2048]{1,0:T(8,128)S(1)}, u32[]{:S(2)}, u32[]{:S(2)}) collective-permute-start(f32[72,2048]{1,0:T(8,128)} %forward.1.e0), channel_id=1, source_target_pairs={{0,96},{32,0},{64,32},{96,64},{1,97},{33,1},{65,33},{97,65},{2,98}... | collective-permute-start | bytes 1769480 | tf_op jit(solution)/shard_map/ppermute | solution.py:436
  26.0 26.5 %collective-permute-start.4 = (f32[72,2048]{1,0:T(8,128)}, f32[72,2048]{1,0:T(8,128)S(1)}, u32[]{:S(2)}, u32[]{:S(2)}) collective-permute-start(f32[72,2048]{1,0:T(8,128)} %forward.1.e0), channel_id=1, source_target_pairs={{0,64},{32,96},{64,0},{96,32},{1,65},{33,97},{65,1},{97,33},{2,66}... | collective-permute-start | bytes 1769480 | tf_op jit(solution)/shard_map/ppermute | solution.py:441
  29.1 24.3 %collective-permute-start.5 = (f32[104,2048]{1,0:T(8,128)S(1)}, f32[104,2048]{1,0:T(8,128)S(1)}, u32[]{:S(2)}, u32[]{:S(2)}) collective-permute-start(f32[104,2048]{1,0:T(8,128)S(1)} %get-tuple-element.48), channel_id=1, source_target_pairs={{0,8},{8,16},{16,24},{24,0},{1,9},{9,17},{17,25},{25,1},{2,10},{10... | collective-permute-start | bytes 2555912 | tf_op jit(solution)/shard_map/ppermute | solution.py:435
  30.7 22.7 %collective-permute-start.6 = (f32[104,2048]{1,0:T(8,128)S(1)}, f32[104,2048]{1,0:T(8,128)S(1)}, u32[]{:S(2)}, u32[]{:S(2)}) collective-permute-start(f32[104,2048]{1,0:T(8,128)S(1)} %get-tuple-element.47), channel_id=1, source_target_pairs={{0,24},{8,0},{16,8},{24,16},{1,25},{9,1},{17,9},{25,17},{2,26},{10... | collective-permute-start | bytes 2555912 | tf_op jit(solution)/shard_map/ppermute | solution.py:436
  53.5 10.9 %collective-permute-start.7 = (f32[40,2048]{1,0:T(8,128)S(1)}, f32[40,2048]{1,0:T(8,128)S(1)}, u32[]{:S(2)}, u32[]{:S(2)}) collective-permute-start(f32[40,2048]{1,0:T(8,128)S(1)} %get-tuple-element.71), channel_id=1, source_target_pairs={{0,8},{8,16},{16,24},{24,0},{1,9},{9,17},{17,25},{25,1},{2,10},{10... | collective-permute-start | bytes 983048 | tf_op jit(solution)/shard_map/ppermute | solution.py:435
  54.7 9.7 %collective-permute-start.8 = (f32[40,2048]{1,0:T(8,128)S(1)}, f32[40,2048]{1,0:T(8,128)S(1)}, u32[]{:S(2)}, u32[]{:S(2)}) collective-permute-start(f32[40,2048]{1,0:T(8,128)S(1)} %get-tuple-element.70), channel_id=1, source_target_pairs={{0,24},{8,0},{16,8},{24,16},{1,25},{9,1},{17,9},{25,17},{2,26},{10... | collective-permute-start | bytes 983048 | tf_op jit(solution)/shard_map/ppermute | solution.py:436
  56.8 7.6 %collective-permute-start.9 = (f32[8,2048]{1,0:T(8,128)S(1)}, f32[8,2048]{1,0:T(8,128)S(1)}, u32[]{:S(2)}, u32[]{:S(2)}) collective-permute-start(f32[8,2048]{1,0:T(8,128)S(1)} %slice_add_fusion.t0), channel_id=1, source_target_pairs={{0,16},{8,24},{16,0},{24,8},{1,17},{9,25},{17,1},{25,9},{2,18},{10... | collective-permute-start | bytes 196616 | tf_op jit(solution)/shard_map/ppermute | solution.py:441
  74.6 1.9 collective-permute-start.10
  77.6 4.8 %collective-permute-start.11 = (f32[40,512]{1,0:T(8,128)S(1)}, f32[40,512]{1,0:T(8,128)S(1)}, u32[]{:S(2)}, u32[]{:S(2)}) collective-permute-start(f32[40,512]{1,0:T(8,128)S(1)} %get-tuple-element.67), channel_id=1, source_target_pairs={{0,2},{2,0},{4,6},{6,4},{1,3},{3,1},{5,7},{7,5},{8,10},{10,8},{12,... | collective-permute-start | bytes 245768 | tf_op jit(solution)/shard_map/ppermute | solution.py:441
  79.2 7.0 %collective-permute-start.12 = (f32[40,512]{1,0:T(8,128)S(1)}, f32[40,512]{1,0:T(8,128)S(1)}, u32[]{:S(2)}, u32[]{:S(2)}) collective-permute-start(f32[40,512]{1,0:T(8,128)S(1)} %get-tuple-element.65), channel_id=1, source_target_pairs={{0,4},{2,6},{4,0},{6,2},{1,5},{3,7},{5,1},{7,3},{8,12},{10,14},{12... | collective-permute-start | bytes 245768 | tf_op jit(solution)/shard_map/ppermute | solution.py:441
  81.9 6.0 %collective-permute-start.13 = (f32[40,512]{1,0:T(8,128)S(1)}, f32[40,512]{1,0:T(8,128)S(1)}, u32[]{:S(2)}, u32[]{:S(2)}) collective-permute-start(f32[40,512]{1,0:T(8,128)S(1)} %get-tuple-element.66), channel_id=1, source_target_pairs={{0,6},{2,4},{4,2},{6,0},{1,7},{3,5},{5,3},{7,1},{8,14},{10,12},{12... | collective-permute-start | bytes 245768 | tf_op jit(solution)/shard_map/ppermute | solution.py:441
  90.1 34.9 %all-to-all-start = ((f32[64,32,256]{2,1,0:T(8,128)}), f32[64,32,256]{2,1,0:T(8,128)S(1)}, u32[]{:S(2)}, u32[]{:S(2)}) async-start(f32[64,32,256]{2,1,0:T(8,128)} %broadcast_in_dim.26), calls=%async_computation | async-start | bytes 4194304 | tf_op jit(solution)/shard_map/all_to_all | solution.py:489
  94.9 103.8 %all-gather.2.cloned.1.call-start = ((), (), s32[]{:S(2)}) async-start(), calls=%async_computation.2 | async-start | bytes 4227072 | tf_op jit(solution)/shard_map/all_gather | solution.py:488
  125.0 6.5 %collective-permute-start.17 = (f32[2048,256]{1,0:T(8,128)S(1)}, f32[2048,256]{1,0:T(8,128)}, u32[]{:S(2)}, u32[]{:S(2)}) collective-permute-start(f32[2048,256]{1,0:T(8,128)S(1)} %bitcast.26), channel_id=1, source_target_pairs={{0,1},{1,0},{2,3},{3,2},{4,5},{5,4},{6,7},{7,6},{8,9},{9,8},{10,11... | collective-permute-start | bytes 6291464 | tf_op jit(solution)/shard_map/ppermute | solution.py:441
  126.7 27.6 %collective-permute-start.14 = (f32[64,2048]{1,0:T(8,128)S(1)}, f32[64,2048]{1,0:T(8,128)S(1)}, u32[]{:S(2)}, u32[]{:S(2)}) collective-permute-start(f32[64,2048]{1,0:T(8,128)S(1)} %get-tuple-element.45), channel_id=1, source_target_pairs={{0,32},{32,0},{64,96},{96,64},{1,33},{33,1},{65,97},{97,65},{2,34}... | collective-permute-start | bytes 1572872 | tf_op jit(solution)/shard_map/ppermute | solution.py:441
  127.1 27.2 %collective-permute-start.15 = (f32[64,2048]{1,0:T(8,128)S(1)}, f32[64,2048]{1,0:T(8,128)S(1)}, u32[]{:S(2)}, u32[]{:S(2)}) collective-permute-start(f32[64,2048]{1,0:T(8,128)S(1)} %get-tuple-element.44), channel_id=1, source_target_pairs={{0,64},{32,96},{64,0},{96,32},{1,65},{33,97},{65,1},{97,33},{2,66}... | collective-permute-start | bytes 1572872 | tf_op jit(solution)/shard_map/ppermute | solution.py:441
  129.0 27.4 %collective-permute-start.16 = (f32[64,2048]{1,0:T(8,128)S(1)}, f32[64,2048]{1,0:T(8,128)S(1)}, u32[]{:S(2)}, u32[]{:S(2)}) collective-permute-start(f32[64,2048]{1,0:T(8,128)S(1)} %get-tuple-element.43), channel_id=1, source_target_pairs={{0,96},{32,64},{64,32},{96,0},{1,97},{33,65},{65,33},{97,1},{2,98}... | collective-permute-start | bytes 1572872 | tf_op jit(solution)/shard_map/ppermute | solution.py:441
  156.7 28.9 %collective-permute-start.20 = (f32[256,512]{1,0:T(8,128)S(1)}, f32[256,512]{1,0:T(8,128)S(1)}, u32[]{:S(2)}, u32[]{:S(2)}) collective-permute-start(f32[256,512]{1,0:T(8,128)S(1)} %pad_maximum_fusion.5), channel_id=1, source_target_pairs={{0,24},{8,16},{16,8},{24,0},{1,25},{9,17},{17,9},{25,1},{2,26},{10... | collective-permute-start | bytes 1572872 | tf_op jit(solution)/shard_map/ppermute | solution.py:441
  157.6 28.0 %collective-permute-start.19 = (f32[256,512]{1,0:T(8,128)S(1)}, f32[256,512]{1,0:T(8,128)S(1)}, u32[]{:S(2)}, u32[]{:S(2)}) collective-permute-start(f32[256,512]{1,0:T(8,128)S(1)} %pad_maximum_fusion.4), channel_id=1, source_target_pairs={{0,16},{8,24},{16,0},{24,8},{1,17},{9,25},{17,1},{25,9},{2,18},{10... | collective-permute-start | bytes 1572872 | tf_op jit(solution)/shard_map/ppermute | solution.py:441
  159.6 28.1 %collective-permute-start.18 = (f32[256,512]{1,0:T(8,128)S(1)}, f32[256,512]{1,0:T(8,128)S(1)}, u32[]{:S(2)}, u32[]{:S(2)}) collective-permute-start(f32[256,512]{1,0:T(8,128)S(1)} %pad_maximum_fusion.3), channel_id=1, source_target_pairs={{0,8},{8,0},{16,24},{24,16},{1,9},{9,1},{17,25},{25,17},{2,10},{10... | collective-permute-start | bytes 1572872 | tf_op jit(solution)/shard_map/ppermute | solution.py:441
  (14 other events, 110.6 us)
Sparse Core Ops, SparseCore 0:
  98.9 92.7 all-gather.1

commit v10 on v9

--- a/solution.py
+++ b/solution.py
@@ -16,7 +16,7 @@
 LANES = 128
 HALF = 128
 TILE = 256
-CHUNK = 1024
+CHUNK = 2048
 f32 = jnp.float32
 
 ANY_VMEM = pl.BlockSpec(memory_space=pltpu.VMEM)

time: 249 us -> 249 us (level)
  transfers between devices with their start and end apart: 23 -> 23, of which waited for: 12 -> 12; matrix products, arithmetic and copies ran while one was open for 2% -> 2% of each run, Pallas kernels for 25% -> 24%
where the time goes in v10:
time: 249 us; the launch traced here: 248 us
  Pallas kernels  78.3 us (31%)
  waiting for transfers between devices  77 us (31%)
  starting transfers between devices  36 us (14%)
  blocking collectives  29.1 us (12%)
  between operations  13.7 us (6%)
  local copies, waits for them, and re-layouts  8.52 us (3%)
  other arithmetic  5.6 us (2%)
    all_to_all x1, waiting for transfers between devices, body(): lax.all_to_all(jnp.broadcast_to(piece[None], (Z * Y * X, 32, TILE)), ('z'...  29.4 us
    all_to_all x1, blocking collectives, body(): lax.all_to_all(change, ('z', 'y'), 0, 1, tiled=True)  29.1 us
    ppermute x13, waiting for transfers between devices, swap(): return lax.ppermute(value, axis, [(i, i ^ bit) for i in range(size)])  23.6 us
    pallas_call x1, Pallas kernels, factor_begin(): pl.pallas_call(begin_kernel, in_specs=[ANY_SMEM, ANY_VMEM, ANY_VMEM, ANY_...  22.8 us
    pallas_call x1, Pallas kernels, factor_finish(): pl.pallas_call(finish_kernel, in_specs=[pl.BlockSpec(memory_space=pl.ANY)...  19.6 us
    ppermute x13, starting transfers between devices, swap(): return lax.ppermute(value, axis, [(i, i ^ bit) for i in range(size)])  17.1 us
    ppermute x4, waiting for transfers between devices, onward(): low = lax.ppermute(low, axis, [(i, (i + 1) % 4) for i in range(4)])  12 us
    ppermute x4, waiting for transfers between devices, onward(): high = lax.ppermute(high, axis, [(i, (i + 3) % 4) for i in range(4)])  11.3 us
  transfers between devices with their start and end apart: 23, of which 12 were waited for; matrix products, arithmetic and copies ran while one was open for 2% of the time, Pallas kernels for 24%

profile of v10, /device:TPU:0, one launch (start us, length us, event | category | flops | bytes accessed | tf_op | source)
XLA Modules:
  0.0 248.2 jit_solution(16714593235838112919)
XLA Ops:
  9.8 7.1 %forward.1.e0 = f32[72,2048]{1,0:T(8,128)} custom-call(f32[64,8192]{1,0:T(8,128)} %effect.1, f32[1,8192]{1,0:T(1,128)} %bitcast.31, f32[1,8192]{1,0:T(1,128)} %bitcast.32, f32[1,8192]{1,0:T(1,128)} %bitcast.33, f32[3,8192]{1,0:T(4,128)} %init.1, f32[6,8192]{1,0:T(8,128)} %fall.1, s32[4,2048]{1,0:T(4,128)} %bitcast.34, f32[4,2048]{1,0:T(4,128)} %bitcast.35, ...), custom_call_target="tpu_custom_call" | custom-call | flops 20000000000 | bytes 10000000 | tf_op jit(solution)/shard_map/forward/pallas_call | solution.py:96
  16.8 4.9 %collective-permute-done.n1 = f32[64,2048]{1,0:T(8,128)S(1)} collective-permute-done((f32[64,2048]{1,0:T(8,128)}, f32[64,2048]{1,0:T(8,128)S(1)}, u32[]{:S(2)}, u32[]{:S(2)}) %collective-permute-start) | collective-permute-done | bytes 524320 | tf_op jit(solution)/shard_map/ppermute | solution.py:435
  21.8 2.0 collective-permute-start.2
  23.8 2.2 collective-permute-start.3
  32.4 7.0 %collective-permute-done.2.p1 = f32[72,2048]{1,0:T(8,128)S(1)} collective-permute-done((f32[72,2048]{1,0:T(8,128)}, f32[72,2048]{1,0:T(8,128)S(1)}, u32[]{:S(2)}, u32[]{:S(2)}) %collective-permute-start.2) | collective-permute-done | bytes 589856 | tf_op jit(solution)/shard_map/ppermute | solution.py:435
  39.4 11.3 %collective-permute-done.3.p2 = f32[72,2048]{1,0:T(8,128)S(1)} collective-permute-done((f32[72,2048]{1,0:T(8,128)}, f32[72,2048]{1,0:T(8,128)S(1)}, u32[]{:S(2)}, u32[]{:S(2)}) %collective-permute-start.3) | collective-permute-done | bytes 589856 | tf_op jit(solution)/shard_map/ppermute | solution.py:436
  54.7 2.1 collective-permute-start.8
  58.8 5.6 %collective-permute-done.9.t2 = f32[8,2048]{1,0:T(8,128)S(1)} collective-permute-done((f32[8,2048]{1,0:T(8,128)S(1)}, f32[8,2048]{1,0:T(8,128)S(1)}, u32[]{:S(2)}, u32[]{:S(2)}) %collective-permute-start.9) | collective-permute-done | bytes 65568 | tf_op jit(solution)/shard_map/ppermute | solution.py:441
  65.9 8.7 %gram.1 = (f32[4,40,512]{2,1,0:T(8,128)}, f32[4,40,512]{2,1,0:T(8,128)}) custom-call(s32[4]{0:T(128)} %pad_add_fusion.where, f32[72,2048]{1,0:T(8,128)} %forward.1.e0, f32[104,2048]{1,0:T(8,128)} %copy-done.7, f32[104,2048]{1,0:T(8,128)} %copy-done.8, f32[40,2048]{1,0:T(8,128)} %copy-done.12, f32[40,2048]{1,0:T(8,128)} %copy-done.13, f32[8,2048]{1,0:T(8,128)} %copy-done.4, ...), custom_call_target="tpu_custom_call" | custom-call | flops 8000000000 | bytes 10000000 | tf_op jit(solution)/shard_map/gram/pallas_call | solution.py:173
  79.2 2.7 %collective-permute-start.12 = (f32[40,512]{1,0:T(8,128)S(1)}, f32[40,512]{1,0:T(8,128)S(1)}, u32[]{:S(2)}, u32[]{:S(2)}) collective-permute-start(f32[40,512]{1,0:T(8,128)S(1)} %get-tuple-element.65), channel_id=1, source_target_pairs={{0,4},{2,6},{4,0},{6,2},{1,5},{3,7},{5,1},{7,3},{8,12},{10,14},{12... | collective-permute-start | bytes 245768 | tf_op jit(solution)/shard_map/ppermute | solution.py:441
  82.4 3.8 %collective-permute-done.12 = f32[40,512]{1,0:T(8,128)S(1)} collective-permute-done((f32[40,512]{1,0:T(8,128)S(1)}, f32[40,512]{1,0:T(8,128)S(1)}, u32[]{:S(2)}, u32[]{:S(2)}) %collective-permute-start.12) | collective-permute-done | bytes 81952 | tf_op jit(solution)/shard_map/ppermute | solution.py:441
  90.1 4.8 %all-to-all-start = ((f32[64,32,256]{2,1,0:T(8,128)}), f32[64,32,256]{2,1,0:T(8,128)S(1)}, u32[]{:S(2)}, u32[]{:S(2)}) async-start(f32[64,32,256]{2,1,0:T(8,128)} %broadcast_in_dim.26), calls=%async_computation | async-start | bytes 4194304 | tf_op jit(solution)/shard_map/all_to_all | solution.py:489
  95.7 29.4 %all-to-all-done = f32[64,32,256]{2,1,0:T(8,128)S(1)} async-done(((f32[64,32,256]{2,1,0:T(8,128)}), f32[64,32,256]{2,1,0:T(8,128)S(1)}, u32[]{:S(2)}, u32[]{:S(2)}) %all-to-all-start) | async-done | bytes 2097184 | tf_op jit(solution)/shard_map/all_to_all | solution.py:489
  127.1 1.9 collective-permute-start.15
  129.0 2.5 %collective-permute-start.16 = (f32[64,2048]{1,0:T(8,128)S(1)}, f32[64,2048]{1,0:T(8,128)S(1)}, u32[]{:S(2)}, u32[]{:S(2)}) collective-permute-start(f32[64,2048]{1,0:T(8,128)S(1)} %get-tuple-element.43), channel_id=1, source_target_pairs={{0,96},{32,64},{64,32},{96,0},{1,97},{33,65},{65,33},{97,1},{2,98}... | collective-permute-start | bytes 1572872 | tf_op jit(solution)/shard_map/ppermute | solution.py:441
  131.5 22.8 %factor_begin.1 = (f32[1024,1024]{1,0:T(8,128)S(1)}, f32[512,256]{1,0:T(8,128)S(1)}) custom-call(s32[4]{0:T(128)S(1)} %copy-done.1, f32[2048,256]{1,0:T(8,128)S(1)} %bitcast.27, f32[2048,256]{1,0:T(8,128)} %collective-permute-done.17.other, f32[8,128]{1,0:T(8,128)S(1)} %slice.69.misfit), custom_call_target="tpu_custom_call" | custom-call | flops 20000000000 | bytes 10000000 | tf_op jit(solution)/shard_map/factor_begin/pallas_call | solution.py:349
  154.3 2.1 collective-permute-done.16
  157.6 1.9 collective-permute-start.19
  161.1 19.6 %factor_finish.1 = (f32[1024,1024]{1,0:T(8,128)S(1)}, f32[512,256]{1,0:T(8,128)S(1)}) custom-call(f32[1024,1024]{1,0:T(8,128)S(1)} %get-tuple-element.35.before, f32[512,256]{1,0:T(8,128)S(1)} %get-tuple-element.36.earlier), custom_call_target="tpu_custom_call" | custom-call | flops 20000000000 | bytes 10000000 | tf_op jit(solution)/shard_map/factor_finish/pallas_call | solution.py:363
  180.8 4.9 %collective-permute-done.20.b3 = f32[256,512]{1,0:T(8,128)S(1)} collective-permute-done((f32[256,512]{1,0:T(8,128)S(1)}, f32[256,512]{1,0:T(8,128)S(1)}, u32[]{:S(2)}, u32[]{:S(2)}) %collective-permute-start.20) | collective-permute-done | bytes 524320 | tf_op jit(solution)/shard_map/ppermute | solution.py:441
  185.6 2.1 collective-permute-done.18.b1
  187.7 9.6 %solve.1.work = f32[1024,512]{1,0:T(8,128)S(1)} custom-call(s32[4]{0:T(128)S(1)} %copy-done.1, f32[1024,1024]{1,0:T(8,128)S(1)} %get-tuple-element.37.system, f32[512,256]{1,0:T(8,128)S(1)} %get-tuple-element.36.earlier, f32[512,256]{1,0:T(8,128)S(1)} %get-tuple-element.38.later, f32[256,512]{1,0:T(8,128)S(1)} %pad_maximum_fusion.2.b0, ...), custom_call_target="tpu_custom_call" | custom-call | flops 5000000000 | bytes 10000000 | tf_op jit(solution)/shard_map/solve/pallas_call | solution.py:400
  198.7 10.4 %combine.1 = f32[1024,512]{1,0:T(8,128)} custom-call(f32[4096,256]{1,0:T(8,128)} %all-gather.2.cloned.1.call-done.rhs, f32[1024,512]{1,0:T(8,128)} %copy-done.2, f32[8,128]{1,0:T(8,128)} %copy-done), custom_call_target="tpu_custom_call" | custom-call | flops 6000000000 | bytes 10000000 | tf_op jit(solution)/shard_map/combine/pallas_call | solution.py:421
  209.1 29.1 %all_to_all.24 = f32[16,64,512]{2,1,0:T(8,128)S(1)} all-to-all(f32[16,64,512]{2,1,0:T(8,128)} %bitcast.30), channel_id=1, replica_groups=mesh['z'=4,'y'=4,'x'=4,'core'=2] {'z','y'}, dimensions={0} | all-to-all | bytes 4194304 | tf_op jit(solution)/shard_map/all_to_all | solution.py:510
  (83 shorter events, 35.9 us)
Async XLA Ops:
  6.5 15.2 %collective-permute-start = (f32[64,2048]{1,0:T(8,128)}, f32[64,2048]{1,0:T(8,128)S(1)}, u32[]{:S(2)}, u32[]{:S(2)}) collective-permute-start(f32[64,2048]{1,0:T(8,128)} %n0.1), channel_id=1, source_target_pairs={{0,8},{8,16},{16,24},{24,0},{1,9},{9,17},{17,25},{25,1},{2,10},{10... | collective-permute-start | bytes 1572872 | tf_op jit(solution)/shard_map/ppermute | solution.py:435
  8.2 13.6 %collective-permute-start.1 = (f32[64,2048]{1,0:T(8,128)}, f32[64,2048]{1,0:T(8,128)S(1)}, u32[]{:S(2)}, u32[]{:S(2)}) collective-permute-start(f32[64,2048]{1,0:T(8,128)} %n0.1), channel_id=1, source_target_pairs={{0,24},{8,0},{16,8},{24,16},{1,25},{9,1},{17,9},{25,17},{2,26},{10... | collective-permute-start | bytes 1572872 | tf_op jit(solution)/shard_map/ppermute | solution.py:436
  21.8 31.6 %copy-start.5 = (f32[64,2048]{1,0:T(8,128)}, f32[64,2048]{1,0:T(8,128)S(1)}, u32[]{:S(2)}) copy-start(f32[64,2048]{1,0:T(8,128)S(1)} %collective-permute-done.n1) | copy-start | bytes 1572868
  21.8 17.6 %collective-permute-start.2 = (f32[72,2048]{1,0:T(8,128)}, f32[72,2048]{1,0:T(8,128)S(1)}, u32[]{:S(2)}, u32[]{:S(2)}) collective-permute-start(f32[72,2048]{1,0:T(8,128)} %forward.1.e0), channel_id=1, source_target_pairs={{0,32},{32,64},{64,96},{96,0},{1,33},{33,65},{65,97},{97,1},{2,34}... | collective-permute-start | bytes 1769480 | tf_op jit(solution)/shard_map/ppermute | solution.py:435
  23.8 27.0 %collective-permute-start.3 = (f32[72,2048]{1,0:T(8,128)}, f32[72,2048]{1,0:T(8,128)S(1)}, u32[]{:S(2)}, u32[]{:S(2)}) collective-permute-start(f32[72,2048]{1,0:T(8,128)} %forward.1.e0), channel_id=1, source_target_pairs={{0,96},{32,0},{64,32},{96,64},{1,97},{33,1},{65,33},{97,65},{2,98}... | collective-permute-start | bytes 1769480 | tf_op jit(solution)/shard_map/ppermute | solution.py:436
  26.0 26.5 %collective-permute-start.4 = (f32[72,2048]{1,0:T(8,128)}, f32[72,2048]{1,0:T(8,128)S(1)}, u32[]{:S(2)}, u32[]{:S(2)}) collective-permute-start(f32[72,2048]{1,0:T(8,128)} %forward.1.e0), channel_id=1, source_target_pairs={{0,64},{32,96},{64,0},{96,32},{1,65},{33,97},{65,1},{97,33},{2,66}... | collective-permute-start | bytes 1769480 | tf_op jit(solution)/shard_map/ppermute | solution.py:441
  29.1 24.3 %collective-permute-start.5 = (f32[104,2048]{1,0:T(8,128)S(1)}, f32[104,2048]{1,0:T(8,128)S(1)}, u32[]{:S(2)}, u32[]{:S(2)}) collective-permute-start(f32[104,2048]{1,0:T(8,128)S(1)} %get-tuple-element.48), channel_id=1, source_target_pairs={{0,8},{8,16},{16,24},{24,0},{1,9},{9,17},{17,25},{25,1},{2,10},{10... | collective-permute-start | bytes 2555912 | tf_op jit(solution)/shard_map/ppermute | solution.py:435
  30.7 22.7 %collective-permute-start.6 = (f32[104,2048]{1,0:T(8,128)S(1)}, f32[104,2048]{1,0:T(8,128)S(1)}, u32[]{:S(2)}, u32[]{:S(2)}) collective-permute-start(f32[104,2048]{1,0:T(8,128)S(1)} %get-tuple-element.47), channel_id=1, source_target_pairs={{0,24},{8,0},{16,8},{24,16},{1,25},{9,1},{17,9},{25,17},{2,26},{10... | collective-permute-start | bytes 2555912 | tf_op jit(solution)/shard_map/ppermute | solution.py:436
  53.5 10.9 %collective-permute-start.7 = (f32[40,2048]{1,0:T(8,128)S(1)}, f32[40,2048]{1,0:T(8,128)S(1)}, u32[]{:S(2)}, u32[]{:S(2)}) collective-permute-start(f32[40,2048]{1,0:T(8,128)S(1)} %get-tuple-element.71), channel_id=1, source_target_pairs={{0,8},{8,16},{16,24},{24,0},{1,9},{9,17},{17,25},{25,1},{2,10},{10... | collective-permute-start | bytes 983048 | tf_op jit(solution)/shard_map/ppermute | solution.py:435
  54.7 9.7 %collective-permute-start.8 = (f32[40,2048]{1,0:T(8,128)S(1)}, f32[40,2048]{1,0:T(8,128)S(1)}, u32[]{:S(2)}, u32[]{:S(2)}) collective-permute-start(f32[40,2048]{1,0:T(8,128)S(1)} %get-tuple-element.70), channel_id=1, source_target_pairs={{0,24},{8,0},{16,8},{24,16},{1,25},{9,1},{17,9},{25,17},{2,26},{10... | collective-permute-start | bytes 983048 | tf_op jit(solution)/shard_map/ppermute | solution.py:436
  56.8 7.6 %collective-permute-start.9 = (f32[8,2048]{1,0:T(8,128)S(1)}, f32[8,2048]{1,0:T(8,128)S(1)}, u32[]{:S(2)}, u32[]{:S(2)}) collective-permute-start(f32[8,2048]{1,0:T(8,128)S(1)} %slice_add_fusion.t0), channel_id=1, source_target_pairs={{0,16},{8,24},{16,0},{24,8},{1,17},{9,25},{17,1},{25,9},{2,18},{10... | collective-permute-start | bytes 196616 | tf_op jit(solution)/shard_map/ppermute | solution.py:441
  74.6 1.9 collective-permute-start.10
  77.6 4.8 %collective-permute-start.11 = (f32[40,512]{1,0:T(8,128)S(1)}, f32[40,512]{1,0:T(8,128)S(1)}, u32[]{:S(2)}, u32[]{:S(2)}) collective-permute-start(f32[40,512]{1,0:T(8,128)S(1)} %get-tuple-element.67), channel_id=1, source_target_pairs={{0,2},{2,0},{4,6},{6,4},{1,3},{3,1},{5,7},{7,5},{8,10},{10,8},{12,... | collective-permute-start | bytes 245768 | tf_op jit(solution)/shard_map/ppermute | solution.py:441
  79.2 7.0 %collective-permute-start.12 = (f32[40,512]{1,0:T(8,128)S(1)}, f32[40,512]{1,0:T(8,128)S(1)}, u32[]{:S(2)}, u32[]{:S(2)}) collective-permute-start(f32[40,512]{1,0:T(8,128)S(1)} %get-tuple-element.65), channel_id=1, source_target_pairs={{0,4},{2,6},{4,0},{6,2},{1,5},{3,7},{5,1},{7,3},{8,12},{10,14},{12... | collective-permute-start | bytes 245768 | tf_op jit(solution)/shard_map/ppermute | solution.py:441
  81.9 6.0 %collective-permute-start.13 = (f32[40,512]{1,0:T(8,128)S(1)}, f32[40,512]{1,0:T(8,128)S(1)}, u32[]{:S(2)}, u32[]{:S(2)}) collective-permute-start(f32[40,512]{1,0:T(8,128)S(1)} %get-tuple-element.66), channel_id=1, source_target_pairs={{0,6},{2,4},{4,2},{6,0},{1,7},{3,5},{5,3},{7,1},{8,14},{10,12},{12... | collective-permute-start | bytes 245768 | tf_op jit(solution)/shard_map/ppermute | solution.py:441
  90.1 34.9 %all-to-all-start = ((f32[64,32,256]{2,1,0:T(8,128)}), f32[64,32,256]{2,1,0:T(8,128)S(1)}, u32[]{:S(2)}, u32[]{:S(2)}) async-start(f32[64,32,256]{2,1,0:T(8,128)} %broadcast_in_dim.26), calls=%async_computation | async-start | bytes 4194304 | tf_op jit(solution)/shard_map/all_to_all | solution.py:489
  94.9 103.8 %all-gather.2.cloned.1.call-start = ((), (), s32[]{:S(2)}) async-start(), calls=%async_computation.2 | async-start | bytes 4227072 | tf_op jit(solution)/shard_map/all_gather | solution.py:488
  125.0 6.5 %collective-permute-start.17 = (f32[2048,256]{1,0:T(8,128)S(1)}, f32[2048,256]{1,0:T(8,128)}, u32[]{:S(2)}, u32[]{:S(2)}) collective-permute-start(f32[2048,256]{1,0:T(8,128)S(1)} %bitcast.26), channel_id=1, source_target_pairs={{0,1},{1,0},{2,3},{3,2},{4,5},{5,4},{6,7},{7,6},{8,9},{9,8},{10,11... | collective-permute-start | bytes 6291464 | tf_op jit(solution)/shard_map/ppermute | solution.py:441
  126.7 27.6 %collective-permute-start.14 = (f32[64,2048]{1,0:T(8,128)S(1)}, f32[64,2048]{1,0:T(8,128)S(1)}, u32[]{:S(2)}, u32[]{:S(2)}) collective-permute-start(f32[64,2048]{1,0:T(8,128)S(1)} %get-tuple-element.45), channel_id=1, source_target_pairs={{0,32},{32,0},{64,96},{96,64},{1,33},{33,1},{65,97},{97,65},{2,34}... | collective-permute-start | bytes 1572872 | tf_op jit(solution)/shard_map/ppermute | solution.py:441
  127.1 27.2 %collective-permute-start.15 = (f32[64,2048]{1,0:T(8,128)S(1)}, f32[64,2048]{1,0:T(8,128)S(1)}, u32[]{:S(2)}, u32[]{:S(2)}) collective-permute-start(f32[64,2048]{1,0:T(8,128)S(1)} %get-tuple-element.44), channel_id=1, source_target_pairs={{0,64},{32,96},{64,0},{96,32},{1,65},{33,97},{65,1},{97,33},{2,66}... | collective-permute-start | bytes 1572872 | tf_op jit(solution)/shard_map/ppermute | solution.py:441
  129.0 27.4 %collective-permute-start.16 = (f32[64,2048]{1,0:T(8,128)S(1)}, f32[64,2048]{1,0:T(8,128)S(1)}, u32[]{:S(2)}, u32[]{:S(2)}) collective-permute-start(f32[64,2048]{1,0:T(8,128)S(1)} %get-tuple-element.43), channel_id=1, source_target_pairs={{0,96},{32,64},{64,32},{96,0},{1,97},{33,65},{65,33},{97,1},{2,98}... | collective-permute-start | bytes 1572872 | tf_op jit(solution)/shard_map/ppermute | solution.py:441
  156.7 28.9 %collective-permute-start.20 = (f32[256,512]{1,0:T(8,128)S(1)}, f32[256,512]{1,0:T(8,128)S(1)}, u32[]{:S(2)}, u32[]{:S(2)}) collective-permute-start(f32[256,512]{1,0:T(8,128)S(1)} %pad_maximum_fusion.5), channel_id=1, source_target_pairs={{0,24},{8,16},{16,8},{24,0},{1,25},{9,17},{17,9},{25,1},{2,26},{10... | collective-permute-start | bytes 1572872 | tf_op jit(solution)/shard_map/ppermute | solution.py:441
  157.6 28.0 %collective-permute-start.19 = (f32[256,512]{1,0:T(8,128)S(1)}, f32[256,512]{1,0:T(8,128)S(1)}, u32[]{:S(2)}, u32[]{:S(2)}) collective-permute-start(f32[256,512]{1,0:T(8,128)S(1)} %pad_maximum_fusion.4), channel_id=1, source_target_pairs={{0,16},{8,24},{16,0},{24,8},{1,17},{9,25},{17,1},{25,9},{2,18},{10... | collective-permute-start | bytes 1572872 | tf_op jit(solution)/shard_map/ppermute | solution.py:441
  159.6 28.1 %collective-permute-start.18 = (f32[256,512]{1,0:T(8,128)S(1)}, f32[256,512]{1,0:T(8,128)S(1)}, u32[]{:S(2)}, u32[]{:S(2)}) collective-permute-start(f32[256,512]{1,0:T(8,128)S(1)} %pad_maximum_fusion.3), channel_id=1, source_target_pairs={{0,8},{8,0},{16,24},{24,16},{1,9},{9,1},{17,25},{25,17},{2,10},{10... | collective-permute-start | bytes 1572872 | tf_op jit(solution)/shard_map/ppermute | solution.py:441
  (14 other events, 110.6 us)
Sparse Core Ops, SparseCore 0:
  98.9 92.7 all-gather.1
